TPU v7x, 512 devices: a whole 4x8x8 slice. The times are simulated.
512 devices in a mesh: freq: 64 (over y_hi, x, z), cuts: 8 (over y_lo, core).
Axes of the slice: x: 4, y: 8 (y_hi: 2, y_lo: 4; y = y_hi * 4 + y_lo), z: 8, core: 2. Of those that a mesh axis runs over, the one named last changes fastest.
Arguments:
- wavefield: bfloat16 [64, 2, 2048, 2048], P('freq', None, 'cuts'), may hold values from -6 to 6
- slowness: bfloat16 [64, 2048, 2048], P('freq', 'cuts'), may hold values from 0.25 to 0.546875
- block_inverse: bfloat16 [64, 2, 40, 64, 64], P('freq', None, 'cuts'), may hold values from -0.75 to 0.75
- block_lengths: int32 [64, 40], replicated, may hold values from 1 to 64, 2048 in all within a row
- slab_owner: int32 [1], replicated, may hold values from 0 to 63
- shot_position: int32 [2], replicated, may hold values from 0 to 2047
Outputs:
- image: float32 [1, 2048, 2048], P(None, 'cuts', 'freq')
Inputs may be any that keep to these rules, and one draw needn't show every extreme that they name: `block_lengths`: each row lists the lengths of the 40 blocks of a line in order; they sum to 2048 and the longest is exactly 64.
All inputs are finite; a program needn't handle non-finite values.
Results may differ from a plain program's by a relative error of at most 0.012.
Values may be sent and summed in bfloat16 or wider, within the bound.
No kernel may reach another device: no remote copies, remote signals or barrier semaphores. Data moves between devices by JAX's collectives and lax.ppermute only.
A program may use at most 64 MiB of HBM per device.

v0:
```python
import math

import jax
import jax.numpy as jnp
from jax import lax
from jax.sharding import PartitionSpec as P

grid_step = 0.0125
depth_step = 0.02
slow_ref = 0.4
band_low = 5.0
band_width = 55.0


def spread(block, axis, owner):
    block = jnp.where(lax.axis_index(axis) == owner, block, jnp.zeros_like(block))
    return lax.psum(block, axis)


def split_length(extent):
    outer_len = 2 ** ((extent.bit_length() - 1) // 2)
    return (outer_len, extent // outer_len)


def outer_table(outer_len, orient):
    first_ids = jnp.arange(outer_len, dtype=jnp.int32)
    indices = first_ids[:, None] * first_ids[None, :] % outer_len
    angles = orient * 2.0 * math.pi / outer_len * indices.astype(jnp.float32)
    cosine = jnp.cos(angles) / math.sqrt(outer_len)
    sine = jnp.sin(angles) / math.sqrt(outer_len)
    first = jnp.stack([cosine, sine], axis=1)
    second = jnp.stack([-sine, cosine], axis=1)
    return jnp.stack([first, second], axis=0).astype(jnp.bfloat16)


def inner_table(outer_len, inner_len, orient):
    extent = outer_len * inner_len
    outer_ids = jnp.arange(outer_len, dtype=jnp.int32)[:, None, None]
    inner_ids = jnp.arange(inner_len, dtype=jnp.int32)[None, :, None]
    freq_ids = jnp.arange(inner_len, dtype=jnp.int32)[None, None, :]
    indices = inner_ids * (outer_ids + outer_len * freq_ids) % extent
    angles = orient * 2.0 * math.pi / extent * indices.astype(jnp.float32)
    cosine = jnp.cos(angles) / math.sqrt(inner_len)
    sine = jnp.sin(angles) / math.sqrt(inner_len)
    first = jnp.stack([cosine, sine], axis=2)
    second = jnp.stack([-sine, cosine], axis=2)
    return jnp.stack([first, second], axis=2).astype(jnp.bfloat16)


def mixing(formula, operand, table):
    return jnp.einsum(formula, operand, table, preferred_element_type=jnp.float32)


def forward_lines(field):
    rows = field.shape[1]
    outer_len, inner_len = split_length(field.shape[2])
    shaped = field.reshape(2, rows, outer_len, inner_len)
    first_section = mixing("cmab,cadk->mbdk", shaped, outer_table(outer_len, -1.0)).astype(
        jnp.bfloat16
    )
    return mixing(
        "mbdk,kbdeq->kmeq", first_section, inner_table(outer_len, inner_len, -1.0)
    ).astype(jnp.bfloat16)


def across_forward(columns):
    count_k, extent_x, _, count_q = columns.shape
    outer_len, inner_len = split_length(extent_x)
    shaped = columns.reshape(count_k, outer_len, inner_len, 2, count_q)
    first_section = mixing("kabcq,cadz->kbqdz", shaped, outer_table(outer_len, -1.0)).astype(
        jnp.bfloat16
    )
    return mixing("kbqdz,zbdwu->zkqwu", first_section, inner_table(outer_len, inner_len, -1.0))


def across_inverse(spectrum, extent_x):
    count_k = spectrum.shape[1]
    count_q = spectrum.shape[2]
    outer_len, inner_len = split_length(extent_x)
    first_section = mixing(
        "zkqwu,zbwdu->zkqdb", spectrum, inner_table(outer_len, inner_len, 1.0)
    ).astype(jnp.bfloat16)
    second_section = mixing("zkqdb,daez->kabeq", first_section, outer_table(outer_len, 1.0)).astype(
        jnp.bfloat16
    )
    return second_section.reshape(count_k, extent_x, 2, count_q)


def lines_inverse(spectrum, extent_y):
    rows = spectrum.shape[1]
    outer_len, inner_len = split_length(extent_y)
    first_section = mixing(
        "kmdq,kbdeq->kmeb", spectrum, inner_table(outer_len, inner_len, 1.0)
    ).astype(jnp.bfloat16)
    second_section = mixing("kmeb,eack->cmab", first_section, outer_table(outer_len, 1.0))
    return second_section.reshape(2, rows, extent_y)


def wave_numbers(indices, extent):
    signed = jnp.where(indices < extent // 2, indices, indices - extent)
    return signed.astype(jnp.float32) * (2.0 * math.pi / (extent * grid_step))


def propagator(angular, k_start, k_count, extent_x, extent_y):
    outer_x, inner_x = split_length(extent_x)
    outer_y, inner_y = split_length(extent_y)
    cross_ids = (
        jnp.arange(outer_x, dtype=jnp.int32)[:, None]
        + outer_x * jnp.arange(inner_x, dtype=jnp.int32)[None, :]
    )
    line_ids = (k_start + jnp.arange(k_count, dtype=jnp.int32))[:, None] + outer_y * jnp.arange(
        inner_y, dtype=jnp.int32
    )[None, :]
    wave_x = wave_numbers(cross_ids, extent_x)
    wave_y = wave_numbers(line_ids, extent_y)
    vertical = (
        (angular * slow_ref) ** 2 - wave_x[:, None, None, :] ** 2 - wave_y[None, :, :, None] ** 2
    )
    root_abs = jnp.sqrt(jnp.abs(vertical))
    real_part = jnp.where(
        vertical > 0, jnp.cos(root_abs * depth_step), jnp.exp(-root_abs * depth_step)
    )
    imag_part = jnp.where(vertical > 0, jnp.sin(root_abs * depth_step), jnp.zeros_like(root_abs))
    return (real_part, imag_part)


def shift_phase(kspace, prop_re, prop_im):
    real_in = kspace[:, :, :, 0, :]
    imag_in = kspace[:, :, :, 1, :]
    real_out = real_in * prop_re - imag_in * prop_im
    imag_out = real_in * prop_im + imag_in * prop_re
    return jnp.stack([real_out, imag_out], axis=3).astype(jnp.bfloat16)


def block_correction(turned, matrices, block_len, extent_y):
    block_count = matrices.shape[1]
    capacity = matrices.shape[2]
    starts = jnp.cumsum(block_len) - block_len
    offsets = jnp.arange(capacity, dtype=jnp.int32)
    source = jnp.minimum(starts[:, None] + offsets[None, :], extent_y - 1).reshape(-1)
    occupied = (offsets[None, :] < block_len[:, None]).reshape(-1)

    def slotted(part):
        picked = jnp.take(part, source, axis=1)
        picked = jnp.where(occupied[None, :], picked, jnp.zeros_like(picked))
        return picked.reshape(part.shape[0], block_count, capacity)

    slot_re = slotted(turned[0])
    slot_im = slotted(turned[1])

    def product(first_op, second_op):
        return jnp.einsum("rcj,cij->rci", first_op, second_op, preferred_element_type=jnp.float32)

    out_re = product(slot_re, matrices[0]) - product(slot_im, matrices[1])
    out_im = product(slot_re, matrices[1]) + product(slot_im, matrices[0])
    cell_ids = jnp.arange(extent_y, dtype=jnp.int32)
    block_end = starts + block_len
    shift_sum = jnp.sum(
        jnp.where(block_end[None, :] <= cell_ids[:, None], capacity - block_len[None, :], 0), axis=1
    )
    position = cell_ids + shift_sum
    back_re = jnp.take(out_re.reshape(out_re.shape[0], -1), position, axis=1)
    back_im = jnp.take(out_im.reshape(out_im.shape[0], -1), position, axis=1)
    return (back_re, back_im)


def image_phase(angular, rows_x, cols_y, shot_position, depth_index):
    offset_x = (rows_x - shot_position[0]).astype(jnp.float32) * grid_step
    offset_y = (cols_y - shot_position[1]).astype(jnp.float32) * grid_step
    depth_now = (depth_index + 1) * depth_step
    distance = jnp.sqrt(offset_x[:, None] ** 2 + offset_y[None, :] ** 2 + depth_now * depth_now)
    return angular * slow_ref * distance


def body(wavefield, slowness, block_inverse, block_lengths, slab_owner, shot_position):
    cut_count = lax.axis_size("cuts")
    freq_total = lax.axis_size("freq")
    row_count = wavefield.shape[2]
    extent_y = wavefield.shape[3]
    extent_x = row_count * cut_count
    outer_y, inner_y = split_length(extent_y)
    local_k = outer_y // cut_count
    freq_index = lax.axis_index("freq")
    cut_index = lax.axis_index("cuts")
    angular = (
        2.0
        * math.pi
        * (band_low + band_width * (freq_index.astype(jnp.float32) + 0.5) / freq_total)
    )
    prop_re, prop_im = propagator(angular, cut_index * local_k, local_k, extent_x, extent_y)
    rows_x = cut_index * row_count + jnp.arange(row_count, dtype=jnp.int32)
    cols_y = jnp.arange(extent_y, dtype=jnp.int32)
    current = wavefield[0]
    spectrum = forward_lines(current)
    columns = lax.all_to_all(spectrum, "cuts", split_axis=0, concat_axis=1, tiled=True)
    kspace = across_forward(columns)
    shifted = shift_phase(kspace, prop_re, prop_im)
    restored = across_inverse(shifted, extent_x)
    row_field = lax.all_to_all(restored, "cuts", split_axis=1, concat_axis=0, tiled=True)
    spatial = lines_inverse(row_field, extent_y)
    owner_id = slab_owner[0]
    slab_now = spread(slowness, "freq", owner_id)
    block_piece = spread(block_inverse, "freq", owner_id)
    matrices = lax.all_gather(block_piece, "cuts", axis=2, tiled=True)
    block_len = lax.dynamic_index_in_dim(block_lengths, owner_id, 0, keepdims=False)
    slab_now, matrices, block_len = (slab_now[0], matrices[0], block_len)
    phases = angular * depth_step * (slab_now.astype(jnp.float32) - slow_ref)
    cos_part = jnp.cos(phases)
    sin_part = jnp.sin(phases)
    turned = (
        (spatial[0] * cos_part - spatial[1] * sin_part).astype(jnp.bfloat16),
        (spatial[0] * sin_part + spatial[1] * cos_part).astype(jnp.bfloat16),
    )
    correction = block_correction(turned, matrices, block_len, extent_y)
    values_re = turned[0].astype(jnp.float32) + correction[0]
    values_im = turned[1].astype(jnp.float32) + correction[1]
    angle_img = image_phase(angular, rows_x, cols_y, shot_position, 0)
    image_part = (values_re * jnp.cos(angle_img) - values_im * jnp.sin(angle_img)) * (
        1.0 / math.sqrt(freq_total)
    )
    images = [lax.psum_scatter(image_part, "freq", scatter_dimension=1, tiled=True)]
    return jnp.stack(images)


def solution(mesh):
    placed = (
        P("freq", None, "cuts", None),
        P("freq", "cuts", None),
        P("freq", None, "cuts", None, None),
        P(),
        P(),
        P(),
    )
    return jax.shard_map(
        body, mesh=mesh, in_specs=placed, out_specs=P(None, "cuts", "freq"), check_vma=False
    )
```

profile of v0, /device:TPU:8, one launch (start us, length us, event | category | flops | bytes accessed | tf_op | source)
XLA Modules:
  0.0 1557.3 jit_solution(3600363477350407030)
XLA Ops:
  6.7 10.6 fusion.62
  17.3 2.9 copy.67
  20.2 1.9 maximum_bitcast_fusion.6
  22.2 1.7 fusion.54
  23.9 3.0 bitcast_convert_fusion.4
  26.9 10.1 all-to-all-start
  37.3 0.4 maximum_bitcast_fusion.4
  37.7 1.9 pad_maximum_fusion
  39.7 42.9 %all-to-all-done = bf16[32,256,2,64]{1,3,2,0:T(8,128)(2,1)} async-done(((bf16[32,256,2,64]{1,3,2,0:T(8,128)(2,1)}), bf16[32,256,2,64]{1,3,2,0:T(8,128)(2,1)}, u32[]{:S(2)}, u32[]{:S(2)}) %all-to-all-start) | async-done | bytes 2097184 | tf_op jit(solution)/shard_map/all_to_all | solution.py:195
  82.6 4.2 copy.161
  86.8 6.1 reshape.441
  92.9 3.6 fusion.15
  96.5 2.7 fusion.27
  99.2 18.3 %fusion.10 = (bf16[32,4,64,1,64]{4,2,3,1,0:T(8,128)(2,1)S(1)}, bf16[32,4,64,1,64]{4,2,3,1,0:T(8,128)(2,1)S(1)}) fusion(f32[32,4,64,2,64]{4,2,3,1,0:T(8,128)S(1)} %fusion.27, f32[4,64]{1,0:T(4,128)S(1)} %fusion.86, f32[32,64]{1,0:T(8,128)S(1)} %fusion.77), kind=kLoop, calls=%fused_computation.19 | loop fusion | flops 8388608 | bytes 6300672 | tf_op jit(solution)/shard_map/convert
  117.5 3.5 fusion.16
  121.1 9.3 copy.77
  130.3 5.4 fusion.17
  135.8 12.4 copy.124
  148.1 7.6 reshape.518
  155.7 7.8 all-to-all-start.1
  164.2 1.5 copy.86
  165.8 0.7 broadcast_select_fusion.1
  166.4 1.0 broadcast_select_fusion
  167.6 0.2 subtract_reduce_fusion
  168.3 0.7 fusion.94
  168.9 0.7 multiply_multiply_fusion.1
  169.6 0.7 multiply_multiply_fusion
  170.5 823.7 %all-reduce.3.cloned.1.call-done = (bf16[1,256,2048]{1,2,0:T(8,128)(2,1)}, bf16[1,2,5,64,64]{4,3,2,1,0:T(8,128)(2,1)}) async-done(((bf16[1,256,2048]{1,2,0:T(8,128)(2,1)}, bf16[1,2,5,64,64]{4,3,2,1,0:T(8,128)(2,1)}), (bf16[1,256,2048]{1,2,0:T(8,128)(2,1)}, bf16[1,2,5,64,64]{4,3,2,1,0:T(8,128)(2,1)})) %all-reduce.3.cloned.1.call-update) | async-done | bytes 1130512 | tf_op jit(solution)/shard_map/psum | solution.py:17
  994.2 17.1 %all_gather.3 = bf16[1,2,40,64,64]{4,3,2,1,0:T(8,128)(2,1)S(1)} all-gather(bf16[1,2,5,64,64]{4,3,2,1,0:T(8,128)(2,1)} %get-tuple-element.10), channel_id=1, replica_groups=mesh['freq'=64,'cuts'=8] {'cuts'}, dimensions={2}, use_global_device_ids=true | all-gather | bytes 737280 | tf_op jit(solution)/shard_map/all_gather | solution.py:204
  1011.3 7.4 reshape.519
  1018.7 10.6 copy.127
  1029.3 2.3 fusion.48
  1031.8 1.7 convolution_bitcast_fusion
  1033.5 0.6 fusion.93
  1034.1 1.2 copy.85
  1035.4 1.2 copy.87
  1036.6 8.4 fusion.43
  1045.0 8.1 gather_fusion
  1053.1 8.1 gather_fusion.1
  1061.3 3.6 bitcast_select_fusion
  1064.9 0.5 fusion.64
  1065.4 0.5 fusion.65
  1065.9 2.0 convolution_subtract_fusion
  1067.9 2.0 convolution_add_fusion
  1069.9 10.4 gather_fusion.2
  1080.3 10.3 gather_fusion.3
  1090.6 12.4 fusion.38
  1103.0 447.4 %reduce-scatter.2.cloned.1.call-done = f32[256,32]{0,1:T(8,128)} async-done(((f32[256,2048]{0,1:T(8,128)}), f32[256,32]{0,1:T(8,128)}) %reduce-scatter.2.cloned.1.call-update) | async-done | bytes 32784 | tf_op jit(solution)/shard_map/reduce_scatter | solution.py:221
  (51 shorter events, 1.4 us)
Async XLA Ops:
  22.2 1.7 copy-start
  26.9 10.4 copy-start.3
  26.9 10.4 copy-start.4
  26.9 10.4 copy-start.5
  26.9 55.7 %all-to-all-start = ((bf16[32,256,2,64]{1,3,2,0:T(8,128)(2,1)}), bf16[32,256,2,64]{1,3,2,0:T(8,128)(2,1)}, u32[]{:S(2)}, u32[]{:S(2)}) async-start(bf16[32,256,2,64]{1,3,2,0:T(8,128)(2,1)} %bitcast_convert_fusion.4), calls=%async_computation | async-start | bytes 4194304 | tf_op jit(solution)/shard_map/all_to_all | solution.py:195
  92.9 3.6 copy-start.1
  99.2 18.3 %copy-start.2 = (bf16[32,64,2,2,64,1]{1,4,3,0,2,5:T(8,128)(2,1)S(1)}, bf16[32,64,2,2,64,1]{1,4,3,0,2,5:T(8,128)(2,1)}, u32[]{:S(2)}) copy-start(bf16[32,64,2,2,64,1]{1,4,3,0,2,5:T(8,128)(2,1)} %get-tuple-element.18) | copy-start | bytes 3145732
  155.7 855.6 %all-to-all-start.1 = ((bf16[8,2,65536]{2,1,0:T(2,128)(2,1)}), bf16[8,2,65536]{2,1,0:T(2,128)(2,1)}, u32[]{:S(2)}, u32[]{:S(2)}) async-start(bf16[8,2,65536]{2,1,0:T(2,128)(2,1)} %reshape.518), calls=%async_computation.1 | async-start | bytes 4194304 | tf_op jit(solution)/shard_map/all_to_all | solution.py:199
  163.5 2.2 copy-start.7
  163.5 830.7 %all-reduce.3.cloned.1.call-start = ((), (), s32[]{:S(2)}) async-start(), calls=%async_computation.4 | async-start | bytes 2424832 | tf_op jit(solution)/shard_map/psum | solution.py:17
  165.7 1.8 copy-start.8
  165.7 2.5 copy-start.9
  167.5 1382.9 %reduce-scatter.2.cloned.1.call-start = ((), (), s32[]{:S(2)}) async-start(), calls=%async_computation.3 | async-start | bytes 2129920 | tf_op jit(solution)/shard_map/reduce_scatter | solution.py:221
  1035.3 1.2 copy-start.6
Sparse Core Ops, SparseCore 0:
  167.6 826.5 all-reduce.2
  1103.2 447.2 reduce-scatter.1
where the time goes:
time: 1560 us
  waiting for transfers between devices  1310 us (84%)
  local copies, waits for them, and re-layouts  103 us (7%)
  other arithmetic  61.8 us (4%)
  matrix products  28.9 us (2%)
  starting transfers between devices  18 us (1%)
  blocking collectives  17.1 us (1%)
    psum x1, waiting for transfers between devices, spread(): return lax.psum(block, axis)  824 us
    reduce_scatter x1, waiting for transfers between devices, body(): lax.psum_scatter(image_part, 'freq', scatter_dimension=1, tiled=True)  447 us
    all_to_all x1, waiting for transfers between devices, body(): lax.all_to_all(spectrum, 'cuts', split_axis=0, concat_axis=1, tiled=True)  42.9 us
  transfers between devices with their start and end apart: 4, of which 3 were waited for; matrix products, arithmetic and copies ran while one was open for 1% of the time, Pallas kernels for 0%

commit v1 on v0

v1 whole, which is shorter than its diff:
```python
import functools
import math

import jax
import jax.numpy as jnp
import numpy as np
from jax import lax
from jax.experimental import pallas as pl
from jax.experimental.pallas import tpu as pltpu
from jax.sharding import Mesh, PartitionSpec as P

grid_step = 0.0125
depth_step = 0.02
slow_ref = 0.4
band_low = 5.0
band_width = 55.0

INTERPRET = False
FREQ_AXES = ("yh", "x", "z")
CUT_AXES = ("yl", "core")
RADIX = 8
BLOCK_GROUP = 4
f32 = jnp.float32
bf16 = jnp.bfloat16


def dft_tables(extent):
    base = extent // RADIX
    ids = np.arange(base)
    angle = 2.0 * np.pi / base * ((ids[:, None] * ids[None, :]) % base)
    cosine = np.cos(angle) / math.sqrt(base)
    sine = np.sin(angle) / math.sqrt(base)
    forward = np.block([[cosine, sine], [-sine, cosine]])
    inverse = np.block([[cosine, -sine], [sine, cosine]])
    twist = 2.0 * np.pi / extent * (np.arange(RADIX)[:, None] * ids[None, :])
    turn = np.stack([np.cos(twist), np.sin(twist)], axis=1) / math.sqrt(RADIX)
    turn = turn.reshape(2 * RADIX, base).astype(np.float32)
    return (
        jnp.asarray(forward, bf16),
        jnp.asarray(inverse, bf16),
        jnp.asarray(turn),
        jnp.asarray(np.ascontiguousarray(turn.T)),
    )


def fft4(parts, s):
    (r0, i0), (r1, i1), (r2, i2), (r3, i3) = parts
    ar, ai, br, bi = r0 + r2, i0 + i2, r0 - r2, i0 - i2
    cr, ci, dr, di = r1 + r3, i1 + i3, r1 - r3, i1 - i3
    if s > 0:
        one, three = (br - di, bi + dr), (br + di, bi - dr)
    else:
        one, three = (br + di, bi - dr), (br - di, bi + dr)
    return [(ar + cr, ai + ci), one, (ar - cr, ai - ci), three]


def fft8(parts, s):
    even = fft4(parts[0::2], s)
    odd = fft4(parts[1::2], s)
    half = math.sqrt(0.5)
    (r0, i0), (r1, i1), (r2, i2), (r3, i3) = odd
    if s > 0:
        turned = [
            (r0, i0),
            ((r1 - i1) * half, (i1 + r1) * half),
            (-i2, r2),
            ((r3 + i3) * -half, (r3 - i3) * half),
        ]
    else:
        turned = [
            (r0, i0),
            ((r1 + i1) * half, (i1 - r1) * half),
            (i2, -r2),
            ((i3 - r3) * half, (r3 + i3) * -half),
        ]
    low = [(e[0] + t[0], e[1] + t[1]) for e, t in zip(even, turned)]
    high = [(e[0] - t[0], e[1] - t[1]) for e, t in zip(even, turned)]
    return low + high


def twist(value, cosine, sine, s):
    real, imag = value
    if s > 0:
        return (real * cosine - imag * sine, imag * cosine + real * sine)
    return (real * cosine + imag * sine, imag * cosine - real * sine)


def lines_forward_kernel(field, table, turn, out, mid):
    rows, base = out.shape[2], out.shape[3]

    def step(tile, carry):
        at = pl.ds(pl.multiple_of(tile * 16, 16), 16)
        for lane in range(0, base, 128):
            parts = []
            for a in range(RADIX):
                here = pl.ds(a * base + lane, 128)
                parts.append((field[0, at, here].astype(f32), field[1, at, here].astype(f32)))
            for k, value in enumerate(fft8(parts, -1)):
                cosine = turn[2 * k : 2 * k + 1, lane : lane + 128]
                sine = turn[2 * k + 1 : 2 * k + 2, lane : lane + 128]
                real, imag = twist(value, cosine, sine, -1)
                mid[k, at, pl.ds(lane, 128)] = real.astype(bf16)
                mid[k, at, pl.ds(base + lane, 128)] = imag.astype(bf16)
        return carry

    lax.fori_loop(0, rows // 16, step, 0)
    for k in range(RADIX):
        both = jnp.dot(mid[k], table[...], preferred_element_type=f32)
        out[k, 0] = both[:, :base].astype(bf16)
        out[k, 1] = both[:, base:].astype(bf16)


def across_kernel(field, prop_re, prop_im, forward, inverse, turn, out, mid, back):
    base, cols = prop_re.shape[1], prop_re.shape[2]

    def fore(tile, carry):
        at = pl.multiple_of(tile * 16, 16)
        for lane in range(0, cols, 128):
            here = pl.ds(lane, 128)
            parts = []
            for a in range(RADIX):
                parts.append(
                    (
                        field[a, pl.ds(at, 16), here].astype(f32),
                        field[a, pl.ds(base + at, 16), here].astype(f32),
                    )
                )
            for k, value in enumerate(fft8(parts, -1)):
                cosine = turn[pl.ds(at, 16), 2 * k : 2 * k + 1]
                sine = turn[pl.ds(at, 16), 2 * k + 1 : 2 * k + 2]
                real, imag = twist(value, cosine, sine, -1)
                mid[k, pl.ds(at, 16), here] = real.astype(bf16)
                mid[k, pl.ds(base + at, 16), here] = imag.astype(bf16)
        return carry

    lax.fori_loop(0, base // 16, fore, 0)
    for k in range(RADIX):
        both = jnp.dot(forward[...], mid[k], preferred_element_type=f32)
        real, imag = both[:base], both[base:]
        p_re, p_im = prop_re[k], prop_im[k]
        mid[k, :base] = (real * p_re - imag * p_im).astype(bf16)
        mid[k, base:] = (real * p_im + imag * p_re).astype(bf16)
        back[k] = jnp.dot(inverse[...], mid[k], preferred_element_type=f32)

    def aft(tile, carry):
        at = pl.multiple_of(tile * 16, 16)
        for lane in range(0, cols, 128):
            here = pl.ds(lane, 128)
            parts = []
            for k in range(RADIX):
                cosine = turn[pl.ds(at, 16), 2 * k : 2 * k + 1]
                sine = turn[pl.ds(at, 16), 2 * k + 1 : 2 * k + 2]
                value = (back[k, pl.ds(at, 16), here], back[k, pl.ds(base + at, 16), here])
                parts.append(twist(value, cosine, sine, 1))
            for a, (real, imag) in enumerate(fft8(parts, 1)):
                out[a, pl.ds(at, 16), here] = real.astype(bf16)
                out[a, pl.ds(base + at, 16), here] = imag.astype(bf16)
        return carry

    lax.fori_loop(0, base // 16, aft, 0)


def lines_inverse_kernel(
    windows, field, cos_u, sin_u, cos_r, sin_r, pairs, table, turn, out, back, turned, final
):
    rows, base = field.shape[2], field.shape[3]
    blocks, reach = pairs.shape[0], pairs.shape[1] // 2
    tail = pl.ds(RADIX * base, turned.shape[1] - RADIX * base)
    turned[:, tail, :] = jnp.zeros((2, tail.size, rows), bf16)
    for k in range(RADIX):
        first = lax.dot_general(
            table[:, :base], field[k, 0], (((1,), (1,)), ((), ())), preferred_element_type=f32
        )
        second = lax.dot_general(
            table[:, base:], field[k, 1], (((1,), (1,)), ((), ())), preferred_element_type=f32
        )
        back[k] = first + second

    def aft(tile, carry):
        at = pl.multiple_of(tile * 16, 16)
        for lane in range(0, rows, 128):
            here = pl.ds(lane, 128)
            parts = []
            for k in range(RADIX):
                cosine = turn[pl.ds(at, 16), 2 * k : 2 * k + 1]
                sine = turn[pl.ds(at, 16), 2 * k + 1 : 2 * k + 2]
                value = (back[k, pl.ds(at, 16), here], back[k, pl.ds(base + at, 16), here])
                parts.append(twist(value, cosine, sine, 1))
            for a, (real, imag) in enumerate(fft8(parts, 1)):
                cell = pl.ds(a * base + at, 16)
                cosine, sine = cos_u[cell, here], sin_u[cell, here]
                u_re = (real * cosine - imag * sine).astype(bf16)
                u_im = (real * sine + imag * cosine).astype(bf16)
                turned[0, cell, here] = u_re
                turned[1, cell, here] = u_im
                final[0, cell, here] = u_re.astype(f32)
                final[1, cell, here] = u_im.astype(f32)
        return carry

    lax.fori_loop(0, base // 16, aft, 0)

    def some_blocks(group, carry):
        cells, changes = [], []
        for one in range(BLOCK_GROUP):
            c = group * BLOCK_GROUP + one
            cell = pl.ds(pl.multiple_of(windows[c] * 16, 16), reach)
            both = jnp.concatenate([turned[0, cell, :], turned[1, cell, :]], axis=0)
            cells.append(cell)
            changes.append(jnp.dot(pairs[c], both, preferred_element_type=f32))
        for cell, change in zip(cells, changes):
            final[0, cell, :] += change[:reach]
            final[1, cell, :] += change[reach:]
        return carry

    lax.fori_loop(0, blocks // BLOCK_GROUP, some_blocks, 0)

    def image(tile, carry):
        cell = pl.ds(pl.multiple_of(tile * 16, 16), 16)
        across, along, high, piece = out.shape[:4]
        owner, place = tile * 16 // piece, tile * 16 % piece
        spot = pl.ds(pl.multiple_of(place, 16), 16)
        out[owner // along % across, owner % along, owner // (along * across), spot, :] = (
            final[0, cell, :] * cos_r[cell, :] - final[1, cell, :] * sin_r[cell, :]
        ).astype(bf16)
        return carry

    lax.fori_loop(0, RADIX * base // 16, image, 0)


def call(kernel, out_shape, scratch, *operands, scalars=0):
    smem = pl.BlockSpec(memory_space=pltpu.SMEM)
    vmem = pl.BlockSpec(memory_space=pltpu.VMEM)
    return pl.pallas_call(
        kernel,
        out_shape=out_shape,
        in_specs=[smem] * scalars + [vmem] * (len(operands) - scalars),
        out_specs=vmem,
        scratch_shapes=scratch,
        interpret=INTERPRET,
    )(*operands)


def wave_numbers(indices, extent):
    signed = jnp.where(indices < extent // 2, indices, indices - extent)
    return signed.astype(f32) * (2.0 * math.pi / (extent * grid_step))


def propagator(angular, cut_index, extent_x, extent_y):
    cross_ids = (
        jnp.arange(RADIX, dtype=jnp.int32)[:, None]
        + RADIX * jnp.arange(extent_x // RADIX, dtype=jnp.int32)[None, :]
    )
    line_ids = cut_index + RADIX * jnp.arange(extent_y // RADIX, dtype=jnp.int32)
    wave_x = wave_numbers(cross_ids, extent_x)
    wave_y = wave_numbers(line_ids, extent_y)
    vertical = (angular * slow_ref) ** 2 - wave_x[:, :, None] ** 2 - wave_y[None, None, :] ** 2
    root_abs = jnp.sqrt(jnp.abs(vertical))
    real_part = jnp.where(
        vertical > 0, jnp.cos(root_abs * depth_step), jnp.exp(-root_abs * depth_step)
    )
    imag_part = jnp.where(vertical > 0, jnp.sin(root_abs * depth_step), jnp.zeros_like(root_abs))
    return (real_part, imag_part)


def rotations(size):
    return [[(i, (i + d) % size) for i in range(size)] for d in range(1, size)]


def split_ring(value, axis, owner):
    size = lax.axis_size(axis)
    me = lax.axis_index(axis)
    shaped = value.reshape((size, value.shape[0] // size) + value.shape[1:])
    piece = lax.dynamic_index_in_dim(shaped, me, 0, keepdims=False)
    for d, pairs in enumerate(rotations(size), 1):
        sent = lax.dynamic_index_in_dim(shaped, (me + d) % size, 0, keepdims=False)
        got = lax.ppermute(sent, axis, pairs)
        piece = jnp.where((me - owner) % size == d, got, piece)
    return piece


def join_ring(piece, axis):
    size = lax.axis_size(axis)
    me = lax.axis_index(axis)
    out = jnp.zeros((size,) + piece.shape, piece.dtype)
    out = lax.dynamic_update_index_in_dim(out, piece, me, 0)
    for d, pairs in enumerate(rotations(size), 1):
        got = lax.ppermute(piece, axis, pairs)
        out = lax.dynamic_update_index_in_dim(out, got, (me - d) % size, 0)
    return out.reshape((-1,) + piece.shape[1:])


def swap(value, axis, bit):
    return lax.ppermute(value, axis, [(i, i ^ bit) for i in range(lax.axis_size(axis))])


def bits_of(size):
    return [1 << i for i in range(size.bit_length() - 1)]


def split_hops(value, axis, owner):
    me = lax.axis_index(axis)
    for bit in bits_of(lax.axis_size(axis)):
        mine = (me & bit) != 0
        half = value.shape[0] // 2
        low, high = value[:half], value[half:]
        got = swap(jnp.where(mine, low, high), axis, bit)
        value = jnp.where(((owner ^ me) & bit) == 0, jnp.where(mine, high, low), got)
    return value


def join_hops(piece, axis, bits=None):
    me = lax.axis_index(axis)
    for bit in bits_of(lax.axis_size(axis))[::-1] if bits is None else bits:
        mine = (me & bit) != 0
        got = swap(piece, axis, bit)
        piece = jnp.concatenate([jnp.where(mine, got, piece), jnp.where(mine, piece, got)], axis=0)
    return piece


def from_owner(value, owner_id):
    across, along = lax.axis_size("x"), lax.axis_size("z")
    piece = split_ring(value, "x", owner_id // along % across)
    piece = split_hops(piece, "z", owner_id % along)
    if lax.axis_size("yh") > 1:
        other = swap(piece, "yh", 1)
        same = lax.axis_index("yh") == owner_id // (across * along)
        piece = jnp.where(same, piece, other)
    return piece


def sum_over(part, axis, kind):
    terms = lax.all_to_all(part, axis, 0, 0)
    return jnp.sum(terms.astype(f32), axis=0).astype(kind)


def block_windows(matrices, starts, lengths):
    capacity = matrices.shape[2]
    reach = capacity + 16
    windows = starts // 16
    slots = jnp.arange(capacity, dtype=jnp.int32)
    spots = jnp.arange(reach, dtype=jnp.int32)
    place = (spots[None, :, None] == slots[None, None, :] + (starts % 16)[:, None, None]) & (
        slots[None, None, :] < lengths[:, None, None]
    )
    place = place.astype(bf16)
    moved = jnp.einsum("cia,dcab->dcib", place, matrices, preferred_element_type=f32).astype(bf16)
    moved = jnp.einsum("dcib,cjb->dcij", moved, place, preferred_element_type=f32).astype(bf16)
    upper = jnp.concatenate([moved[0], -moved[1]], axis=2)
    lower = jnp.concatenate([moved[1], moved[0]], axis=2)
    return windows, jnp.concatenate([upper, lower], axis=1)


def body(wavefield, slowness, block_inverse, block_lengths, slab_owner, shot_position):
    counts = tuple(lax.axis_size(name) for name in FREQ_AXES)
    freq_total = math.prod(counts)
    cut_count = lax.axis_size("yl") * lax.axis_size("core")
    row_count, extent_y = wavefield.shape[2], wavefield.shape[3]
    extent_x = row_count * cut_count
    base = extent_y // RADIX
    freq_index = lax.axis_index(FREQ_AXES)
    cut_index = lax.axis_index(CUT_AXES)
    angular = (
        2.0 * math.pi * (band_low + band_width * (freq_index.astype(f32) + 0.5) / freq_total)
    )
    forward, inverse, turn_rows, turn_cols = dft_tables(extent_y)

    spectrum = call(
        lines_forward_kernel,
        jax.ShapeDtypeStruct((RADIX, 2, row_count, base), bf16),
        [pltpu.VMEM((RADIX, row_count, 2 * base), bf16)],
        wavefield[0], inverse, turn_rows,
    )
    spectrum, slowness, block_inverse = lax.optimization_barrier(
        (spectrum, slowness, block_inverse)
    )
    columns = lax.all_to_all(
        spectrum.reshape(RADIX, 2 * row_count, base), CUT_AXES, 0, 0, tiled=True
    )
    prop_re, prop_im = propagator(angular, cut_index, extent_x, extent_y)

    owner_id = slab_owner[0]
    with jax.named_scope("spread"):
        pieces = counts[1] * counts[2] * 16
        joined = jnp.concatenate(
            [slowness[0].T, block_inverse[0].reshape(-1, row_count)], axis=0
        )
        filled = joined.shape[0]
        joined = jnp.pad(joined, ((0, -filled % pieces), (0, 0)))
        share = from_owner(joined, owner_id)
        along_bits = bits_of(counts[2])[::-1]
        share = join_hops(share, "z", along_bits[:2])
        columns, prop_re, prop_im, share = lax.optimization_barrier(
            (columns, prop_re, prop_im, share)
        )
        share = join_hops(share, "z", along_bits[2:])
        joined = join_ring(share, "x")
        slab = joined[:extent_y]
        operators = join_hops(joined[extent_y:filled], "core")
        operators = join_ring(operators, "yl")
    shape = block_inverse.shape
    matrices = operators.reshape((cut_count,) + shape[1:]).transpose(1, 0, 2, 3, 4)
    matrices = matrices.reshape(2, -1, shape[3], shape[4])
    lengths = lax.dynamic_index_in_dim(block_lengths, owner_id, 0, keepdims=False)
    starts = jnp.cumsum(lengths) - lengths
    windows, pairs = block_windows(matrices, starts, lengths)
    phases = angular * depth_step * (slab.astype(f32) - slow_ref)
    cos_u, sin_u = jnp.cos(phases), jnp.sin(phases)

    rows_x = cut_index * row_count + jnp.arange(row_count, dtype=jnp.int32)
    offset_x = (rows_x - shot_position[0]).astype(f32) * grid_step
    offset_y = (jnp.arange(extent_y, dtype=jnp.int32) - shot_position[1]).astype(f32) * grid_step
    distance = jnp.sqrt(
        offset_x[None, :] ** 2 + offset_y[:, None] ** 2 + depth_step * depth_step
    )
    ray = angular * slow_ref * distance
    level = 1.0 / math.sqrt(freq_total)
    cos_r, sin_r = jnp.cos(ray) * level, jnp.sin(ray) * level

    restored = call(
        across_kernel,
        jax.ShapeDtypeStruct((RADIX, 2 * row_count, base), bf16),
        [
            pltpu.VMEM((RADIX, 2 * row_count, base), bf16),
            pltpu.VMEM((RADIX, 2 * row_count, base), f32),
        ],
        columns, prop_re, prop_im, forward, inverse, turn_cols,
    )
    row_field = lax.all_to_all(restored, CUT_AXES, 0, 0, tiled=True)
    capacity = block_inverse.shape[3]
    part = call(
        lines_inverse_kernel,
        jax.ShapeDtypeStruct(
            counts[1:] + (counts[0], extent_y // freq_total, row_count), bf16
        ),
        [
            pltpu.VMEM((RADIX, 2 * base, row_count), f32),
            pltpu.VMEM((2, extent_y + capacity, row_count), bf16),
            pltpu.VMEM((2, extent_y + capacity, row_count), f32),
        ],
        windows, row_field.reshape(RADIX, 2, row_count, base),
        cos_u, sin_u, cos_r, sin_r, pairs, inverse, turn_cols,
        scalars=1,
    )
    part = sum_over(part, "x", bf16)
    part = sum_over(part, "z", bf16)
    image = sum_over(part, "yh", f32)
    return image.T[None]


def solution(mesh):
    sizes = {"yh": 2, "x": 4, "z": 8, "yl": 4, "core": 2}
    if mesh.devices.size != math.prod(sizes.values()):
        sizes = {"yh": 1, "x": 1, "z": 1, "yl": 4, "core": 2}
    fine = Mesh(mesh.devices.reshape(tuple(sizes.values())), tuple(sizes))
    placed = (
        P(FREQ_AXES, None, CUT_AXES, None),
        P(FREQ_AXES, CUT_AXES, None),
        P(FREQ_AXES, None, CUT_AXES, None, None),
        P(),
        P(),
        P(),
    )
    return jax.shard_map(
        body, mesh=fine, in_specs=placed, out_specs=P(None, CUT_AXES, FREQ_AXES), check_vma=False
    )
```

time: 1560 us -> 286 us (0.18)
  the two profiles are of different devices: /device:TPU:8 before, /device:TPU:24 now
where the time goes in v1:
time: 286 us; the launch traced here: 285 us
  starting transfers between devices  78 us (27%)
  waiting for transfers between devices  56.8 us (20%)
  blocking collectives  48.5 us (17%)
  other arithmetic  39 us (14%)
  Pallas kernels  35 us (12%)
  local copies, waits for them, and re-layouts  22.2 us (8%)
  matrix products  4.34 us (2%)
    all_to_all x3, blocking collectives, sum_over(): terms = lax.all_to_all(part, axis, 0, 0)  48.5 us
    ppermute x8, starting transfers between devices, swap(): lax.ppermute(value, axis, [(i, i ^ bit) for i in range(lax.axis_size(axis...  38.5 us
    pallas_call x3, Pallas kernels, call(): pl.pallas_call(kernel, out_shape=out_shape, in_specs=[smem] * scalars + [...  35 us
    ppermute x6, waiting for transfers between devices, join_ring(): got = lax.ppermute(piece, axis, pairs)  28.3 us
    ppermute x8, waiting for transfers between devices, swap(): lax.ppermute(value, axis, [(i, i ^ bit) for i in range(lax.axis_size(axis...  18.4 us
    ppermute x6, starting transfers between devices, join_ring(): got = lax.ppermute(piece, axis, pairs)  17.4 us
    ppermute x3, waiting for transfers between devices, split_ring(): got = lax.ppermute(sent, axis, pairs)  10.2 us
    select_n x1, other arithmetic, propagator(): jnp.where(vertical > 0, jnp.sin(root_abs * depth_step), jnp.zeros_like(ro...  9.91 us
  transfers between devices with their start and end apart: 19, of which 11 were waited for; matrix products, arithmetic and copies ran while one was open for 22% of the time, Pallas kernels for 5%

profile of v1, /device:TPU:24, one launch (start us, length us, event | category | flops | bytes accessed | tf_op | source)
XLA Modules:
  0.0 285.2 jit_solution(1220342411396360222)
XLA Ops:
  0.0 5.7 %shard_map.100 = bf16[8,2,256,256]{3,2,1,0:T(8,128)(2,1)} custom-call(bf16[2,256,2048]{2,1,0:T(8,128)(2,1)} %bitcast.75, bf16[512,512]{1,0:T(8,128)(2,1)} %constant.249.clone.table.inverse, f32[16,256]{1,0:T(8,128)} %constant.250.clone.turn), custom_call_target="tpu_custom_call" | custom-call | tf_op jit(solution)/shard_map/pallas_call | solution.py:233
  5.7 9.2 %all-to-all-start = ((bf16[8,512,256]{2,1,0:T(8,128)(2,1)}), bf16[8,512,256]{2,1,0:T(8,128)(2,1)S(1)}, u32[]{:S(2)}, u32[]{:S(2)}) async-start(bf16[8,512,256]{2,1,0:T(8,128)(2,1)} %bitcast.70), calls=%async_computation | async-start | bytes 4194304 | tf_op jit(solution)/shard_map/all_to_all | solution.py:376
  15.2 1.2 fusion.15
  16.4 2.7 reshape.167
  19.1 4.0 %constant_dynamic-slice_fusion = (bf16[1,640,256]{1,0,2:T(2,128)(2,1)}, bf16[1,640,256]{1,0,2:T(2,128)(2,1)}, bf16[1,640,256]{1,0,2:T(2,128)(2,1)}, bf16[1,640,256]{1,0,2:T(2,128)(2,1)}) fusion(bf16[4,640,256]{1,0,2:T(4,128)(2,1)S(1)} %reshape.167, s32[]{:T(128)S(6)} %select_n.282, s32[]{:T(128)S(6)} %select_n.281, s32[]{:T(128)S(6)} %select_n.278, ...), kind=kLoop, calls=%fused_computation.80 | loop fusion | bytes 2621456 | tf_op jit(solution)/shard_map/spread/jit(dynamic_index_in_dim)/dynamic_slice | solution.py:273
  23.1 2.1 copy.36
  25.2 1.9 collective-permute-start
  27.1 2.0 copy.37
  29.1 1.9 collective-permute-start.1
  32.2 3.9 %collective-permute-start.2 = (bf16[640,256]{1,0:T(8,128)(2,1)}, bf16[640,256]{1,0:T(8,128)(2,1)S(1)}, u32[]{:S(2)}, u32[]{:S(2)}) collective-permute-start(bf16[640,256]{1,0:T(8,128)(2,1)} %bitcast.80), channel_id=1, source_target_pairs={{0,64},{64,128},{128,192},{192,0},{1,65},{65,129},{129,193},{193,1... | collective-permute-start | bytes 983048 | tf_op jit(solution)/shard_map/spread/ppermute | solution.py:276
  39.3 4.2 %collective-permute-done.1 = bf16[640,256]{1,0:T(8,128)(2,1)} collective-permute-done((bf16[640,256]{1,0:T(8,128)(2,1)}, bf16[640,256]{1,0:T(8,128)(2,1)}, u32[]{:S(2)}, u32[]{:S(2)}) %collective-permute-start.1) | collective-permute-done | bytes 327712 | tf_op jit(solution)/shard_map/spread/ppermute | solution.py:276
  43.5 6.0 %collective-permute-done.2 = bf16[640,256]{1,0:T(8,128)(2,1)S(1)} collective-permute-done((bf16[640,256]{1,0:T(8,128)(2,1)}, bf16[640,256]{1,0:T(8,128)(2,1)S(1)}, u32[]{:S(2)}, u32[]{:S(2)}) %collective-permute-start.2) | collective-permute-done | bytes 327712 | tf_op jit(solution)/shard_map/spread/ppermute | solution.py:276
  50.6 2.7 collective-permute-start.3
  53.3 9.7 %sine_multiply_fusion = (f32[2048,256]{1,0:T(8,128)}, f32[2048,256]{1,0:T(8,128)}) fusion(f32[2048]{0:T(1024)S(1)} %multiply_multiply_fusion, f32[256]{0:T(256)S(1)} %multiply_multiply_fusion.1, f32[]{:T(128)S(6)} %mul.117), kind=kLoop, calls=%fused_computation.15 | loop fusion | flops 2621440 | bytes 4203524 | tf_op jit(solution)/shard_map/mul | solution.py:417
  63.1 6.1 %collective-permute-start.4 = (bf16[160,256]{1,0:T(8,128)(2,1)S(1)}, bf16[160,256]{1,0:T(8,128)(2,1)S(1)}, u32[]{:S(2)}, u32[]{:S(2)}) collective-permute-start(bf16[160,256]{1,0:T(8,128)(2,1)S(1)} %broadcast_select_fusion.7), channel_id=1, source_target_pairs={{0,16},{8,24},{16,0},{24,8},{32,48},{40,56},{48,32},{56,40},{1,17}... | collective-permute-start | bytes 245768 | tf_op jit(solution)/shard_map/spread/ppermute | solution.py:293
  69.2 3.8 %collective-permute-done.4 = bf16[160,256]{1,0:T(8,128)(2,1)S(1)} collective-permute-done((bf16[160,256]{1,0:T(8,128)(2,1)S(1)}, bf16[160,256]{1,0:T(8,128)(2,1)S(1)}, u32[]{:S(2)}, u32[]{:S(2)}) %collective-permute-start.4) | collective-permute-done | bytes 81952 | tf_op jit(solution)/shard_map/spread/ppermute | solution.py:293
  73.0 8.7 %collective-permute-start.5 = (bf16[80,256]{1,0:T(8,128)(2,1)S(1)}, bf16[80,256]{1,0:T(8,128)(2,1)S(1)}, u32[]{:S(2)}, u32[]{:S(2)}) collective-permute-start(bf16[80,256]{1,0:T(8,128)(2,1)S(1)} %broadcast_select_fusion.11), channel_id=1, source_target_pairs={{0,32},{8,40},{16,48},{24,56},{32,0},{40,8},{48,16},{56,24},{1,33}... | collective-permute-start | bytes 122888 | tf_op jit(solution)/shard_map/spread/ppermute | solution.py:293
  81.8 1.9 collective-permute-done.5
  83.8 6.4 %collective-permute-start.6 = (bf16[80,256]{1,0:T(8,128)(2,1)S(1)}, bf16[80,256]{1,0:T(8,128)(2,1)S(1)}, u32[]{:S(2)}, u32[]{:S(2)}) collective-permute-start(bf16[80,256]{1,0:T(8,128)(2,1)S(1)} %select_select_fusion.2), channel_id=1, source_target_pairs={{0,256},{256,0},{1,257},{257,1},{2,258},{258,2},{3,259},{259,3},{4... | collective-permute-start | bytes 122888 | tf_op jit(solution)/shard_map/spread/ppermute | solution.py:293
  90.2 9.9 %fusion.2 = (f32[8,256,256]{2,1,0:T(8,128)}, f32[8,256,256]{2,1,0:T(8,128)}) fusion(f32[256]{0:T(256)S(1)} %fusion.35, f32[8,256]{1,0:T(8,128)S(1)} %fusion.32), kind=kLoop, calls=%fused_computation.6 | loop fusion | flops 4194304 | bytes 4203520 | tf_op jit(solution)/shard_map/jit(_where)/select_n | solution.py:261
  100.1 7.8 %collective-permute-start.7 = (bf16[80,256]{1,0:T(8,128)(2,1)S(1)}, bf16[80,256]{1,0:T(8,128)(2,1)S(1)}, u32[]{:S(2)}, u32[]{:S(2)}) collective-permute-start(bf16[80,256]{1,0:T(8,128)(2,1)S(1)} %broadcast_select_fusion.8), channel_id=1, source_target_pairs={{0,32},{8,40},{16,48},{24,56},{32,0},{40,8},{48,16},{56,24},{1,33}... | collective-permute-start | bytes 122888 | tf_op jit(solution)/shard_map/spread/ppermute | solution.py:293
  108.3 2.0 collective-permute-done.7
  110.4 2.9 %collective-permute-start.8 = (bf16[160,256]{1,0:T(8,128)(2,1)S(1)}, bf16[160,256]{1,0:T(8,128)(2,1)S(1)}, u32[]{:S(2)}, u32[]{:S(2)}) collective-permute-start(bf16[160,256]{1,0:T(8,128)(2,1)S(1)} %pad_maximum_fusion.3), channel_id=1, source_target_pairs={{0,16},{8,24},{16,0},{24,8},{32,48},{40,56},{48,32},{56,40},{1,17}... | collective-permute-start | bytes 245768 | tf_op jit(solution)/shard_map/spread/ppermute | solution.py:293
  113.4 4.4 %collective-permute-done.8 = bf16[160,256]{1,0:T(8,128)(2,1)S(1)} collective-permute-done((bf16[160,256]{1,0:T(8,128)(2,1)S(1)}, bf16[160,256]{1,0:T(8,128)(2,1)S(1)}, u32[]{:S(2)}, u32[]{:S(2)}) %collective-permute-start.8) | collective-permute-done | bytes 81952 | tf_op jit(solution)/shard_map/spread/ppermute | solution.py:293
  117.9 1.9 collective-permute-start.9
  119.9 5.2 %collective-permute-done.9 = bf16[320,256]{1,0:T(8,128)(2,1)S(1)} collective-permute-done((bf16[320,256]{1,0:T(8,128)(2,1)S(1)}, bf16[320,256]{1,0:T(8,128)(2,1)S(1)}, u32[]{:S(2)}, u32[]{:S(2)}) %collective-permute-start.9) | collective-permute-done | bytes 163872 | tf_op jit(solution)/shard_map/spread/ppermute | solution.py:293
  126.5 2.1 collective-permute-start.10
  128.7 13.1 %shard_map.101 = bf16[8,512,256]{2,1,0:T(8,128)(2,1)} custom-call(bf16[8,512,256]{2,1,0:T(8,128)(2,1)} %copy-done.1, f32[8,256,256]{2,1,0:T(8,128)} %get-tuple-element.16.prop_re, f32[8,256,256]{2,1,0:T(8,128)} %get-tuple-element.17.prop_im, bf16[512,512]{1,0:T(8,128)(2,1)} %constant.248.clone.forward, bf16[512,512]{1,0:T(8,128)(2,1)} %constant.249.clone.table.inverse, ...), custom_call_target="tpu_custom_call" | custom-call | tf_op jit(solution)/shard_map/pallas_call | solution.py:233
  141.8 5.1 %all-to-all-start.1 = ((bf16[8,512,256]{2,1,0:T(8,128)(2,1)}), bf16[8,512,256]{2,1,0:T(8,128)(2,1)S(1)}, u32[]{:S(2)}, u32[]{:S(2)}) async-start(bf16[8,512,256]{2,1,0:T(8,128)(2,1)} %shard_map.101), calls=%async_computation.1 | async-start | bytes 4194304 | tf_op jit(solution)/shard_map/all_to_all | solution.py:428
  146.9 3.1 %collective-permute-start.11 = (bf16[640,256]{1,0:T(8,128)(2,1)}, bf16[640,256]{1,0:T(8,128)(2,1)S(1)}, u32[]{:S(2)}, u32[]{:S(2)}) collective-permute-start(bf16[640,256]{1,0:T(8,128)(2,1)} %pad_maximum_fusion), channel_id=1, source_target_pairs={{0,128},{64,192},{128,0},{192,64},{1,129},{65,193},{129,1},{193,65... | collective-permute-start | bytes 983048 | tf_op jit(solution)/shard_map/spread/ppermute | solution.py:287
  150.0 4.0 %collective-permute-start.12 = (bf16[640,256]{1,0:T(8,128)(2,1)}, bf16[640,256]{1,0:T(8,128)(2,1)S(1)}, u32[]{:S(2)}, u32[]{:S(2)}) collective-permute-start(bf16[640,256]{1,0:T(8,128)(2,1)} %pad_maximum_fusion), channel_id=1, source_target_pairs={{0,192},{64,0},{128,64},{192,128},{1,193},{65,1},{129,65},{193,129... | collective-permute-start | bytes 983048 | tf_op jit(solution)/shard_map/spread/ppermute | solution.py:287
  156.1 4.1 %collective-permute-done.11 = bf16[640,256]{1,0:T(8,128)(2,1)S(1)} collective-permute-done((bf16[640,256]{1,0:T(8,128)(2,1)}, bf16[640,256]{1,0:T(8,128)(2,1)S(1)}, u32[]{:S(2)}, u32[]{:S(2)}) %collective-permute-start.11) | collective-permute-done | bytes 327712 | tf_op jit(solution)/shard_map/spread/ppermute | solution.py:287
  160.3 7.6 %collective-permute-done.12 = bf16[640,256]{1,0:T(8,128)(2,1)S(1)} collective-permute-done((bf16[640,256]{1,0:T(8,128)(2,1)}, bf16[640,256]{1,0:T(8,128)(2,1)S(1)}, u32[]{:S(2)}, u32[]{:S(2)}) %collective-permute-start.12) | collective-permute-done | bytes 327712 | tf_op jit(solution)/shard_map/spread/ppermute | solution.py:287
  168.5 1.9 collective-permute-start.13
  171.9 2.3 collective-permute-start.14
  174.2 8.4 %fusion.11 = (f32[2048,256]{1,0:T(8,128)}, f32[2048,256]{1,0:T(8,128)}) fusion(f32[]{:T(128)S(6)} %mul.114, bf16[2560,256]{1,0:T(8,128)(2,1)S(1)} %bitcast.74), kind=kLoop, calls=%fused_computation.19 | loop fusion | flops 1572864 | bytes 5242884 | tf_op jit(solution)/shard_map/sin | solution.py:407
  182.7 3.5 %collective-permute-start.15 = (bf16[320,256]{1,0:T(8,128)(2,1)S(1)}, bf16[320,256]{1,0:T(8,128)(2,1)S(1)}, u32[]{:S(2)}, u32[]{:S(2)}) collective-permute-start(bf16[320,256]{1,0:T(8,128)(2,1)S(1)} %pad_maximum_fusion.2), channel_id=1, source_target_pairs={{0,4},{2,6},{4,0},{6,2},{1,5},{3,7},{5,1},{7,3},{8,12},{10,14},{12... | collective-permute-start | bytes 491528 | tf_op jit(solution)/shard_map/spread/ppermute | solution.py:287
  186.2 2.5 collective-permute-start.16
  190.9 16.5 %collective-permute-done.15 = bf16[320,256]{1,0:T(8,128)(2,1)S(1)} collective-permute-done((bf16[320,256]{1,0:T(8,128)(2,1)S(1)}, bf16[320,256]{1,0:T(8,128)(2,1)S(1)}, u32[]{:S(2)}, u32[]{:S(2)}) %collective-permute-start.15) | collective-permute-done | bytes 163872 | tf_op jit(solution)/shard_map/spread/ppermute | solution.py:287
  208.8 1.7 reshape.170
  210.6 2.0 fusion.14
  212.7 2.3 fusion.13
  215.2 3.0 %maximum_maximum_fusion.pairs = bf16[40,160,160]{2,1,0:T(8,128)(2,1)} fusion(bf16[40,80,80]{2,1,0:T(8,128)(2,1)S(1)} %get-tuple-element.22, bf16[40,80,80]{2,1,0:T(8,128)(2,1)S(1)} %get-tuple-element.21, bf16[40,80,80]{2,1,0:T(8,128)(2,1)S(1)} %fusion.36), kind=kLoop, calls=%fused_computation | loop fusion | flops 8192000 | bytes 3584000 | tf_op jit(solution)/shard_map/concatenate | solution.py:350
  218.2 1.4 copy-done
  219.6 16.3 %shard_map.102 = bf16[4,8,2,32,256]{4,3,2,1,0:T(8,128)(2,1)} custom-call(s32[40]{0:T(128)} %and_select_fusion.1.windows, bf16[8,2,256,256]{3,2,1,0:T(8,128)(2,1)} %bitcast.69, f32[2048,256]{1,0:T(8,128)} %get-tuple-element.26.cos_u, f32[2048,256]{1,0:T(8,128)} %get-tuple-element.25.sin_u, f32[2048,256]{1,0:T(8,128)} %get-tuple-element.40.cos_r, ...), custom_call_target="tpu_custom_call" | custom-call | tf_op jit(solution)/shard_map/pallas_call | solution.py:233
  235.8 19.8 %all_to_all.25 = bf16[4,8,2,32,256]{4,3,2,1,0:T(8,128)(2,1)S(1)} all-to-all(bf16[4,8,2,32,256]{4,3,2,1,0:T(8,128)(2,1)} %shard_map.102), channel_id=1, replica_groups=mesh['yh'=2,'x'=4,'z'=8,'yl'=4,'core'=2] {'x'}, dimensions={0} | all-to-all | bytes 2097152 | tf_op jit(solution)/shard_map/all_to_all | solution.py:332
  255.9 18.3 %all_to_all.26 = bf16[8,2,32,256]{3,2,1,0:T(8,128)(2,1)S(1)} all-to-all(bf16[8,2,32,256]{3,2,1,0:T(8,128)(2,1)S(1)} %reduce_sum.33), channel_id=1, replica_groups=mesh['yh'=2,'x'=4,'z'=8,'yl'=4,'core'=2] {'z'}, dimensions={0} | all-to-all | bytes 524288 | tf_op jit(solution)/shard_map/all_to_all | solution.py:332
  274.2 10.4 %all_to_all.27 = bf16[2,32,256]{2,1,0:T(8,128)(2,1)S(1)} all-to-all(bf16[2,32,256]{2,1,0:T(8,128)(2,1)S(1)} %reduce_sum.34), channel_id=1, replica_groups=mesh['yh'=2,'x'=4,'z'=8,'yl'=4,'core'=2] {'yh'}, dimensions={0} | all-to-all | bytes 65536 | tf_op jit(solution)/shard_map/all_to_all | solution.py:332
  (78 shorter events, 16.0 us)
Async XLA Ops:
  5.7 9.2 %copy-start.7 = (bf16[1,2,5,64,64]{4,3,2,1,0:T(8,128)(2,1)S(1)}, bf16[1,2,5,64,64]{4,3,2,1,0:T(8,128)(2,1)}, u32[]{:S(2)}) copy-start(bf16[1,2,5,64,64]{4,3,2,1,0:T(8,128)(2,1)} %param.12) | copy-start | bytes 245764
  5.7 9.5 %copy-start.6 = (bf16[1,256,2048]{2,1,0:T(8,128)(2,1)S(1)}, bf16[1,256,2048]{2,1,0:T(8,128)(2,1)}, u32[]{:S(2)}) copy-start(bf16[1,256,2048]{2,1,0:T(8,128)(2,1)} %param.11) | copy-start | bytes 3145732
  5.7 112.2 %all-to-all-start = ((bf16[8,512,256]{2,1,0:T(8,128)(2,1)}), bf16[8,512,256]{2,1,0:T(8,128)(2,1)S(1)}, u32[]{:S(2)}, u32[]{:S(2)}) async-start(bf16[8,512,256]{2,1,0:T(8,128)(2,1)} %bitcast.70), calls=%async_computation | async-start | bytes 4194304 | tf_op jit(solution)/shard_map/all_to_all | solution.py:376
  23.1 8.0 %copy-start.3 = (bf16[1,640,256]{1,0,2:T(2,128)(2,1)S(1)}, bf16[1,640,256]{1,0,2:T(2,128)(2,1)}, u32[]{:S(2)}) copy-start(bf16[1,640,256]{1,0,2:T(2,128)(2,1)} %get-tuple-element.28) | copy-start | bytes 983044
  23.1 13.8 %copy-start.2 = (bf16[1,640,256]{1,0,2:T(2,128)(2,1)S(1)}, bf16[1,640,256]{1,0,2:T(2,128)(2,1)}, u32[]{:S(2)}) copy-start(bf16[1,640,256]{1,0,2:T(2,128)(2,1)} %get-tuple-element.27) | copy-start | bytes 983044
  23.1 14.3 %copy-start.9 = (s32[2]{0:T(128)S(1)}, s32[2]{0:T(128)}, u32[]{:S(2)}) copy-start(s32[2]{0:T(128)} %param.15) | copy-start | bytes 28
  25.2 14.1 %collective-permute-start = (bf16[640,256]{1,0:T(8,128)(2,1)}, bf16[640,256]{1,0:T(8,128)(2,1)}, u32[]{:S(2)}, u32[]{:S(2)}) collective-permute-start(bf16[640,256]{1,0:T(8,128)(2,1)} %bitcast.78), channel_id=1, source_target_pairs={{0,192},{64,0},{128,64},{192,128},{1,193},{65,1},{129,65},{193,129... | collective-permute-start | bytes 983048 | tf_op jit(solution)/shard_map/spread/ppermute | solution.py:276
  29.1 14.3 %collective-permute-start.1 = (bf16[640,256]{1,0:T(8,128)(2,1)}, bf16[640,256]{1,0:T(8,128)(2,1)}, u32[]{:S(2)}, u32[]{:S(2)}) collective-permute-start(bf16[640,256]{1,0:T(8,128)(2,1)} %bitcast.79), channel_id=1, source_target_pairs={{0,128},{64,192},{128,0},{192,64},{1,129},{65,193},{129,1},{193,65... | collective-permute-start | bytes 983048 | tf_op jit(solution)/shard_map/spread/ppermute | solution.py:276
  32.2 17.3 %collective-permute-start.2 = (bf16[640,256]{1,0:T(8,128)(2,1)}, bf16[640,256]{1,0:T(8,128)(2,1)S(1)}, u32[]{:S(2)}, u32[]{:S(2)}) collective-permute-start(bf16[640,256]{1,0:T(8,128)(2,1)} %bitcast.80), channel_id=1, source_target_pairs={{0,64},{64,128},{128,192},{192,0},{1,65},{65,129},{129,193},{193,1... | collective-permute-start | bytes 983048 | tf_op jit(solution)/shard_map/spread/ppermute | solution.py:276
  50.6 12.5 %collective-permute-start.3 = (bf16[320,256]{1,0:T(8,128)(2,1)S(1)}, bf16[320,256]{1,0:T(8,128)(2,1)S(1)}, u32[]{:S(2)}, u32[]{:S(2)}) collective-permute-start(bf16[320,256]{1,0:T(8,128)(2,1)S(1)} %broadcast_select_fusion.2), channel_id=1, source_target_pairs={{0,8},{8,0},{16,24},{24,16},{32,40},{40,32},{48,56},{56,48},{1,9},... | collective-permute-start | bytes 491528 | tf_op jit(solution)/shard_map/spread/ppermute | solution.py:293
  63.1 9.9 %collective-permute-start.4 = (bf16[160,256]{1,0:T(8,128)(2,1)S(1)}, bf16[160,256]{1,0:T(8,128)(2,1)S(1)}, u32[]{:S(2)}, u32[]{:S(2)}) collective-permute-start(bf16[160,256]{1,0:T(8,128)(2,1)S(1)} %broadcast_select_fusion.7), channel_id=1, source_target_pairs={{0,16},{8,24},{16,0},{24,8},{32,48},{40,56},{48,32},{56,40},{1,17}... | collective-permute-start | bytes 245768 | tf_op jit(solution)/shard_map/spread/ppermute | solution.py:293
  73.0 10.7 %collective-permute-start.5 = (bf16[80,256]{1,0:T(8,128)(2,1)S(1)}, bf16[80,256]{1,0:T(8,128)(2,1)S(1)}, u32[]{:S(2)}, u32[]{:S(2)}) collective-permute-start(bf16[80,256]{1,0:T(8,128)(2,1)S(1)} %broadcast_select_fusion.11), channel_id=1, source_target_pairs={{0,32},{8,40},{16,48},{24,56},{32,0},{40,8},{48,16},{56,24},{1,33}... | collective-permute-start | bytes 122888 | tf_op jit(solution)/shard_map/spread/ppermute | solution.py:293
  83.7 24.2 %copy-start.8 = (s32[64,40]{0,1:T(8,128)S(1)}, s32[64,40]{0,1:T(8,128)}, u32[]{:S(2)}) copy-start(s32[64,40]{0,1:T(8,128)} %param.13) | copy-start | bytes 30724
  83.8 16.3 %collective-permute-start.6 = (bf16[80,256]{1,0:T(8,128)(2,1)S(1)}, bf16[80,256]{1,0:T(8,128)(2,1)S(1)}, u32[]{:S(2)}, u32[]{:S(2)}) collective-permute-start(bf16[80,256]{1,0:T(8,128)(2,1)S(1)} %select_select_fusion.2), channel_id=1, source_target_pairs={{0,256},{256,0},{1,257},{257,1},{2,258},{258,2},{3,259},{259,3},{4... | collective-permute-start | bytes 122888 | tf_op jit(solution)/shard_map/spread/ppermute | solution.py:293
  100.1 10.2 %collective-permute-start.7 = (bf16[80,256]{1,0:T(8,128)(2,1)S(1)}, bf16[80,256]{1,0:T(8,128)(2,1)S(1)}, u32[]{:S(2)}, u32[]{:S(2)}) collective-permute-start(bf16[80,256]{1,0:T(8,128)(2,1)S(1)} %broadcast_select_fusion.8), channel_id=1, source_target_pairs={{0,32},{8,40},{16,48},{24,56},{32,0},{40,8},{48,16},{56,24},{1,33}... | collective-permute-start | bytes 122888 | tf_op jit(solution)/shard_map/spread/ppermute | solution.py:293
  110.4 7.4 %collective-permute-start.8 = (bf16[160,256]{1,0:T(8,128)(2,1)S(1)}, bf16[160,256]{1,0:T(8,128)(2,1)S(1)}, u32[]{:S(2)}, u32[]{:S(2)}) collective-permute-start(bf16[160,256]{1,0:T(8,128)(2,1)S(1)} %pad_maximum_fusion.3), channel_id=1, source_target_pairs={{0,16},{8,24},{16,0},{24,8},{32,48},{40,56},{48,32},{56,40},{1,17}... | collective-permute-start | bytes 245768 | tf_op jit(solution)/shard_map/spread/ppermute | solution.py:293
  117.9 10.8 %copy-start.1 = (bf16[8,512,256]{2,1,0:T(8,128)(2,1)}, bf16[8,512,256]{2,1,0:T(8,128)(2,1)S(1)}, u32[]{:S(2)}) copy-start(bf16[8,512,256]{2,1,0:T(8,128)(2,1)S(1)} %all-to-all-done.field) | copy-start | bytes 6291460
  117.9 7.2 %collective-permute-start.9 = (bf16[320,256]{1,0:T(8,128)(2,1)S(1)}, bf16[320,256]{1,0:T(8,128)(2,1)S(1)}, u32[]{:S(2)}, u32[]{:S(2)}) collective-permute-start(bf16[320,256]{1,0:T(8,128)(2,1)S(1)} %pad_maximum_fusion.1), channel_id=1, source_target_pairs={{0,8},{8,0},{16,24},{24,16},{32,40},{40,32},{48,56},{56,48},{1,9},... | collective-permute-start | bytes 491528 | tf_op jit(solution)/shard_map/spread/ppermute | solution.py:293
  125.1 0.7 copy-start.4
  125.1 1.4 copy-start.5
  126.5 28.6 %collective-permute-start.10 = (bf16[640,256]{1,0:T(8,128)(2,1)}, bf16[640,256]{1,0:T(8,128)(2,1)}, u32[]{:S(2)}, u32[]{:S(2)}) collective-permute-start(bf16[640,256]{1,0:T(8,128)(2,1)} %pad_maximum_fusion), channel_id=1, source_target_pairs={{0,64},{64,128},{128,192},{192,0},{1,65},{65,129},{129,193},{193,1... | collective-permute-start | bytes 983048 | tf_op jit(solution)/shard_map/spread/ppermute | solution.py:287
  141.8 76.4 %all-to-all-start.1 = ((bf16[8,512,256]{2,1,0:T(8,128)(2,1)}), bf16[8,512,256]{2,1,0:T(8,128)(2,1)S(1)}, u32[]{:S(2)}, u32[]{:S(2)}) async-start(bf16[8,512,256]{2,1,0:T(8,128)(2,1)} %shard_map.101), calls=%async_computation.1 | async-start | bytes 4194304 | tf_op jit(solution)/shard_map/all_to_all | solution.py:428
  146.9 13.3 %collective-permute-start.11 = (bf16[640,256]{1,0:T(8,128)(2,1)}, bf16[640,256]{1,0:T(8,128)(2,1)S(1)}, u32[]{:S(2)}, u32[]{:S(2)}) collective-permute-start(bf16[640,256]{1,0:T(8,128)(2,1)} %pad_maximum_fusion), channel_id=1, source_target_pairs={{0,128},{64,192},{128,0},{192,64},{1,129},{65,193},{129,1},{193,65... | collective-permute-start | bytes 983048 | tf_op jit(solution)/shard_map/spread/ppermute | solution.py:287
  150.0 17.9 %collective-permute-start.12 = (bf16[640,256]{1,0:T(8,128)(2,1)}, bf16[640,256]{1,0:T(8,128)(2,1)S(1)}, u32[]{:S(2)}, u32[]{:S(2)}) collective-permute-start(bf16[640,256]{1,0:T(8,128)(2,1)} %pad_maximum_fusion), channel_id=1, source_target_pairs={{0,192},{64,0},{128,64},{192,128},{1,193},{65,1},{129,65},{193,129... | collective-permute-start | bytes 983048 | tf_op jit(solution)/shard_map/spread/ppermute | solution.py:287
  168.5 3.4 %collective-permute-start.13 = (bf16[160,256]{1,0:T(8,128)(2,1)}, bf16[160,256]{1,0:T(8,128)(2,1)S(1)}, u32[]{:S(2)}, u32[]{:S(2)}) collective-permute-start(bf16[160,256]{1,0:T(8,128)(2,1)} %slice.57), channel_id=1, source_target_pairs={{0,1},{1,0},{2,3},{3,2},{4,5},{5,4},{6,7},{7,6},{8,9},{9,8},{10,11... | collective-permute-start | bytes 245768 | tf_op jit(solution)/shard_map/spread/ppermute | solution.py:293
  171.9 18.3 %collective-permute-start.14 = (bf16[320,256]{1,0:T(8,128)(2,1)S(1)}, bf16[320,256]{1,0:T(8,128)(2,1)S(1)}, u32[]{:S(2)}, u32[]{:S(2)}) collective-permute-start(bf16[320,256]{1,0:T(8,128)(2,1)S(1)} %pad_maximum_fusion.2), channel_id=1, source_target_pairs={{0,2},{2,4},{4,6},{6,0},{1,3},{3,5},{5,7},{7,1},{8,10},{10,12},{12... | collective-permute-start | bytes 491528 | tf_op jit(solution)/shard_map/spread/ppermute | solution.py:287
  182.7 24.8 %collective-permute-start.15 = (bf16[320,256]{1,0:T(8,128)(2,1)S(1)}, bf16[320,256]{1,0:T(8,128)(2,1)S(1)}, u32[]{:S(2)}, u32[]{:S(2)}) collective-permute-start(bf16[320,256]{1,0:T(8,128)(2,1)S(1)} %pad_maximum_fusion.2), channel_id=1, source_target_pairs={{0,4},{2,6},{4,0},{6,2},{1,5},{3,7},{5,1},{7,3},{8,12},{10,14},{12... | collective-permute-start | bytes 491528 | tf_op jit(solution)/shard_map/spread/ppermute | solution.py:287
  186.2 21.9 %collective-permute-start.16 = (bf16[320,256]{1,0:T(8,128)(2,1)S(1)}, bf16[320,256]{1,0:T(8,128)(2,1)S(1)}, u32[]{:S(2)}, u32[]{:S(2)}) collective-permute-start(bf16[320,256]{1,0:T(8,128)(2,1)S(1)} %pad_maximum_fusion.2), channel_id=1, source_target_pairs={{0,6},{2,0},{4,2},{6,4},{1,7},{3,1},{5,3},{7,5},{8,14},{10,8},{12,... | collective-permute-start | bytes 491528 | tf_op jit(solution)/shard_map/spread/ppermute | solution.py:287
  218.2 1.4 copy-start

commit v2 on v1

v2 whole, which is shorter than its diff:
```python
import math

import jax
import jax.numpy as jnp
import numpy as np
from jax import lax
from jax.experimental import pallas as pl
from jax.experimental.pallas import tpu as pltpu
from jax.sharding import Mesh, PartitionSpec as P

grid_step = 0.0125
depth_step = 0.02
slow_ref = 0.4
band_low = 5.0
band_width = 55.0

INTERPRET = False
FREQ_AXES = ("yh", "x", "z")
CUT_AXES = ("yl", "core")
RADIX = 8
BLOCK_GROUP = 4
f32 = jnp.float32
bf16 = jnp.bfloat16


def dft_tables(extent):
    base = extent // RADIX
    ids = np.arange(base)
    angle = 2.0 * np.pi / base * ((ids[:, None] * ids[None, :]) % base)
    cosine = np.cos(angle) / math.sqrt(base)
    sine = np.sin(angle) / math.sqrt(base)
    inverse = np.block([[cosine, -sine], [sine, cosine]])
    twists = 2.0 * np.pi / extent * (np.arange(RADIX)[:, None] * np.arange(extent)[None, :])
    turn = np.stack([np.cos(twists), np.sin(twists)], axis=1) / math.sqrt(RADIX)
    turn = turn.reshape(2 * RADIX, extent).astype(np.float32)
    return jnp.asarray(inverse, bf16), jnp.asarray(turn)


def fft4(parts, s):
    (r0, i0), (r1, i1), (r2, i2), (r3, i3) = parts
    ar, ai, br, bi = r0 + r2, i0 + i2, r0 - r2, i0 - i2
    cr, ci, dr, di = r1 + r3, i1 + i3, r1 - r3, i1 - i3
    if s > 0:
        one, three = (br - di, bi + dr), (br + di, bi - dr)
    else:
        one, three = (br + di, bi - dr), (br - di, bi + dr)
    return [(ar + cr, ai + ci), one, (ar - cr, ai - ci), three]


def fft8(parts, s):
    even = fft4(parts[0::2], s)
    odd = fft4(parts[1::2], s)
    half = math.sqrt(0.5)
    (r0, i0), (r1, i1), (r2, i2), (r3, i3) = odd
    if s > 0:
        turned = [
            (r0, i0),
            ((r1 - i1) * half, (i1 + r1) * half),
            (-i2, r2),
            ((r3 + i3) * -half, (r3 - i3) * half),
        ]
    else:
        turned = [
            (r0, i0),
            ((r1 + i1) * half, (i1 - r1) * half),
            (i2, -r2),
            ((i3 - r3) * half, (r3 + i3) * -half),
        ]
    low = [(e[0] + t[0], e[1] + t[1]) for e, t in zip(even, turned)]
    high = [(e[0] - t[0], e[1] - t[1]) for e, t in zip(even, turned)]
    return low + high


def twist(value, cosine, sine, s):
    real, imag = value
    if s > 0:
        return (real * cosine - imag * sine, imag * cosine + real * sine)
    return (real * cosine + imag * sine, imag * cosine - real * sine)


def lines_forward_kernel(me, field, table, turn, *outs_mid):
    outs, mid = outs_mid[:RADIX], outs_mid[RADIX]
    rows, base = mid.shape[1], mid.shape[2] // 2

    def step(tile, carry):
        at = pl.ds(pl.multiple_of(tile * 16, 16), 16)
        for lane in range(0, base, 128):
            parts = []
            for a in range(RADIX):
                here = pl.ds(a * base + lane, 128)
                parts.append((field[0, at, here].astype(f32), field[1, at, here].astype(f32)))
            for k, value in enumerate(fft8(parts, -1)):
                cosine = turn[2 * k : 2 * k + 1, lane : lane + 128]
                sine = turn[2 * k + 1 : 2 * k + 2, lane : lane + 128]
                real, imag = twist(value, cosine, sine, -1)
                mid[k, at, pl.ds(lane, 128)] = real.astype(bf16)
                mid[k, at, pl.ds(base + lane, 128)] = imag.astype(bf16)
        return carry

    lax.fori_loop(0, rows // 16, step, 0)
    for d, out in enumerate(outs):
        both = jnp.dot(mid[(me[0] + d) % RADIX], table[...], preferred_element_type=f32)
        out[:rows] = both[:, :base].astype(bf16)
        out[rows:] = both[:, base:].astype(bf16)


def across_kernel(*refs):
    fields, refs = refs[:RADIX], refs[RADIX:]
    prop_re, prop_im, table, turn = refs[:4]
    outs, (mid, back) = refs[4 : 4 + RADIX], refs[4 + RADIX :]
    base, cols = prop_re.shape[1], prop_re.shape[2]

    def fore(tile, carry):
        at = pl.multiple_of(tile * 16, 16)
        for lane in range(0, cols, 128):
            here = pl.ds(lane, 128)
            parts = []
            for field in fields:
                parts.append(
                    (
                        field[pl.ds(at, 16), here].astype(f32),
                        field[pl.ds(base + at, 16), here].astype(f32),
                    )
                )
            for k, value in enumerate(fft8(parts, 1)):
                cosine = turn[pl.ds(at, 16), 2 * k : 2 * k + 1]
                sine = turn[pl.ds(at, 16), 2 * k + 1 : 2 * k + 2]
                real, imag = twist(value, cosine, sine, -1)
                mid[k, pl.ds(at, 16), here] = real.astype(bf16)
                mid[k, pl.ds(base + at, 16), here] = (-imag).astype(bf16)
        return carry

    lax.fori_loop(0, base // 16, fore, 0)
    for k in range(RADIX):
        both = jnp.dot(table[...], mid[k], preferred_element_type=f32)
        real, minus = both[:base], both[base:]
        p_re, p_im = prop_re[k], prop_im[k]
        mid[k, :base] = (real * p_re + minus * p_im).astype(bf16)
        mid[k, base:] = (real * p_im - minus * p_re).astype(bf16)
        back[k] = jnp.dot(table[...], mid[k], preferred_element_type=f32)

    def aft(tile, carry):
        at = pl.multiple_of(tile * 16, 16)
        for lane in range(0, cols, 128):
            here = pl.ds(lane, 128)
            parts = []
            for k in range(RADIX):
                cosine = turn[pl.ds(at, 16), 2 * k : 2 * k + 1]
                sine = turn[pl.ds(at, 16), 2 * k + 1 : 2 * k + 2]
                value = (back[k, pl.ds(at, 16), here], back[k, pl.ds(base + at, 16), here])
                parts.append(twist(value, cosine, sine, 1))
            for out, (real, imag) in zip(outs, fft8(parts, 1)):
                out[pl.ds(at, 16), here] = real.astype(bf16)
                out[pl.ds(base + at, 16), here] = imag.astype(bf16)
        return carry

    lax.fori_loop(0, base // 16, aft, 0)


def lines_inverse_kernel(me, windows, *refs):
    fields, refs = refs[:RADIX], refs[RADIX:]
    cos_u, sin_u, cos_r, sin_r, pairs, table, turn, out, back, turned, final = refs
    rows, base = fields[0].shape[0] // 2, fields[0].shape[1]
    blocks, reach = pairs.shape[0], pairs.shape[1] // 2
    tail = pl.ds(RADIX * base, turned.shape[1] - RADIX * base)
    turned[:, tail, :] = jnp.zeros((2, tail.size, rows), bf16)
    for d, field in enumerate(fields):
        first = lax.dot_general(
            table[:, :base], field[:rows], (((1,), (1,)), ((), ())), preferred_element_type=f32
        )
        second = lax.dot_general(
            table[:, base:], field[rows:], (((1,), (1,)), ((), ())), preferred_element_type=f32
        )
        back[(me[0] + RADIX - d) % RADIX] = first + second

    def aft(tile, carry):
        at = pl.multiple_of(tile * 16, 16)
        for lane in range(0, rows, 128):
            here = pl.ds(lane, 128)
            parts = []
            for k in range(RADIX):
                cosine = turn[pl.ds(at, 16), 2 * k : 2 * k + 1]
                sine = turn[pl.ds(at, 16), 2 * k + 1 : 2 * k + 2]
                value = (back[k, pl.ds(at, 16), here], back[k, pl.ds(base + at, 16), here])
                parts.append(twist(value, cosine, sine, 1))
            for a, (real, imag) in enumerate(fft8(parts, 1)):
                cell = pl.ds(a * base + at, 16)
                cosine, sine = cos_u[cell, here], sin_u[cell, here]
                u_re = (real * cosine - imag * sine).astype(bf16)
                u_im = (real * sine + imag * cosine).astype(bf16)
                turned[0, cell, here] = u_re
                turned[1, cell, here] = u_im
                final[0, cell, here] = u_re.astype(f32)
                final[1, cell, here] = u_im.astype(f32)
        return carry

    lax.fori_loop(0, base // 16, aft, 0)

    def some_blocks(group, carry):
        cells, changes = [], []
        for one in range(BLOCK_GROUP):
            c = group * BLOCK_GROUP + one
            cell = pl.ds(pl.multiple_of(windows[c] * 16, 16), reach)
            both = jnp.concatenate([turned[0, cell, :], turned[1, cell, :]], axis=0)
            cells.append(cell)
            changes.append(jnp.dot(pairs[c], both, preferred_element_type=f32))
        for cell, change in zip(cells, changes):
            final[0, cell, :] += change[:reach]
            final[1, cell, :] += change[reach:]
        return carry

    lax.fori_loop(0, blocks // BLOCK_GROUP, some_blocks, 0)

    def image(tile, carry):
        cell = pl.ds(pl.multiple_of(tile * 16, 16), 16)
        across, _, along, piece = out.shape[:4]
        owner, place = tile * 16 // piece, tile * 16 % piece
        spot = pl.ds(pl.multiple_of(place, 16), 16)
        out[owner // along % across, owner // (along * across), owner % along, spot, :] = (
            final[0, cell, :] * cos_r[cell, :] - final[1, cell, :] * sin_r[cell, :]
        ).astype(bf16)
        return carry

    lax.fori_loop(0, RADIX * base // 16, image, 0)


def call(kernel, out_shape, scratch, *operands, scalars=0):
    smem = pl.BlockSpec(memory_space=pltpu.SMEM)
    vmem = pl.BlockSpec(memory_space=pltpu.VMEM)
    return pl.pallas_call(
        kernel,
        out_shape=out_shape,
        in_specs=[smem] * scalars + [vmem] * (len(operands) - scalars),
        out_specs=jax.tree.map(lambda _: vmem, out_shape),
        scratch_shapes=scratch,
        interpret=INTERPRET,
    )(*operands)


def wave_numbers(indices, extent):
    signed = jnp.where(indices < extent // 2, indices, indices - extent)
    return signed.astype(f32) * (2.0 * math.pi / (extent * grid_step))


def propagator(angular, cut_index, extent_x, extent_y):
    cross_ids = (
        jnp.arange(RADIX, dtype=jnp.int32)[:, None]
        + RADIX * jnp.arange(extent_x // RADIX, dtype=jnp.int32)[None, :]
    )
    line_ids = cut_index + RADIX * jnp.arange(extent_y // RADIX, dtype=jnp.int32)
    wave_x = wave_numbers(cross_ids, extent_x)
    wave_y = wave_numbers(line_ids, extent_y)
    vertical = (angular * slow_ref) ** 2 - wave_x[:, :, None] ** 2 - wave_y[None, None, :] ** 2
    root_abs = jnp.sqrt(jnp.abs(vertical))
    real_part = jnp.where(
        vertical > 0, jnp.cos(root_abs * depth_step), jnp.exp(-root_abs * depth_step)
    )
    imag_part = jnp.where(vertical > 0, jnp.sin(root_abs * depth_step), jnp.zeros_like(root_abs))
    return (real_part, imag_part)


def rotate(values, axes):
    size = math.prod(lax.axis_size(axis) for axis in axes)
    got = [values[0]]
    for d in range(1, size):
        got.append(lax.ppermute(values[d], axes, [(i, (i + d) % size) for i in range(size)]))
    return got


def split(value, axis, owner):
    size = lax.axis_size(axis)
    shaped = value.reshape((size, value.shape[0] // size) + value.shape[1:])
    shaped = lax.all_to_all(shaped, axis, 0, 0)
    return lax.dynamic_index_in_dim(shaped, owner, 0, keepdims=False)


def join(piece, axis):
    copies = jnp.broadcast_to(piece[None], (lax.axis_size(axis),) + piece.shape)
    copies = lax.all_to_all(copies, axis, 0, 0)
    return copies.reshape((-1,) + piece.shape[1:])


def swap(value, axis, bit):
    return lax.ppermute(value, axis, [(i, i ^ bit) for i in range(lax.axis_size(axis))])


def from_owner(value, owner_id):
    across, along = lax.axis_size("x"), lax.axis_size("z")
    piece = split(value, "x", owner_id // along % across)
    piece = split(piece, "z", owner_id % along)
    if lax.axis_size("yh") > 1:
        other = swap(piece, "yh", 1)
        same = lax.axis_index("yh") == owner_id // (across * along)
        piece = jnp.where(same, piece, other)
    return piece


def sum_over(part, axis, kind):
    terms = lax.all_to_all(part, axis, 0, 0, tiled=True)
    return jnp.sum(terms.astype(f32), axis=0).astype(kind)


def block_windows(matrices, starts, lengths):
    capacity = matrices.shape[2]
    reach = capacity + 16
    windows = starts // 16
    slots = jnp.arange(capacity, dtype=jnp.int32)
    spots = jnp.arange(reach, dtype=jnp.int32)
    place = (spots[None, :, None] == slots[None, None, :] + (starts % 16)[:, None, None]) & (
        slots[None, None, :] < lengths[:, None, None]
    )
    place = place.astype(bf16)
    moved = jnp.einsum("cia,dcab->dcib", place, matrices, preferred_element_type=f32).astype(bf16)
    moved = jnp.einsum("dcib,cjb->dcij", moved, place, preferred_element_type=f32).astype(bf16)
    upper = jnp.concatenate([moved[0], -moved[1]], axis=2)
    lower = jnp.concatenate([moved[1], moved[0]], axis=2)
    return windows, jnp.concatenate([upper, lower], axis=1)


def step(wavefield, slowness, block_inverse, block_lengths, slab_owner, shot_position):
    counts = tuple(lax.axis_size(name) for name in FREQ_AXES)
    freq_total = math.prod(counts)
    cut_count = lax.axis_size("yl") * lax.axis_size("core")
    row_count, extent_y = wavefield.shape[2], wavefield.shape[3]
    extent_x = row_count * cut_count
    base = extent_y // RADIX
    freq_index = lax.axis_index(FREQ_AXES)
    cut_index = lax.axis_index(CUT_AXES)
    device = cut_index.reshape(1).astype(jnp.int32)
    angular = (
        2.0 * math.pi * (band_low + band_width * (freq_index.astype(f32) + 0.5) / freq_total)
    )
    inverse, turn = dft_tables(extent_y)
    turn_rows = turn[:, :base]
    turn_here = lax.dynamic_slice_in_dim(turn, cut_index * base, base, 1).T
    turn_cols = turn_rows.T
    chunk = jax.ShapeDtypeStruct((2 * row_count, base), bf16)

    spectrum = call(
        lines_forward_kernel,
        [chunk] * RADIX,
        [pltpu.VMEM((RADIX, row_count, 2 * base), bf16)],
        device, wavefield[0], inverse, turn_rows,
        scalars=1,
    )
    spectrum, slowness, block_inverse = lax.optimization_barrier(
        (spectrum, slowness, block_inverse)
    )
    columns = rotate(spectrum, CUT_AXES)

    prop_re, prop_im = propagator(angular, cut_index, extent_x, extent_y)
    rows_x = cut_index * row_count + jnp.arange(row_count, dtype=jnp.int32)
    offset_x = (rows_x - shot_position[0]).astype(f32) * grid_step
    offset_y = (jnp.arange(extent_y, dtype=jnp.int32) - shot_position[1]).astype(f32) * grid_step
    distance = jnp.sqrt(
        offset_x[None, :] ** 2 + offset_y[:, None] ** 2 + depth_step * depth_step
    )
    ray = angular * slow_ref * distance
    level = 1.0 / math.sqrt(freq_total)
    cos_r, sin_r = jnp.cos(ray) * level, jnp.sin(ray) * level
    owner_id = slab_owner[0]
    pieces = counts[1] * counts[2] * 16
    joined = jnp.concatenate([slowness[0].T, block_inverse[0].reshape(-1, row_count)], axis=0)
    filled = joined.shape[0]
    joined = jnp.pad(joined, ((0, -filled % pieces), (0, 0)))
    share = join(from_owner(joined, owner_id), "z")
    columns, prop_re, prop_im, cos_r, sin_r, share = lax.optimization_barrier(
        (columns, prop_re, prop_im, cos_r, sin_r, share)
    )

    restored = call(
        across_kernel,
        [chunk] * RADIX,
        [
            pltpu.VMEM((RADIX, 2 * row_count, base), bf16),
            pltpu.VMEM((RADIX, 2 * row_count, base), f32),
        ],
        *columns, prop_re, prop_im, inverse, turn_here,
    )
    row_field = rotate(restored, CUT_AXES)

    joined, _ = lax.optimization_barrier((join(share, "x"), restored[0]))
    mine = joined[extent_y:filled]
    other = swap(mine, "core", 1)
    first = lax.axis_index("core") == 0
    operators = jnp.concatenate(
        [jnp.where(first, mine, other), jnp.where(first, other, mine)], axis=0
    )
    operators = join(operators, "yl")
    shape = block_inverse.shape
    matrices = operators.reshape((cut_count,) + shape[1:]).transpose(1, 0, 2, 3, 4)
    matrices = matrices.reshape(2, -1, shape[3], shape[4])
    lengths = lax.dynamic_index_in_dim(block_lengths, owner_id, 0, keepdims=False)
    starts = jnp.cumsum(lengths) - lengths
    windows, pairs = block_windows(matrices, starts, lengths)
    phases = angular * depth_step * (joined[:extent_y].astype(f32) - slow_ref)
    cos_u, sin_u = jnp.cos(phases), jnp.sin(phases)

    part = call(
        lines_inverse_kernel,
        jax.ShapeDtypeStruct(
            (counts[1], counts[0], counts[2], extent_y // freq_total, row_count), bf16
        ),
        [
            pltpu.VMEM((RADIX, 2 * base, row_count), f32),
            pltpu.VMEM((2, extent_y + shape[3], row_count), bf16),
            pltpu.VMEM((2, extent_y + shape[3], row_count), f32),
        ],
        device, windows, *row_field,
        cos_u, sin_u, cos_r, sin_r, pairs, inverse, turn_cols,
        scalars=2,
    )
    part = sum_over(part, "x", bf16)
    part = part.reshape((counts[0] * counts[2],) + part.shape[2:])
    image = sum_over(part, ("yh", "z"), f32)
    return image.T[None]


def solution(mesh):
    sizes = {"yh": 2, "x": 4, "z": 8, "yl": 4, "core": 2}
    if mesh.devices.size != math.prod(sizes.values()):
        sizes = {"yh": 1, "x": 1, "z": 1, "yl": 4, "core": 2}
    fine = Mesh(mesh.devices.reshape(tuple(sizes.values())), tuple(sizes))
    placed = (
        P(FREQ_AXES, None, CUT_AXES, None),
        P(FREQ_AXES, CUT_AXES, None),
        P(FREQ_AXES, None, CUT_AXES, None, None),
        P(),
        P(),
        P(),
    )
    return jax.shard_map(
        step, mesh=fine, in_specs=placed, out_specs=P(None, CUT_AXES, FREQ_AXES), check_vma=False
    )
```

time: 286 us -> 242 us (0.85)
  the two profiles are of different devices: /device:TPU:24 before, /device:TPU:8 now
where the time goes in v2:
time: 242 us; the launch traced here: 241 us
  starting transfers between devices  97.5 us (40%)
  blocking collectives  42.6 us (18%)
  Pallas kernels  34.9 us (14%)
  other arithmetic  34.3 us (14%)
  waiting for transfers between devices  15.4 us (6%)
  local copies, waits for them, and re-layouts  10.6 us (4%)
  matrix products  4.33 us (2%)
    ppermute x14, starting transfers between devices, rotate(): lax.ppermute(values[d], axes, [(i, (i + d) % size) for i in range(size)])  60.7 us
    all_to_all x2, blocking collectives, sum_over(): terms = lax.all_to_all(part, axis, 0, 0, tiled=True)  42.6 us
    pallas_call x3, Pallas kernels, call(): pl.pallas_call(kernel, out_shape=out_shape, in_specs=[smem] * scalars + [...  34.9 us
    all_to_all x2, starting transfers between devices, split(): shaped = lax.all_to_all(shaped, axis, 0, 0)  14.6 us
    all_to_all x3, starting transfers between devices, join(): copies = lax.all_to_all(copies, axis, 0, 0)  13.5 us
    select_n x1, other arithmetic, propagator(): jnp.where(vertical > 0, jnp.sin(root_abs * depth_step), jnp.zeros_like(ro...  9.9 us
    mul x1, other arithmetic, step(): cos_r, sin_r = (jnp.cos(ray) * level, jnp.sin(ray) * level)  9.71 us
    ppermute x2, starting transfers between devices, swap(): lax.ppermute(value, axis, [(i, i ^ bit) for i in range(lax.axis_size(axis...  8.74 us
  transfers between devices with their start and end apart: 21, of which 6 were waited for; matrix products, arithmetic and copies ran while one was open for 18% of the time, Pallas kernels for 5%

profile of v2, /device:TPU:8, one launch (start us, length us, event | category | flops | bytes accessed | tf_op | source)
XLA Modules:
  0.0 241.0 jit_solution(8082045629728891992)
XLA Ops:
  0.0 5.3 %shard_map.82 = (bf16[512,256]{1,0:T(8,128)(2,1)}, bf16[512,256]{1,0:T(8,128)(2,1)}, bf16[512,256]{1,0:T(8,128)(2,1)}, bf16[512,256]{1,0:T(8,128)(2,1)}, bf16[51...) custom-call(s32[1]{0:T(128)} %bitcast.me, ...), custom_call_target="tpu_custom_call" | custom-call | tf_op jit(solution)/shard_map/pallas_call | solution.py:230
  5.7 0.7 copy.33
  6.4 1.2 pad.4.clone
  7.6 4.3 %all-to-all-start = ((bf16[4,640,256]{2,1,0:T(8,128)(2,1)}), bf16[4,640,256]{2,1,0:T(8,128)(2,1)S(1)}, u32[]{:S(2)}, u32[]{:S(2)}) async-start(bf16[4,640,256]{2,1,0:T(8,128)(2,1)} %bitcast.8), calls=%async_computation | async-start | bytes 2621440 | tf_op jit(solution)/shard_map/all_to_all | solution.py:273
  11.9 1.9 collective-permute-start
  13.8 3.5 %collective-permute-start.1 = (bf16[512,256]{1,0:T(8,128)(2,1)}, bf16[512,256]{1,0:T(8,128)(2,1)S(1)}, u32[]{:S(2)}, u32[]{:S(2)}) collective-permute-start(bf16[512,256]{1,0:T(8,128)(2,1)} %get-tuple-element.55), channel_id=1, source_target_pairs={{0,2},{1,3},{2,4},{3,5},{4,6},{5,7},{6,0},{7,1},{8,10},{9,11},{10,... | collective-permute-start | bytes 786440 | tf_op jit(solution)/shard_map/ppermute | solution.py:266
  17.3 7.7 %collective-permute-start.2 = (bf16[512,256]{1,0:T(8,128)(2,1)}, bf16[512,256]{1,0:T(8,128)(2,1)S(1)}, u32[]{:S(2)}, u32[]{:S(2)}) collective-permute-start(bf16[512,256]{1,0:T(8,128)(2,1)} %get-tuple-element.56), channel_id=1, source_target_pairs={{0,3},{1,4},{2,5},{3,6},{4,7},{5,0},{6,1},{7,2},{8,11},{9,12},{10,... | collective-permute-start | bytes 786440 | tf_op jit(solution)/shard_map/ppermute | solution.py:266
  25.1 1.9 collective-permute-start.3
  28.4 0.7 multiply_multiply_fusion
  29.1 0.7 all-to-all-done
  29.8 0.7 constant_dynamic-slice_fusion
  30.6 10.3 %all-to-all-start.1 = ((bf16[8,80,256]{2,1,0:T(8,128)(2,1)}), bf16[8,80,256]{2,1,0:T(8,128)(2,1)S(1)}, u32[]{:S(2)}, u32[]{:S(2)}) async-start(bf16[8,80,256]{2,1,0:T(8,128)(2,1)} %bitcast.9), calls=%async_computation.1 | async-start | bytes 655360 | tf_op jit(solution)/shard_map/all_to_all | solution.py:273
  40.9 0.7 multiply_multiply_fusion.1
  41.6 9.7 %sine_multiply_fusion = (f32[2048,256]{1,0:T(8,128)}, f32[2048,256]{1,0:T(8,128)}) fusion(f32[2048]{0:T(1024)S(1)} %multiply_multiply_fusion, f32[256]{0:T(256)S(1)} %multiply_multiply_fusion.1, f32[]{:T(128)S(6)} %mul.115), kind=kLoop, calls=%fused_computation.15 | loop fusion | flops 2621440 | bytes 4203524 | tf_op jit(solution)/shard_map/mul | solution.py:360
  51.4 1.7 all-to-all-done.1
  53.0 6.8 %collective-permute-start.7 = (bf16[80,256]{1,0:T(8,128)(2,1)S(1)}, bf16[80,256]{1,0:T(8,128)(2,1)S(1)}, u32[]{:S(2)}, u32[]{:S(2)}) collective-permute-start(bf16[80,256]{1,0:T(8,128)(2,1)S(1)} %dynamic-slice_bitcast_fusion.1), channel_id=1, source_target_pairs={{0,256},{256,0},{1,257},{257,1},{2,258},{258,2},{3,259},{259,3},{4... | collective-permute-start | bytes 122888 | tf_op jit(solution)/shard_map/ppermute | solution.py:284
  59.9 3.0 %collective-permute-done.7 = bf16[80,256]{1,0:T(8,128)(2,1)S(1)} collective-permute-done((bf16[80,256]{1,0:T(8,128)(2,1)S(1)}, bf16[80,256]{1,0:T(8,128)(2,1)S(1)}, u32[]{:S(2)}, u32[]{:S(2)}) %collective-permute-start.7) | collective-permute-done | bytes 40992 | tf_op jit(solution)/shard_map/ppermute | solution.py:284
  62.9 1.9 collective-permute-start.4
  64.9 0.8 broadcast_in_dim.8
  65.6 5.6 %all-to-all-start.2 = ((bf16[8,80,256]{2,1,0:T(8,128)(2,1)}), bf16[8,80,256]{2,1,0:T(8,128)(2,1)S(1)}, u32[]{:S(2)}, u32[]{:S(2)}) async-start(bf16[8,80,256]{2,1,0:T(8,128)(2,1)} %broadcast_in_dim.8), calls=%async_computation.2 | async-start | bytes 655360 | tf_op jit(solution)/shard_map/all_to_all | solution.py:279
  71.2 2.3 collective-permute-start.5
  73.6 5.4 %collective-permute-start.6 = (bf16[512,256]{1,0:T(8,128)(2,1)S(1)}, bf16[512,256]{1,0:T(8,128)(2,1)S(1)}, u32[]{:S(2)}, u32[]{:S(2)}) collective-permute-start(bf16[512,256]{1,0:T(8,128)(2,1)S(1)} %copy-done.18), channel_id=1, source_target_pairs={{0,7},{1,0},{2,1},{3,2},{4,3},{5,4},{6,5},{7,6},{8,15},{9,8},{10,9... | collective-permute-start | bytes 786440 | tf_op jit(solution)/shard_map/ppermute | solution.py:266
  79.0 9.9 %fusion = (f32[8,256,256]{2,1,0:T(8,128)}, f32[8,256,256]{2,1,0:T(8,128)}) fusion(f32[256]{0:T(256)S(1)} %fusion.30, f32[8,256]{1,0:T(8,128)S(1)} %fusion.27), kind=kLoop, calls=%fused_computation.3 | loop fusion | flops 4194304 | bytes 4203520 | tf_op jit(solution)/shard_map/jit(_where)/select_n | solution.py:258
  89.0 1.3 broadcast_in_dim.9
  90.3 3.5 %all-to-all-start.3 = ((bf16[4,640,256]{2,1,0:T(8,128)(2,1)}), bf16[4,640,256]{2,1,0:T(8,128)(2,1)S(1)}, u32[]{:S(2)}, u32[]{:S(2)}) async-start(bf16[4,640,256]{2,1,0:T(8,128)(2,1)} %broadcast_in_dim.9), calls=%async_computation.3 | async-start | bytes 2621440 | tf_op jit(solution)/shard_map/all_to_all | solution.py:279
  94.3 1.6 dynamic-slice_bitcast_fusion.refs_11_
  95.9 12.9 %shard_map.83 = (bf16[512,256]{1,0:T(8,128)(2,1)}, bf16[512,256]{1,0:T(8,128)(2,1)}, bf16[512,256]{1,0:T(8,128)(2,1)}, bf16[512,256]{1,0:T(8,128)(2,1)}, bf16[51...) custom-call(bf16[512,256]{1,0:T(8,128)(2,1)} %get-tuple-element.63.refs_0_, ...), custom_call_target="tpu_custom_call" | custom-call | tf_op jit(solution)/shard_map/pallas_call | solution.py:230
  108.8 3.1 %all-to-all-done.3 = bf16[4,640,256]{2,1,0:T(8,128)(2,1)S(1)} async-done(((bf16[4,640,256]{2,1,0:T(8,128)(2,1)}), bf16[4,640,256]{2,1,0:T(8,128)(2,1)S(1)}, u32[]{:S(2)}, u32[]{:S(2)}) %all-to-all-start.3) | async-done | bytes 1310752 | tf_op jit(solution)/shard_map/all_to_all | solution.py:279
  111.9 1.9 collective-permute-start.15
  113.9 1.2 collective-permute-done.15
  115.1 0.9 broadcast_in_dim.10
  116.0 4.4 %all-to-all-start.4 = ((bf16[4,320,256]{2,1,0:T(8,128)(2,1)}), bf16[4,320,256]{2,1,0:T(8,128)(2,1)S(1)}, u32[]{:S(2)}, u32[]{:S(2)}) async-start(bf16[4,320,256]{2,1,0:T(8,128)(2,1)} %broadcast_in_dim.10), calls=%async_computation.4 | async-start | bytes 1310720 | tf_op jit(solution)/shard_map/all_to_all | solution.py:279
  121.0 1.9 collective-permute-start.8
  122.9 3.4 %collective-permute-start.9 = (bf16[512,256]{1,0:T(8,128)(2,1)}, bf16[512,256]{1,0:T(8,128)(2,1)S(1)}, u32[]{:S(2)}, u32[]{:S(2)}) collective-permute-start(bf16[512,256]{1,0:T(8,128)(2,1)} %get-tuple-element.75), channel_id=1, source_target_pairs={{0,2},{1,3},{2,4},{3,5},{4,6},{5,7},{6,0},{7,1},{8,10},{9,11},{10,... | collective-permute-start | bytes 786440 | tf_op jit(solution)/shard_map/ppermute | solution.py:266
  126.3 3.1 %collective-permute-start.10 = (bf16[512,256]{1,0:T(8,128)(2,1)}, bf16[512,256]{1,0:T(8,128)(2,1)S(1)}, u32[]{:S(2)}, u32[]{:S(2)}) collective-permute-start(bf16[512,256]{1,0:T(8,128)(2,1)} %get-tuple-element.76), channel_id=1, source_target_pairs={{0,3},{1,4},{2,5},{3,6},{4,7},{5,0},{6,1},{7,2},{8,11},{9,12},{10,... | collective-permute-start | bytes 786440 | tf_op jit(solution)/shard_map/ppermute | solution.py:266
  129.4 4.5 %collective-permute-start.11 = (bf16[512,256]{1,0:T(8,128)(2,1)}, bf16[512,256]{1,0:T(8,128)(2,1)S(1)}, u32[]{:S(2)}, u32[]{:S(2)}) collective-permute-start(bf16[512,256]{1,0:T(8,128)(2,1)} %get-tuple-element.77), channel_id=1, source_target_pairs={{0,4},{1,5},{2,6},{3,7},{4,0},{5,1},{6,2},{7,3},{8,12},{9,13},{10,... | collective-permute-start | bytes 786440 | tf_op jit(solution)/shard_map/ppermute | solution.py:266
  133.9 2.1 collective-permute-start.12
  136.0 8.4 %fusion.9 = (f32[2048,256]{1,0:T(8,128)}, f32[2048,256]{1,0:T(8,128)}) fusion(f32[]{:T(128)S(6)} %mul.125, bf16[2560,256]{1,0:T(8,128)(2,1)S(1)} %bitcast.54), kind=kLoop, calls=%fused_computation.13 | loop fusion | flops 1572864 | bytes 5242884 | tf_op jit(solution)/shard_map/sin | solution.py:397
  145.1 2.0 fusion.12
  147.1 2.3 fusion.11
  149.7 0.7 copy-done.23
  150.4 19.1 %collective-permute-start.13 = (bf16[512,256]{1,0:T(8,128)(2,1)S(1)}, bf16[512,256]{1,0:T(8,128)(2,1)S(1)}, u32[]{:S(2)}, u32[]{:S(2)}) collective-permute-start(bf16[512,256]{1,0:T(8,128)(2,1)S(1)} %copy-done.23), channel_id=1, source_target_pairs={{0,6},{1,7},{2,0},{3,1},{4,2},{5,3},{6,4},{7,5},{8,14},{9,15},{10,... | collective-permute-start | bytes 786440 | tf_op jit(solution)/shard_map/ppermute | solution.py:266
  169.5 1.9 collective-permute-start.14
  171.4 3.0 %maximum_maximum_fusion.refs_12_ = bf16[40,160,160]{2,1,0:T(8,128)(2,1)} fusion(bf16[40,80,80]{2,1,0:T(8,128)(2,1)S(1)} %get-tuple-element.88, bf16[40,80,80]{2,1,0:T(8,128)(2,1)S(1)} %get-tuple-element.87, bf16[40,80,80]{2,1,0:T(8,128)(2,1)S(1)} %fusion.31), kind=kLoop, calls=%fused_computation | loop fusion | flops 8192000 | bytes 3584000 | tf_op jit(solution)/shard_map/concatenate | solution.py:317
  174.4 5.6 %collective-permute-done.12.refs_5_ = bf16[512,256]{1,0:T(8,128)(2,1)S(1)} collective-permute-done((bf16[512,256]{1,0:T(8,128)(2,1)}, bf16[512,256]{1,0:T(8,128)(2,1)S(1)}, u32[]{:S(2)}, u32[]{:S(2)}) %collective-permute-start.12) | collective-permute-done | bytes 262176 | tf_op jit(solution)/shard_map/ppermute | solution.py:266
  180.9 16.7 %shard_map.84 = bf16[4,2,8,32,256]{4,3,2,1,0:T(8,128)(2,1)} custom-call(s32[1]{0:T(128)} %bitcast.me, s32[40]{0:T(128)} %and_select_fusion.1.windows, bf16[512,256]{1,0:T(8,128)(2,1)} %get-tuple-element.73.refs_0_, bf16[512,256]{1,0:T(8,128)(2,1)} %copy-done.1, bf16[512,256]{1,0:T(8,128)(2,1)} %copy-done.2, bf16[512,256]{1,0:T(8,128)(2,1)} %copy-done.3, ...), custom_call_target="tpu_custom_call" | custom-call | tf_op jit(solution)/shard_map/pallas_call | solution.py:230
  197.6 19.5 %all_to_all.35 = bf16[4,2,8,32,256]{4,3,2,1,0:T(8,128)(2,1)S(1)} all-to-all(bf16[4,2,8,32,256]{4,3,2,1,0:T(8,128)(2,1)} %shard_map.84), channel_id=1, replica_groups=mesh['yh'=2,'x'=4,'z'=8,'yl'=4,'core'=2] {'x'}, dimensions={0} | all-to-all | bytes 2097152 | tf_op jit(solution)/shard_map/all_to_all | solution.py:299
  217.3 23.1 %all_to_all.36 = bf16[16,32,256]{2,1,0:T(8,128)(2,1)S(1)} all-to-all(bf16[16,32,256]{2,1,0:T(8,128)(2,1)S(1)} %bitcast.58), channel_id=1, replica_groups=mesh['yh'=2,'x'=4,'z'=8,'yl'=4,'core'=2] {'yh','z'}, dimensions={0} | all-to-all | bytes 524288 | tf_op jit(solution)/shard_map/all_to_all | solution.py:299
  (87 shorter events, 4.8 us)
Async XLA Ops:
  0.0 5.3 %copy-start.15 = (bf16[1,2,5,64,64]{4,3,2,1,0:T(8,128)(2,1)S(1)}, bf16[1,2,5,64,64]{4,3,2,1,0:T(8,128)(2,1)}, u32[]{:S(2)}) copy-start(bf16[1,2,5,64,64]{4,3,2,1,0:T(8,128)(2,1)} %param.10) | copy-start | bytes 245764
  0.0 5.6 %copy-start = (bf16[1,256,2048]{2,1,0:T(8,128)(2,1)S(1)}, bf16[1,256,2048]{2,1,0:T(8,128)(2,1)}, u32[]{:S(2)}) copy-start(bf16[1,256,2048]{2,1,0:T(8,128)(2,1)} %param.9) | copy-start | bytes 3145732
  6.4 18.7 %copy-start.21 = (bf16[512,256]{1,0:T(8,128)(2,1)S(1)}, bf16[512,256]{1,0:T(8,128)(2,1)}, u32[]{:S(2)}) copy-start(bf16[512,256]{1,0:T(8,128)(2,1)} %get-tuple-element.57) | copy-start | bytes 786436
  6.4 21.3 %copy-start.17 = (s32[2]{0:T(128)S(1)}, s32[2]{0:T(128)}, u32[]{:S(2)}) copy-start(s32[2]{0:T(128)} %param.13) | copy-start | bytes 28
  7.6 22.2 %all-to-all-start = ((bf16[4,640,256]{2,1,0:T(8,128)(2,1)}), bf16[4,640,256]{2,1,0:T(8,128)(2,1)S(1)}, u32[]{:S(2)}, u32[]{:S(2)}) async-start(bf16[4,640,256]{2,1,0:T(8,128)(2,1)} %bitcast.8), calls=%async_computation | async-start | bytes 2621440 | tf_op jit(solution)/shard_map/all_to_all | solution.py:273
  11.9 59.3 %collective-permute-start = (bf16[512,256]{1,0:T(8,128)(2,1)}, bf16[512,256]{1,0:T(8,128)(2,1)S(1)}, u32[]{:S(2)}, u32[]{:S(2)}) collective-permute-start(bf16[512,256]{1,0:T(8,128)(2,1)} %get-tuple-element.54), channel_id=1, source_target_pairs={{0,1},{1,2},{2,3},{3,4},{4,5},{5,6},{6,7},{7,0},{8,9},{9,10},{10,1... | collective-permute-start | bytes 786440 | tf_op jit(solution)/shard_map/ppermute | solution.py:266
  13.8 59.7 %collective-permute-start.1 = (bf16[512,256]{1,0:T(8,128)(2,1)}, bf16[512,256]{1,0:T(8,128)(2,1)S(1)}, u32[]{:S(2)}, u32[]{:S(2)}) collective-permute-start(bf16[512,256]{1,0:T(8,128)(2,1)} %get-tuple-element.55), channel_id=1, source_target_pairs={{0,2},{1,3},{2,4},{3,5},{4,6},{5,7},{6,0},{7,1},{8,10},{9,11},{10,... | collective-permute-start | bytes 786440 | tf_op jit(solution)/shard_map/ppermute | solution.py:266
  17.3 71.5 %collective-permute-start.2 = (bf16[512,256]{1,0:T(8,128)(2,1)}, bf16[512,256]{1,0:T(8,128)(2,1)S(1)}, u32[]{:S(2)}, u32[]{:S(2)}) collective-permute-start(bf16[512,256]{1,0:T(8,128)(2,1)} %get-tuple-element.56), channel_id=1, source_target_pairs={{0,3},{1,4},{2,5},{3,6},{4,7},{5,0},{6,1},{7,2},{8,11},{9,12},{10,... | collective-permute-start | bytes 786440 | tf_op jit(solution)/shard_map/ppermute | solution.py:266
  25.1 63.8 %collective-permute-start.3 = (bf16[512,256]{1,0:T(8,128)(2,1)S(1)}, bf16[512,256]{1,0:T(8,128)(2,1)S(1)}, u32[]{:S(2)}, u32[]{:S(2)}) collective-permute-start(bf16[512,256]{1,0:T(8,128)(2,1)S(1)} %copy-done.21), channel_id=1, source_target_pairs={{0,4},{1,5},{2,6},{3,7},{4,0},{5,1},{6,2},{7,3},{8,12},{9,13},{10,... | collective-permute-start | bytes 786440 | tf_op jit(solution)/shard_map/ppermute | solution.py:266
  30.6 22.5 %all-to-all-start.1 = ((bf16[8,80,256]{2,1,0:T(8,128)(2,1)}), bf16[8,80,256]{2,1,0:T(8,128)(2,1)S(1)}, u32[]{:S(2)}, u32[]{:S(2)}) async-start(bf16[8,80,256]{2,1,0:T(8,128)(2,1)} %bitcast.9), calls=%async_computation.1 | async-start | bytes 655360 | tf_op jit(solution)/shard_map/all_to_all | solution.py:273
  41.6 21.3 %copy-start.20 = (bf16[512,256]{1,0:T(8,128)(2,1)S(1)}, bf16[512,256]{1,0:T(8,128)(2,1)}, u32[]{:S(2)}) copy-start(bf16[512,256]{1,0:T(8,128)(2,1)} %get-tuple-element.58) | copy-start | bytes 786436
  41.6 29.6 %copy-start.19 = (bf16[512,256]{1,0:T(8,128)(2,1)S(1)}, bf16[512,256]{1,0:T(8,128)(2,1)}, u32[]{:S(2)}) copy-start(bf16[512,256]{1,0:T(8,128)(2,1)} %get-tuple-element.59) | copy-start | bytes 786436
  41.6 31.9 %copy-start.18 = (bf16[512,256]{1,0:T(8,128)(2,1)S(1)}, bf16[512,256]{1,0:T(8,128)(2,1)}, u32[]{:S(2)}) copy-start(bf16[512,256]{1,0:T(8,128)(2,1)} %get-tuple-element.60) | copy-start | bytes 786436
  53.0 9.9 %collective-permute-start.7 = (bf16[80,256]{1,0:T(8,128)(2,1)S(1)}, bf16[80,256]{1,0:T(8,128)(2,1)S(1)}, u32[]{:S(2)}, u32[]{:S(2)}) collective-permute-start(bf16[80,256]{1,0:T(8,128)(2,1)S(1)} %dynamic-slice_bitcast_fusion.1), channel_id=1, source_target_pairs={{0,256},{256,0},{1,257},{257,1},{2,258},{258,2},{3,259},{259,3},{4... | collective-permute-start | bytes 122888 | tf_op jit(solution)/shard_map/ppermute | solution.py:284
  62.9 26.0 %collective-permute-start.4 = (bf16[512,256]{1,0:T(8,128)(2,1)S(1)}, bf16[512,256]{1,0:T(8,128)(2,1)S(1)}, u32[]{:S(2)}, u32[]{:S(2)}) collective-permute-start(bf16[512,256]{1,0:T(8,128)(2,1)S(1)} %copy-done.20), channel_id=1, source_target_pairs={{0,5},{1,6},{2,7},{3,0},{4,1},{5,2},{6,3},{7,4},{8,13},{9,14},{10,... | collective-permute-start | bytes 786440 | tf_op jit(solution)/shard_map/ppermute | solution.py:266
  65.6 23.3 %all-to-all-start.2 = ((bf16[8,80,256]{2,1,0:T(8,128)(2,1)}), bf16[8,80,256]{2,1,0:T(8,128)(2,1)S(1)}, u32[]{:S(2)}, u32[]{:S(2)}) async-start(bf16[8,80,256]{2,1,0:T(8,128)(2,1)} %broadcast_in_dim.8), calls=%async_computation.2 | async-start | bytes 655360 | tf_op jit(solution)/shard_map/all_to_all | solution.py:279
  71.2 17.6 %copy-start.8 = (bf16[512,256]{1,0:T(8,128)(2,1)}, bf16[512,256]{1,0:T(8,128)(2,1)S(1)}, u32[]{:S(2)}) copy-start(bf16[512,256]{1,0:T(8,128)(2,1)S(1)} %collective-permute-done.refs_1_) | copy-start | bytes 786436
  71.2 17.7 %collective-permute-start.5 = (bf16[512,256]{1,0:T(8,128)(2,1)S(1)}, bf16[512,256]{1,0:T(8,128)(2,1)S(1)}, u32[]{:S(2)}, u32[]{:S(2)}) collective-permute-start(bf16[512,256]{1,0:T(8,128)(2,1)S(1)} %copy-done.19), channel_id=1, source_target_pairs={{0,6},{1,7},{2,0},{3,1},{4,2},{5,3},{6,4},{7,5},{8,14},{9,15},{10,... | collective-permute-start | bytes 786440 | tf_op jit(solution)/shard_map/ppermute | solution.py:266
  73.6 15.3 %copy-start.9 = (bf16[512,256]{1,0:T(8,128)(2,1)}, bf16[512,256]{1,0:T(8,128)(2,1)S(1)}, u32[]{:S(2)}) copy-start(bf16[512,256]{1,0:T(8,128)(2,1)S(1)} %collective-permute-done.1.refs_2_) | copy-start | bytes 786436
  73.6 15.4 %collective-permute-start.6 = (bf16[512,256]{1,0:T(8,128)(2,1)S(1)}, bf16[512,256]{1,0:T(8,128)(2,1)S(1)}, u32[]{:S(2)}, u32[]{:S(2)}) collective-permute-start(bf16[512,256]{1,0:T(8,128)(2,1)S(1)} %copy-done.18), channel_id=1, source_target_pairs={{0,7},{1,0},{2,1},{3,2},{4,3},{5,4},{6,5},{7,6},{8,15},{9,8},{10,9... | collective-permute-start | bytes 786440 | tf_op jit(solution)/shard_map/ppermute | solution.py:266
  88.9 1.4 copy-start.10
  88.9 1.4 copy-start.11
  88.9 1.3 copy-start.12
  88.9 1.3 copy-start.13
  89.0 1.4 copy-start.14
  89.0 4.9 %copy-start.16 = (s32[64,40]{0,1:T(8,128)S(1)}, s32[64,40]{0,1:T(8,128)}, u32[]{:S(2)}) copy-start(s32[64,40]{0,1:T(8,128)} %param.11) | copy-start | bytes 30724
  90.3 21.6 %all-to-all-start.3 = ((bf16[4,640,256]{2,1,0:T(8,128)(2,1)}), bf16[4,640,256]{2,1,0:T(8,128)(2,1)S(1)}, u32[]{:S(2)}, u32[]{:S(2)}) async-start(bf16[4,640,256]{2,1,0:T(8,128)(2,1)} %broadcast_in_dim.9), calls=%async_computation.3 | async-start | bytes 2621440 | tf_op jit(solution)/shard_map/all_to_all | solution.py:279
  111.9 3.2 %collective-permute-start.15 = (bf16[160,256]{1,0:T(8,128)(2,1)S(1)}, bf16[160,256]{1,0:T(8,128)(2,1)S(1)}, u32[]{:S(2)}, u32[]{:S(2)}) collective-permute-start(bf16[160,256]{1,0:T(8,128)(2,1)S(1)} %slice.27), channel_id=1, source_target_pairs={{0,1},{1,0},{2,3},{3,2},{4,5},{5,4},{6,7},{7,6},{8,9},{9,8},{10,11... | collective-permute-start | bytes 245768 | tf_op jit(solution)/shard_map/ppermute | solution.py:284
  116.0 28.4 %all-to-all-start.4 = ((bf16[4,320,256]{2,1,0:T(8,128)(2,1)}), bf16[4,320,256]{2,1,0:T(8,128)(2,1)S(1)}, u32[]{:S(2)}, u32[]{:S(2)}) async-start(bf16[4,320,256]{2,1,0:T(8,128)(2,1)} %broadcast_in_dim.10), calls=%async_computation.4 | async-start | bytes 1310720 | tf_op jit(solution)/shard_map/all_to_all | solution.py:279
  121.0 28.7 %collective-permute-start.8 = (bf16[512,256]{1,0:T(8,128)(2,1)}, bf16[512,256]{1,0:T(8,128)(2,1)S(1)}, u32[]{:S(2)}, u32[]{:S(2)}) collective-permute-start(bf16[512,256]{1,0:T(8,128)(2,1)} %get-tuple-element.74), channel_id=1, source_target_pairs={{0,1},{1,2},{2,3},{3,4},{4,5},{5,6},{6,7},{7,0},{8,9},{9,10},{10,1... | collective-permute-start | bytes 786440 | tf_op jit(solution)/shard_map/ppermute | solution.py:266
  122.9 46.6 %collective-permute-start.9 = (bf16[512,256]{1,0:T(8,128)(2,1)}, bf16[512,256]{1,0:T(8,128)(2,1)S(1)}, u32[]{:S(2)}, u32[]{:S(2)}) collective-permute-start(bf16[512,256]{1,0:T(8,128)(2,1)} %get-tuple-element.75), channel_id=1, source_target_pairs={{0,2},{1,3},{2,4},{3,5},{4,6},{5,7},{6,0},{7,1},{8,10},{9,11},{10,... | collective-permute-start | bytes 786440 | tf_op jit(solution)/shard_map/ppermute | solution.py:266
  126.3 48.1 %collective-permute-start.10 = (bf16[512,256]{1,0:T(8,128)(2,1)}, bf16[512,256]{1,0:T(8,128)(2,1)S(1)}, u32[]{:S(2)}, u32[]{:S(2)}) collective-permute-start(bf16[512,256]{1,0:T(8,128)(2,1)} %get-tuple-element.76), channel_id=1, source_target_pairs={{0,3},{1,4},{2,5},{3,6},{4,7},{5,0},{6,1},{7,2},{8,11},{9,12},{10,... | collective-permute-start | bytes 786440 | tf_op jit(solution)/shard_map/ppermute | solution.py:266
  129.4 45.0 %collective-permute-start.11 = (bf16[512,256]{1,0:T(8,128)(2,1)}, bf16[512,256]{1,0:T(8,128)(2,1)S(1)}, u32[]{:S(2)}, u32[]{:S(2)}) collective-permute-start(bf16[512,256]{1,0:T(8,128)(2,1)} %get-tuple-element.77), channel_id=1, source_target_pairs={{0,4},{1,5},{2,6},{3,7},{4,0},{5,1},{6,2},{7,3},{8,12},{9,13},{10,... | collective-permute-start | bytes 786440 | tf_op jit(solution)/shard_map/ppermute | solution.py:266
  133.9 46.1 %collective-permute-start.12 = (bf16[512,256]{1,0:T(8,128)(2,1)}, bf16[512,256]{1,0:T(8,128)(2,1)S(1)}, u32[]{:S(2)}, u32[]{:S(2)}) collective-permute-start(bf16[512,256]{1,0:T(8,128)(2,1)} %get-tuple-element.78), channel_id=1, source_target_pairs={{0,5},{1,6},{2,7},{3,0},{4,1},{5,2},{6,3},{7,4},{8,13},{9,14},{10,... | collective-permute-start | bytes 786440 | tf_op jit(solution)/shard_map/ppermute | solution.py:266
  149.4 1.0 copy-start.23
  149.4 20.1 %copy-start.22 = (bf16[512,256]{1,0:T(8,128)(2,1)S(1)}, bf16[512,256]{1,0:T(8,128)(2,1)}, u32[]{:S(2)}) copy-start(bf16[512,256]{1,0:T(8,128)(2,1)} %get-tuple-element.80) | copy-start | bytes 786436
  149.7 24.7 %copy-start.1 = (bf16[512,256]{1,0:T(8,128)(2,1)}, bf16[512,256]{1,0:T(8,128)(2,1)S(1)}, u32[]{:S(2)}) copy-start(bf16[512,256]{1,0:T(8,128)(2,1)S(1)} %collective-permute-done.8.refs_1_) | copy-start | bytes 786436
  150.4 29.7 %collective-permute-start.13 = (bf16[512,256]{1,0:T(8,128)(2,1)S(1)}, bf16[512,256]{1,0:T(8,128)(2,1)S(1)}, u32[]{:S(2)}, u32[]{:S(2)}) collective-permute-start(bf16[512,256]{1,0:T(8,128)(2,1)S(1)} %copy-done.23), channel_id=1, source_target_pairs={{0,6},{1,7},{2,0},{3,1},{4,2},{5,3},{6,4},{7,5},{8,14},{9,15},{10,... | collective-permute-start | bytes 786440 | tf_op jit(solution)/shard_map/ppermute | solution.py:266
  169.5 4.9 %copy-start.2 = (bf16[512,256]{1,0:T(8,128)(2,1)}, bf16[512,256]{1,0:T(8,128)(2,1)S(1)}, u32[]{:S(2)}) copy-start(bf16[512,256]{1,0:T(8,128)(2,1)S(1)} %collective-permute-done.9.refs_2_) | copy-start | bytes 786436
  169.5 10.5 %collective-permute-start.14 = (bf16[512,256]{1,0:T(8,128)(2,1)S(1)}, bf16[512,256]{1,0:T(8,128)(2,1)S(1)}, u32[]{:S(2)}, u32[]{:S(2)}) collective-permute-start(bf16[512,256]{1,0:T(8,128)(2,1)S(1)} %copy-done.22), channel_id=1, source_target_pairs={{0,7},{1,0},{2,1},{3,2},{4,3},{5,4},{6,5},{7,6},{8,15},{9,8},{10,9... | collective-permute-start | bytes 786440 | tf_op jit(solution)/shard_map/ppermute | solution.py:266
  174.4 5.7 %copy-start.3 = (bf16[512,256]{1,0:T(8,128)(2,1)}, bf16[512,256]{1,0:T(8,128)(2,1)S(1)}, u32[]{:S(2)}) copy-start(bf16[512,256]{1,0:T(8,128)(2,1)S(1)} %collective-permute-done.10.refs_3_) | copy-start | bytes 786436
  174.4 5.6 %copy-start.4 = (bf16[512,256]{1,0:T(8,128)(2,1)}, bf16[512,256]{1,0:T(8,128)(2,1)S(1)}, u32[]{:S(2)}) copy-start(bf16[512,256]{1,0:T(8,128)(2,1)S(1)} %collective-permute-done.11.refs_4_) | copy-start | bytes 786436
  180.0 0.7 copy-start.5
  180.0 0.8 copy-start.6
  180.1 0.9 copy-start.7

commit v3 on v2

--- a/solution.py
+++ b/solution.py
@@ -78,6 +78,16 @@
     return (real * cosine + imag * sine, imag * cosine - real * sine)
 
 
+def fetch(sources, targets, done):
+    copies = [
+        pltpu.make_async_copy(source, target, done.at[i])
+        for i, (source, target) in enumerate(zip(sources, targets))
+    ]
+    for copy in copies:
+        copy.start()
+    return copies
+
+
 def lines_forward_kernel(me, field, table, turn, *outs_mid):
     outs, mid = outs_mid[:RADIX], outs_mid[RADIX]
     rows, base = mid.shape[1], mid.shape[2] // 2
@@ -106,8 +116,10 @@
 
 def across_kernel(*refs):
     fields, refs = refs[:RADIX], refs[RADIX:]
-    prop_re, prop_im, table, turn = refs[:4]
-    outs, (mid, back) = refs[4 : 4 + RADIX], refs[4 + RADIX :]
+    table, turn = refs[:2]
+    later, refs = refs[2:4], refs[4:]
+    outs, (mid, back, prop_re, prop_im, done) = refs[:RADIX], refs[RADIX:]
+    copies = fetch(later, (prop_re, prop_im), done)
     base, cols = prop_re.shape[1], prop_re.shape[2]
 
     def fore(tile, carry):
@@ -131,13 +143,20 @@
         return carry
 
     lax.fori_loop(0, base // 16, fore, 0)
-    for k in range(RADIX):
-        both = jnp.dot(table[...], mid[k], preferred_element_type=f32)
-        real, minus = both[:base], both[base:]
-        p_re, p_im = prop_re[k], prop_im[k]
-        mid[k, :base] = (real * p_re + minus * p_im).astype(bf16)
-        mid[k, base:] = (real * p_im - minus * p_re).astype(bf16)
-        back[k] = jnp.dot(table[...], mid[k], preferred_element_type=f32)
+    for copy in copies:
+        copy.wait()
+
+    def waves(step, carry):
+        for k in (2 * step, 2 * step + 1):
+            both = jnp.dot(table[...], mid[k], preferred_element_type=f32)
+            real, minus = both[:base], both[base:]
+            p_re, p_im = prop_re[k], prop_im[k]
+            mid[k, :base] = (real * p_re + minus * p_im).astype(bf16)
+            mid[k, base:] = (real * p_im - minus * p_re).astype(bf16)
+            back[k] = jnp.dot(table[...], mid[k], preferred_element_type=f32)
+        return carry
+
+    lax.fori_loop(0, RADIX // 2, waves, 0)
 
     def aft(tile, carry):
         at = pl.multiple_of(tile * 16, 16)
@@ -159,7 +178,10 @@
 
 def lines_inverse_kernel(me, windows, *refs):
     fields, refs = refs[:RADIX], refs[RADIX:]
-    cos_u, sin_u, cos_r, sin_r, pairs, table, turn, out, back, turned, final = refs
+    table, turn = refs[:2]
+    later, (out, back, turned, final), held, done = refs[2:7], refs[7:11], refs[11:16], refs[16]
+    cos_u, sin_u, pairs, cos_r, sin_r = held
+    copies = fetch(later, held, done)
     rows, base = fields[0].shape[0] // 2, fields[0].shape[1]
     blocks, reach = pairs.shape[0], pairs.shape[1] // 2
     tail = pl.ds(RADIX * base, turned.shape[1] - RADIX * base)
@@ -172,6 +194,8 @@
             table[:, base:], field[rows:], (((1,), (1,)), ((), ())), preferred_element_type=f32
         )
         back[(me[0] + RADIX - d) % RADIX] = first + second
+    for copy in copies:
+        copy.wait()
 
     def aft(tile, carry):
         at = pl.multiple_of(tile * 16, 16)
@@ -224,17 +248,40 @@
     lax.fori_loop(0, RADIX * base // 16, image, 0)
 
 
-def call(kernel, out_shape, scratch, *operands, scalars=0):
+def call(kernel, out_shape, scratch, *operands, scalars=0, later=0):
+    anywhere = pl.BlockSpec(memory_space=pl.ANY)
     smem = pl.BlockSpec(memory_space=pltpu.SMEM)
     vmem = pl.BlockSpec(memory_space=pltpu.VMEM)
     return pl.pallas_call(
         kernel,
         out_shape=out_shape,
-        in_specs=[smem] * scalars + [vmem] * (len(operands) - scalars),
+        in_specs=[smem] * scalars
+        + [vmem] * (len(operands) - scalars - later)
+        + [anywhere] * later,
         out_specs=jax.tree.map(lambda _: vmem, out_shape),
         scratch_shapes=scratch,
         interpret=INTERPRET,
     )(*operands)
+
+
+def cos_sin(angle):
+    quarters = jnp.round(angle * (2.0 / math.pi))
+    rest = angle - quarters * 1.5703125
+    rest = rest - quarters * 4.837512969970703125e-4
+    rest = rest - quarters * 7.549789948768648e-8
+    square = rest * rest
+    sine = ((-1.9515295891e-4 * square + 8.3321608736e-3) * square - 1.6666654611e-1) * square
+    sine = sine * rest + rest
+    cosine = (2.443315711809948e-5 * square - 1.388731625493765e-3) * square
+    cosine = (cosine + 4.166664568298827e-2) * (square * square) - 0.5 * square + 1.0
+    count = quarters.astype(jnp.int32)
+    odd = (count & 1) != 0
+    first = jnp.where(odd, sine, cosine)
+    second = jnp.where(odd, cosine, sine)
+    return (
+        jnp.where(((count + 1) & 2) != 0, -first, first),
+        jnp.where((count & 2) != 0, -second, second),
+    )
 
 
 def wave_numbers(indices, extent):
@@ -252,10 +299,9 @@
     wave_y = wave_numbers(line_ids, extent_y)
     vertical = (angular * slow_ref) ** 2 - wave_x[:, :, None] ** 2 - wave_y[None, None, :] ** 2
     root_abs = jnp.sqrt(jnp.abs(vertical))
-    real_part = jnp.where(
-        vertical > 0, jnp.cos(root_abs * depth_step), jnp.exp(-root_abs * depth_step)
-    )
-    imag_part = jnp.where(vertical > 0, jnp.sin(root_abs * depth_step), jnp.zeros_like(root_abs))
+    cosine, sine = cos_sin(root_abs * depth_step)
+    real_part = jnp.where(vertical > 0, cosine, jnp.exp(-root_abs * depth_step))
+    imag_part = jnp.where(vertical > 0, sine, jnp.zeros_like(root_abs))
     return (real_part, imag_part)
 
 
@@ -343,9 +389,6 @@
         device, wavefield[0], inverse, turn_rows,
         scalars=1,
     )
-    spectrum, slowness, block_inverse = lax.optimization_barrier(
-        (spectrum, slowness, block_inverse)
-    )
     columns = rotate(spectrum, CUT_AXES)
 
     prop_re, prop_im = propagator(angular, cut_index, extent_x, extent_y)
@@ -357,7 +400,8 @@
     )
     ray = angular * slow_ref * distance
     level = 1.0 / math.sqrt(freq_total)
-    cos_r, sin_r = jnp.cos(ray) * level, jnp.sin(ray) * level
+    cos_r, sin_r = cos_sin(ray)
+    cos_r, sin_r = cos_r * level, sin_r * level
     owner_id = slab_owner[0]
     pieces = counts[1] * counts[2] * 16
     joined = jnp.concatenate([slowness[0].T, block_inverse[0].reshape(-1, row_count)], axis=0)
@@ -374,8 +418,12 @@
         [
             pltpu.VMEM((RADIX, 2 * row_count, base), bf16),
             pltpu.VMEM((RADIX, 2 * row_count, base), f32),
+            pltpu.VMEM(prop_re.shape, f32),
+            pltpu.VMEM(prop_im.shape, f32),
+            pltpu.SemaphoreType.DMA((2,)),
         ],
-        *columns, prop_re, prop_im, inverse, turn_here,
+        *columns, inverse, turn_here, prop_re, prop_im,
+        later=2,
     )
     row_field = rotate(restored, CUT_AXES)
 
@@ -394,8 +442,9 @@
     starts = jnp.cumsum(lengths) - lengths
     windows, pairs = block_windows(matrices, starts, lengths)
     phases = angular * depth_step * (joined[:extent_y].astype(f32) - slow_ref)
-    cos_u, sin_u = jnp.cos(phases), jnp.sin(phases)
-
+    cos_u, sin_u = cos_sin(phases)
+
+    late = (cos_u, sin_u, pairs, cos_r, sin_r)
     part = call(
         lines_inverse_kernel,
         jax.ShapeDtypeStruct(
@@ -405,10 +454,12 @@
             pltpu.VMEM((RADIX, 2 * base, row_count), f32),
             pltpu.VMEM((2, extent_y + shape[3], row_count), bf16),
             pltpu.VMEM((2, extent_y + shape[3], row_count), f32),
+            *[pltpu.VMEM(value.shape, value.dtype) for value in late],
+            pltpu.SemaphoreType.DMA((len(late),)),
         ],
-        device, windows, *row_field,
-        cos_u, sin_u, cos_r, sin_r, pairs, inverse, turn_cols,
+        device, windows, *row_field, inverse, turn_cols, *late,
         scalars=2,
+        later=len(late),
     )
     part = sum_over(part, "x", bf16)
     part = part.reshape((counts[0] * counts[2],) + part.shape[2:])

time: 242 us -> 239 us (0.988)
  other arithmetic: 34.3 us -> 21.9 us
  waiting for transfers between devices: 15.4 us -> 21.3 us
    sin x1 -> x0, other arithmetic: 8.41 us -> none  [step(): cos_u, sin_u = (jnp.cos(phases), jnp.sin(phases))]
    mul x1, other arithmetic: 9.71 us -> 4.95 us  [step(): cos_r, sin_r = (cos_r * level, sin_r * level)]
    all_to_all x2, waiting for transfers between devices: 2.41 us -> 7.12 us  [split(): shaped = lax.all_to_all(shaped, axis, 0, 0)]
    ppermute x14, starting transfers between devices: 60.7 us -> 65.2 us  [rotate(): lax.ppermute(values[d], axes, [(i, (i + d) % size) for i in range(size)])]
    select_n x1 -> x2, other arithmetic: 9.9 us -> 9.44 us  [the longest x1 5.24 us: propagator(): imag_part = jnp.where(vertical > 0, sine, jnp.zeros_like(root_abs))]
  transfers between devices with their start and end apart: 21 -> 21, of which waited for: 6 -> 7; matrix products, arithmetic and copies ran while one was open for 18% -> 12% of each run, Pallas kernels for 5% -> 8%
where the time goes in v3:
time: 239 us; the launch traced here: 238 us
  starting transfers between devices  99.3 us (42%)
  blocking collectives  42.5 us (18%)
  Pallas kernels  35.9 us (15%)
  other arithmetic  21.9 us (9%)
  waiting for transfers between devices  21.3 us (9%)
  local copies, waits for them, and re-layouts  11.4 us (5%)
  matrix products  4.34 us (2%)
    ppermute x14, starting transfers between devices, rotate(): lax.ppermute(values[d], axes, [(i, (i + d) % size) for i in range(size)])  65.2 us
    all_to_all x2, blocking collectives, sum_over(): terms = lax.all_to_all(part, axis, 0, 0, tiled=True)  42.5 us
    pallas_call x3, Pallas kernels, call(): pl.pallas_call(kernel, out_shape=out_shape, in_specs=[smem] * scalars + [...  35.9 us
    all_to_all x3, starting transfers between devices, join(): copies = lax.all_to_all(copies, axis, 0, 0)  13.1 us
    all_to_all x2, starting transfers between devices, split(): shaped = lax.all_to_all(shaped, axis, 0, 0)  12.7 us
    ppermute x2, starting transfers between devices, swap(): lax.ppermute(value, axis, [(i, i ^ bit) for i in range(lax.axis_size(axis...  8.34 us
    all_to_all x2, waiting for transfers between devices, split(): shaped = lax.all_to_all(shaped, axis, 0, 0)  7.12 us
    ppermute x14, waiting for transfers between devices, rotate(): lax.ppermute(values[d], axes, [(i, (i + d) % size) for i in range(size)])  5.78 us
  transfers between devices with their start and end apart: 21, of which 7 were waited for; matrix products, arithmetic and copies ran while one was open for 12% of the time, Pallas kernels for 8%

profile of v3, /device:TPU:8, one launch (start us, length us, event | category | flops | bytes accessed | tf_op | source)
XLA Modules:
  0.0 237.9 jit_solution(17321826447645799200)
XLA Ops:
  0.0 1.1 reshape_squeeze.3
  1.2 1.3 pad_maximum_fusion
  2.5 0.7 copy.33
  3.3 1.2 pad.4.clone
  4.5 4.4 %all-to-all-start = ((bf16[4,640,256]{2,1,0:T(8,128)(2,1)}), bf16[4,640,256]{2,1,0:T(8,128)(2,1)S(1)}, u32[]{:S(2)}, u32[]{:S(2)}) async-start(bf16[4,640,256]{2,1,0:T(8,128)(2,1)} %bitcast.8), calls=%async_computation | async-start | bytes 2621440 | tf_op jit(solution)/shard_map/all_to_all | solution.py:319
  8.9 5.3 %shard_map.82 = (bf16[512,256]{1,0:T(8,128)(2,1)}, bf16[512,256]{1,0:T(8,128)(2,1)}, bf16[512,256]{1,0:T(8,128)(2,1)}, bf16[512,256]{1,0:T(8,128)(2,1)}, bf16[51...) custom-call(s32[1]{0:T(128)} %bitcast.me, ...), custom_call_target="tpu_custom_call" | custom-call | tf_op jit(solution)/shard_map/pallas_call | solution.py:255
  14.2 1.9 collective-permute-start
  16.1 3.5 %collective-permute-start.1 = (bf16[512,256]{1,0:T(8,128)(2,1)}, bf16[512,256]{1,0:T(8,128)(2,1)S(1)}, u32[]{:S(2)}, u32[]{:S(2)}) collective-permute-start(bf16[512,256]{1,0:T(8,128)(2,1)} %get-tuple-element.37), channel_id=1, source_target_pairs={{0,2},{1,3},{2,4},{3,5},{4,6},{5,7},{6,0},{7,1},{8,10},{9,11},{10,... | collective-permute-start | bytes 786440 | tf_op jit(solution)/shard_map/ppermute | solution.py:312
  19.6 7.8 %collective-permute-start.2 = (bf16[512,256]{1,0:T(8,128)(2,1)}, bf16[512,256]{1,0:T(8,128)(2,1)S(1)}, u32[]{:S(2)}, u32[]{:S(2)}) collective-permute-start(bf16[512,256]{1,0:T(8,128)(2,1)} %get-tuple-element.38), channel_id=1, source_target_pairs={{0,3},{1,4},{2,5},{3,6},{4,7},{5,0},{6,1},{7,2},{8,11},{9,12},{10,... | collective-permute-start | bytes 786440 | tf_op jit(solution)/shard_map/ppermute | solution.py:312
  27.3 1.9 collective-permute-start.3
  31.3 0.8 constant_dynamic-slice_fusion
  32.1 8.3 %all-to-all-start.1 = ((bf16[8,80,256]{2,1,0:T(8,128)(2,1)}), bf16[8,80,256]{2,1,0:T(8,128)(2,1)S(1)}, u32[]{:S(2)}, u32[]{:S(2)}) async-start(bf16[8,80,256]{2,1,0:T(8,128)(2,1)} %bitcast.9), calls=%async_computation.1 | async-start | bytes 655360 | tf_op jit(solution)/shard_map/all_to_all | solution.py:319
  40.4 5.2 %fusion = (f32[8,256,256]{2,1,0:T(8,128)}, f32[8,256,256]{2,1,0:T(8,128)}) fusion(f32[256]{0:T(256)S(1)} %fusion.47, f32[8,256]{1,0:T(8,128)S(1)} %fusion.44), kind=kLoop, calls=%fused_computation.12 | loop fusion | flops 24641536 | bytes 4203520 | tf_op jit(solution)/shard_map/jit(_where)/select_n | solution.py:304
  45.6 7.1 %all-to-all-done.1 = bf16[8,80,256]{2,1,0:T(8,128)(2,1)S(1)} async-done(((bf16[8,80,256]{2,1,0:T(8,128)(2,1)}), bf16[8,80,256]{2,1,0:T(8,128)(2,1)S(1)}, u32[]{:S(2)}, u32[]{:S(2)}) %all-to-all-start.1) | async-done | bytes 327712 | tf_op jit(solution)/shard_map/all_to_all | solution.py:319
  52.8 6.4 %collective-permute-start.7 = (bf16[80,256]{1,0:T(8,128)(2,1)S(1)}, bf16[80,256]{1,0:T(8,128)(2,1)S(1)}, u32[]{:S(2)}, u32[]{:S(2)}) collective-permute-start(bf16[80,256]{1,0:T(8,128)(2,1)S(1)} %dynamic-slice_bitcast_fusion.1), channel_id=1, source_target_pairs={{0,256},{256,0},{1,257},{257,1},{2,258},{258,2},{3,259},{259,3},{4... | collective-permute-start | bytes 122888 | tf_op jit(solution)/shard_map/ppermute | solution.py:330
  59.9 2.7 %collective-permute-done.7 = bf16[80,256]{1,0:T(8,128)(2,1)S(1)} collective-permute-done((bf16[80,256]{1,0:T(8,128)(2,1)S(1)}, bf16[80,256]{1,0:T(8,128)(2,1)S(1)}, u32[]{:S(2)}, u32[]{:S(2)}) %collective-permute-start.7) | collective-permute-done | bytes 40992 | tf_op jit(solution)/shard_map/ppermute | solution.py:330
  62.6 1.9 collective-permute-start.4
  64.5 0.8 broadcast_in_dim.8
  65.3 3.4 %all-to-all-start.2 = ((bf16[8,80,256]{2,1,0:T(8,128)(2,1)}), bf16[8,80,256]{2,1,0:T(8,128)(2,1)S(1)}, u32[]{:S(2)}, u32[]{:S(2)}) async-start(bf16[8,80,256]{2,1,0:T(8,128)(2,1)} %broadcast_in_dim.8), calls=%async_computation.2 | async-start | bytes 655360 | tf_op jit(solution)/shard_map/all_to_all | solution.py:325
  68.7 2.9 %collective-permute-start.5 = (bf16[512,256]{1,0:T(8,128)(2,1)S(1)}, bf16[512,256]{1,0:T(8,128)(2,1)S(1)}, u32[]{:S(2)}, u32[]{:S(2)}) collective-permute-start(bf16[512,256]{1,0:T(8,128)(2,1)S(1)} %copy-done.17), channel_id=1, source_target_pairs={{0,6},{1,7},{2,0},{3,1},{4,2},{5,3},{6,4},{7,5},{8,14},{9,15},{10,... | collective-permute-start | bytes 786440 | tf_op jit(solution)/shard_map/ppermute | solution.py:312
  71.6 5.3 %collective-permute-start.6 = (bf16[512,256]{1,0:T(8,128)(2,1)S(1)}, bf16[512,256]{1,0:T(8,128)(2,1)S(1)}, u32[]{:S(2)}, u32[]{:S(2)}) collective-permute-start(bf16[512,256]{1,0:T(8,128)(2,1)S(1)} %copy-done.16), channel_id=1, source_target_pairs={{0,7},{1,0},{2,1},{3,2},{4,3},{5,4},{6,5},{7,6},{8,15},{9,8},{10,9... | collective-permute-start | bytes 786440 | tf_op jit(solution)/shard_map/ppermute | solution.py:312
  76.9 5.0 %fusion.24 = (f32[2048,256]{1,0:T(8,128)}, f32[2048,256]{1,0:T(8,128)}) fusion(f32[2048]{0:T(1024)S(1)} %multiply_multiply_fusion.3, f32[256]{0:T(256)S(1)} %multiply_multiply_fusion.4, f32[]{:T(128)S(6)} %mul.282), kind=kLoop, calls=%fused_computation.36 | loop fusion | flops 23068672 | bytes 4203524 | tf_op jit(solution)/shard_map/mul | solution.py:404
  82.3 1.0 all-to-all-done.2
  83.3 1.1 broadcast_in_dim.9
  84.5 4.8 %all-to-all-start.3 = ((bf16[4,640,256]{2,1,0:T(8,128)(2,1)}), bf16[4,640,256]{2,1,0:T(8,128)(2,1)S(1)}, u32[]{:S(2)}, u32[]{:S(2)}) async-start(bf16[4,640,256]{2,1,0:T(8,128)(2,1)} %broadcast_in_dim.9), calls=%async_computation.3 | async-start | bytes 2621440 | tf_op jit(solution)/shard_map/all_to_all | solution.py:325
  89.6 1.6 dynamic-slice_bitcast_fusion.refs_9_
  91.3 13.3 %shard_map.83 = (bf16[512,256]{1,0:T(8,128)(2,1)}, bf16[512,256]{1,0:T(8,128)(2,1)}, bf16[512,256]{1,0:T(8,128)(2,1)}, bf16[512,256]{1,0:T(8,128)(2,1)}, bf16[51...) custom-call(bf16[512,256]{1,0:T(8,128)(2,1)} %get-tuple-element.43.refs_0_, ...), custom_call_target="tpu_custom_call" | custom-call | tf_op jit(solution)/shard_map/pallas_call | solution.py:255
  104.6 3.5 %all-to-all-done.3 = bf16[4,640,256]{2,1,0:T(8,128)(2,1)S(1)} async-done(((bf16[4,640,256]{2,1,0:T(8,128)(2,1)}), bf16[4,640,256]{2,1,0:T(8,128)(2,1)S(1)}, u32[]{:S(2)}, u32[]{:S(2)}) %all-to-all-start.3) | async-done | bytes 1310752 | tf_op jit(solution)/shard_map/all_to_all | solution.py:325
  108.2 1.9 collective-permute-start.15
  110.1 1.2 collective-permute-done.15
  111.4 0.9 broadcast_in_dim.10
  112.3 4.8 %all-to-all-start.4 = ((bf16[4,320,256]{2,1,0:T(8,128)(2,1)}), bf16[4,320,256]{2,1,0:T(8,128)(2,1)S(1)}, u32[]{:S(2)}, u32[]{:S(2)}) async-start(bf16[4,320,256]{2,1,0:T(8,128)(2,1)} %broadcast_in_dim.10), calls=%async_computation.4 | async-start | bytes 1310720 | tf_op jit(solution)/shard_map/all_to_all | solution.py:325
  117.7 1.9 collective-permute-start.8
  119.7 3.4 %collective-permute-start.9 = (bf16[512,256]{1,0:T(8,128)(2,1)}, bf16[512,256]{1,0:T(8,128)(2,1)S(1)}, u32[]{:S(2)}, u32[]{:S(2)}) collective-permute-start(bf16[512,256]{1,0:T(8,128)(2,1)} %get-tuple-element.55), channel_id=1, source_target_pairs={{0,2},{1,3},{2,4},{3,5},{4,6},{5,7},{6,0},{7,1},{8,10},{9,11},{10,... | collective-permute-start | bytes 786440 | tf_op jit(solution)/shard_map/ppermute | solution.py:312
  123.0 3.1 %collective-permute-start.10 = (bf16[512,256]{1,0:T(8,128)(2,1)}, bf16[512,256]{1,0:T(8,128)(2,1)S(1)}, u32[]{:S(2)}, u32[]{:S(2)}) collective-permute-start(bf16[512,256]{1,0:T(8,128)(2,1)} %get-tuple-element.56), channel_id=1, source_target_pairs={{0,3},{1,4},{2,5},{3,6},{4,7},{5,0},{6,1},{7,2},{8,11},{9,12},{10,... | collective-permute-start | bytes 786440 | tf_op jit(solution)/shard_map/ppermute | solution.py:312
  126.1 4.5 %collective-permute-start.11 = (bf16[512,256]{1,0:T(8,128)(2,1)}, bf16[512,256]{1,0:T(8,128)(2,1)S(1)}, u32[]{:S(2)}, u32[]{:S(2)}) collective-permute-start(bf16[512,256]{1,0:T(8,128)(2,1)} %get-tuple-element.57), channel_id=1, source_target_pairs={{0,4},{1,5},{2,6},{3,7},{4,0},{5,1},{6,2},{7,3},{8,12},{9,13},{10,... | collective-permute-start | bytes 786440 | tf_op jit(solution)/shard_map/ppermute | solution.py:312
  130.7 2.1 collective-permute-start.12
  132.8 4.2 %negate_select_fusion = (f32[2048,256]{1,0:T(8,128)}, f32[2048,256]{1,0:T(8,128)}) fusion(f32[]{:T(128)S(6)} %mul.306, bf16[2560,256]{1,0:T(8,128)(2,1)S(1)} %bitcast.54), kind=kLoop, calls=%fused_computation.1 | loop fusion | flops 22020096 | bytes 5242884 | tf_op jit(solution)/shard_map/jit(_where)/select_n | solution.py:283
  137.6 2.0 fusion.29
  139.7 2.3 fusion.28
  142.2 0.7 copy-done.20
  142.9 23.1 %collective-permute-start.13 = (bf16[512,256]{1,0:T(8,128)(2,1)S(1)}, bf16[512,256]{1,0:T(8,128)(2,1)S(1)}, u32[]{:S(2)}, u32[]{:S(2)}) collective-permute-start(bf16[512,256]{1,0:T(8,128)(2,1)S(1)} %copy-done.20), channel_id=1, source_target_pairs={{0,6},{1,7},{2,0},{3,1},{4,2},{5,3},{6,4},{7,5},{8,14},{9,15},{10,... | collective-permute-start | bytes 786440 | tf_op jit(solution)/shard_map/ppermute | solution.py:312
  166.1 1.9 collective-permute-start.14
  168.0 3.0 %maximum_maximum_fusion.refs_12_ = bf16[40,160,160]{2,1,0:T(8,128)(2,1)} fusion(bf16[40,80,80]{2,1,0:T(8,128)(2,1)S(1)} %get-tuple-element.68, bf16[40,80,80]{2,1,0:T(8,128)(2,1)S(1)} %get-tuple-element.67, bf16[40,80,80]{2,1,0:T(8,128)(2,1)S(1)} %fusion.48), kind=kLoop, calls=%fused_computation | loop fusion | flops 8192000 | bytes 3584000 | tf_op jit(solution)/shard_map/concatenate | solution.py:363
  171.0 5.4 %collective-permute-done.12.refs_5_ = bf16[512,256]{1,0:T(8,128)(2,1)S(1)} collective-permute-done((bf16[512,256]{1,0:T(8,128)(2,1)}, bf16[512,256]{1,0:T(8,128)(2,1)S(1)}, u32[]{:S(2)}, u32[]{:S(2)}) %collective-permute-start.12) | collective-permute-done | bytes 262176 | tf_op jit(solution)/shard_map/ppermute | solution.py:312
  177.3 17.3 %shard_map.84 = bf16[4,2,8,32,256]{4,3,2,1,0:T(8,128)(2,1)} custom-call(s32[1]{0:T(128)} %bitcast.me, s32[40]{0:T(128)} %and_select_fusion.1.windows, bf16[512,256]{1,0:T(8,128)(2,1)} %get-tuple-element.53.refs_0_, bf16[512,256]{1,0:T(8,128)(2,1)} %copy-done, bf16[512,256]{1,0:T(8,128)(2,1)} %copy-done.1, bf16[512,256]{1,0:T(8,128)(2,1)} %copy-done.2, ...), custom_call_target="tpu_custom_call" | custom-call | tf_op jit(solution)/shard_map/pallas_call | solution.py:255
  194.6 19.5 %all_to_all.35 = bf16[4,2,8,32,256]{4,3,2,1,0:T(8,128)(2,1)S(1)} all-to-all(bf16[4,2,8,32,256]{4,3,2,1,0:T(8,128)(2,1)} %shard_map.84), channel_id=1, replica_groups=mesh['yh'=2,'x'=4,'z'=8,'yl'=4,'core'=2] {'x'}, dimensions={0} | all-to-all | bytes 2097152 | tf_op jit(solution)/shard_map/all_to_all | solution.py:345
  214.3 22.9 %all_to_all.36 = bf16[16,32,256]{2,1,0:T(8,128)(2,1)S(1)} all-to-all(bf16[16,32,256]{2,1,0:T(8,128)(2,1)S(1)} %bitcast.58), channel_id=1, replica_groups=mesh['yh'=2,'x'=4,'z'=8,'yl'=4,'core'=2] {'yh','z'}, dimensions={0} | all-to-all | bytes 524288 | tf_op jit(solution)/shard_map/all_to_all | solution.py:345
  (81 shorter events, 6.2 us)
Async XLA Ops:
  4.5 25.6 %copy-start.15 = (s32[2]{0:T(128)S(1)}, s32[2]{0:T(128)}, u32[]{:S(2)}) copy-start(s32[2]{0:T(128)} %param.13) | copy-start | bytes 28
  4.5 26.9 %all-to-all-start = ((bf16[4,640,256]{2,1,0:T(8,128)(2,1)}), bf16[4,640,256]{2,1,0:T(8,128)(2,1)S(1)}, u32[]{:S(2)}, u32[]{:S(2)}) async-start(bf16[4,640,256]{2,1,0:T(8,128)(2,1)} %bitcast.8), calls=%async_computation | async-start | bytes 2621440 | tf_op jit(solution)/shard_map/all_to_all | solution.py:319
  14.2 54.5 %collective-permute-start = (bf16[512,256]{1,0:T(8,128)(2,1)}, bf16[512,256]{1,0:T(8,128)(2,1)S(1)}, u32[]{:S(2)}, u32[]{:S(2)}) collective-permute-start(bf16[512,256]{1,0:T(8,128)(2,1)} %get-tuple-element.36), channel_id=1, source_target_pairs={{0,1},{1,2},{2,3},{3,4},{4,5},{5,6},{6,7},{7,0},{8,9},{9,10},{10,1... | collective-permute-start | bytes 786440 | tf_op jit(solution)/shard_map/ppermute | solution.py:312
  16.1 55.5 %collective-permute-start.1 = (bf16[512,256]{1,0:T(8,128)(2,1)}, bf16[512,256]{1,0:T(8,128)(2,1)S(1)}, u32[]{:S(2)}, u32[]{:S(2)}) collective-permute-start(bf16[512,256]{1,0:T(8,128)(2,1)} %get-tuple-element.37), channel_id=1, source_target_pairs={{0,2},{1,3},{2,4},{3,5},{4,6},{5,7},{6,0},{7,1},{8,10},{9,11},{10,... | collective-permute-start | bytes 786440 | tf_op jit(solution)/shard_map/ppermute | solution.py:312
  19.6 62.3 %collective-permute-start.2 = (bf16[512,256]{1,0:T(8,128)(2,1)}, bf16[512,256]{1,0:T(8,128)(2,1)S(1)}, u32[]{:S(2)}, u32[]{:S(2)}) collective-permute-start(bf16[512,256]{1,0:T(8,128)(2,1)} %get-tuple-element.38), channel_id=1, source_target_pairs={{0,3},{1,4},{2,5},{3,6},{4,7},{5,0},{6,1},{7,2},{8,11},{9,12},{10,... | collective-permute-start | bytes 786440 | tf_op jit(solution)/shard_map/ppermute | solution.py:312
  27.3 54.6 %collective-permute-start.3 = (bf16[512,256]{1,0:T(8,128)(2,1)}, bf16[512,256]{1,0:T(8,128)(2,1)S(1)}, u32[]{:S(2)}, u32[]{:S(2)}) collective-permute-start(bf16[512,256]{1,0:T(8,128)(2,1)} %get-tuple-element.39), channel_id=1, source_target_pairs={{0,4},{1,5},{2,6},{3,7},{4,0},{5,1},{6,2},{7,3},{8,12},{9,13},{10,... | collective-permute-start | bytes 786440 | tf_op jit(solution)/shard_map/ppermute | solution.py:312
  32.1 20.7 %all-to-all-start.1 = ((bf16[8,80,256]{2,1,0:T(8,128)(2,1)}), bf16[8,80,256]{2,1,0:T(8,128)(2,1)S(1)}, u32[]{:S(2)}, u32[]{:S(2)}) async-start(bf16[8,80,256]{2,1,0:T(8,128)(2,1)} %bitcast.9), calls=%async_computation.1 | async-start | bytes 655360 | tf_op jit(solution)/shard_map/all_to_all | solution.py:319
  40.4 22.2 %copy-start.18 = (bf16[512,256]{1,0:T(8,128)(2,1)S(1)}, bf16[512,256]{1,0:T(8,128)(2,1)}, u32[]{:S(2)}) copy-start(bf16[512,256]{1,0:T(8,128)(2,1)} %get-tuple-element.40) | copy-start | bytes 786436
  40.4 28.3 %copy-start.17 = (bf16[512,256]{1,0:T(8,128)(2,1)S(1)}, bf16[512,256]{1,0:T(8,128)(2,1)}, u32[]{:S(2)}) copy-start(bf16[512,256]{1,0:T(8,128)(2,1)} %get-tuple-element.41) | copy-start | bytes 786436
  40.4 31.2 %copy-start.16 = (bf16[512,256]{1,0:T(8,128)(2,1)S(1)}, bf16[512,256]{1,0:T(8,128)(2,1)}, u32[]{:S(2)}) copy-start(bf16[512,256]{1,0:T(8,128)(2,1)} %get-tuple-element.42) | copy-start | bytes 786436
  52.8 9.8 %collective-permute-start.7 = (bf16[80,256]{1,0:T(8,128)(2,1)S(1)}, bf16[80,256]{1,0:T(8,128)(2,1)S(1)}, u32[]{:S(2)}, u32[]{:S(2)}) collective-permute-start(bf16[80,256]{1,0:T(8,128)(2,1)S(1)} %dynamic-slice_bitcast_fusion.1), channel_id=1, source_target_pairs={{0,256},{256,0},{1,257},{257,1},{2,258},{258,2},{3,259},{259,3},{4... | collective-permute-start | bytes 122888 | tf_op jit(solution)/shard_map/ppermute | solution.py:330
  62.6 19.4 %collective-permute-start.4 = (bf16[512,256]{1,0:T(8,128)(2,1)S(1)}, bf16[512,256]{1,0:T(8,128)(2,1)S(1)}, u32[]{:S(2)}, u32[]{:S(2)}) collective-permute-start(bf16[512,256]{1,0:T(8,128)(2,1)S(1)} %copy-done.18), channel_id=1, source_target_pairs={{0,5},{1,6},{2,7},{3,0},{4,1},{5,2},{6,3},{7,4},{8,13},{9,14},{10,... | collective-permute-start | bytes 786440 | tf_op jit(solution)/shard_map/ppermute | solution.py:312
  65.3 18.0 %all-to-all-start.2 = ((bf16[8,80,256]{2,1,0:T(8,128)(2,1)}), bf16[8,80,256]{2,1,0:T(8,128)(2,1)S(1)}, u32[]{:S(2)}, u32[]{:S(2)}) async-start(bf16[8,80,256]{2,1,0:T(8,128)(2,1)} %broadcast_in_dim.8), calls=%async_computation.2 | async-start | bytes 655360 | tf_op jit(solution)/shard_map/all_to_all | solution.py:325
  68.7 13.2 %copy-start.7 = (bf16[512,256]{1,0:T(8,128)(2,1)}, bf16[512,256]{1,0:T(8,128)(2,1)S(1)}, u32[]{:S(2)}) copy-start(bf16[512,256]{1,0:T(8,128)(2,1)S(1)} %collective-permute-done.refs_1_) | copy-start | bytes 786436
  68.7 13.2 %collective-permute-start.5 = (bf16[512,256]{1,0:T(8,128)(2,1)S(1)}, bf16[512,256]{1,0:T(8,128)(2,1)S(1)}, u32[]{:S(2)}, u32[]{:S(2)}) collective-permute-start(bf16[512,256]{1,0:T(8,128)(2,1)S(1)} %copy-done.17), channel_id=1, source_target_pairs={{0,6},{1,7},{2,0},{3,1},{4,2},{5,3},{6,4},{7,5},{8,14},{9,15},{10,... | collective-permute-start | bytes 786440 | tf_op jit(solution)/shard_map/ppermute | solution.py:312
  71.6 10.3 %copy-start.8 = (bf16[512,256]{1,0:T(8,128)(2,1)}, bf16[512,256]{1,0:T(8,128)(2,1)S(1)}, u32[]{:S(2)}) copy-start(bf16[512,256]{1,0:T(8,128)(2,1)S(1)} %collective-permute-done.1.refs_2_) | copy-start | bytes 786436
  71.6 10.7 %collective-permute-start.6 = (bf16[512,256]{1,0:T(8,128)(2,1)S(1)}, bf16[512,256]{1,0:T(8,128)(2,1)S(1)}, u32[]{:S(2)}, u32[]{:S(2)}) collective-permute-start(bf16[512,256]{1,0:T(8,128)(2,1)S(1)} %copy-done.16), channel_id=1, source_target_pairs={{0,7},{1,0},{2,1},{3,2},{4,3},{5,4},{6,5},{7,6},{8,15},{9,8},{10,9... | collective-permute-start | bytes 786440 | tf_op jit(solution)/shard_map/ppermute | solution.py:312
  81.9 2.5 %copy-start.9 = (bf16[512,256]{1,0:T(8,128)(2,1)}, bf16[512,256]{1,0:T(8,128)(2,1)S(1)}, u32[]{:S(2)}) copy-start(bf16[512,256]{1,0:T(8,128)(2,1)S(1)} %collective-permute-done.2.refs_3_) | copy-start | bytes 786436
  81.9 2.5 %copy-start.10 = (bf16[512,256]{1,0:T(8,128)(2,1)}, bf16[512,256]{1,0:T(8,128)(2,1)S(1)}, u32[]{:S(2)}) copy-start(bf16[512,256]{1,0:T(8,128)(2,1)S(1)} %collective-permute-done.3.refs_4_) | copy-start | bytes 786436
  81.9 2.5 %copy-start.11 = (bf16[512,256]{1,0:T(8,128)(2,1)}, bf16[512,256]{1,0:T(8,128)(2,1)S(1)}, u32[]{:S(2)}) copy-start(bf16[512,256]{1,0:T(8,128)(2,1)S(1)} %collective-permute-done.4.refs_5_) | copy-start | bytes 786436
  82.0 2.5 %copy-start.12 = (bf16[512,256]{1,0:T(8,128)(2,1)}, bf16[512,256]{1,0:T(8,128)(2,1)S(1)}, u32[]{:S(2)}) copy-start(bf16[512,256]{1,0:T(8,128)(2,1)S(1)} %collective-permute-done.5.refs_6_) | copy-start | bytes 786436
  82.3 2.1 copy-start.13
  83.3 6.0 %copy-start.14 = (s32[64,40]{0,1:T(8,128)S(1)}, s32[64,40]{0,1:T(8,128)}, u32[]{:S(2)}) copy-start(s32[64,40]{0,1:T(8,128)} %param.11) | copy-start | bytes 30724
  84.5 23.7 %all-to-all-start.3 = ((bf16[4,640,256]{2,1,0:T(8,128)(2,1)}), bf16[4,640,256]{2,1,0:T(8,128)(2,1)S(1)}, u32[]{:S(2)}, u32[]{:S(2)}) async-start(bf16[4,640,256]{2,1,0:T(8,128)(2,1)} %broadcast_in_dim.9), calls=%async_computation.3 | async-start | bytes 2621440 | tf_op jit(solution)/shard_map/all_to_all | solution.py:325
  108.2 3.2 %collective-permute-start.15 = (bf16[160,256]{1,0:T(8,128)(2,1)S(1)}, bf16[160,256]{1,0:T(8,128)(2,1)S(1)}, u32[]{:S(2)}, u32[]{:S(2)}) collective-permute-start(bf16[160,256]{1,0:T(8,128)(2,1)S(1)} %slice.27), channel_id=1, source_target_pairs={{0,1},{1,0},{2,3},{3,2},{4,5},{5,4},{6,7},{7,6},{8,9},{9,8},{10,11... | collective-permute-start | bytes 245768 | tf_op jit(solution)/shard_map/ppermute | solution.py:330
  112.3 24.7 %all-to-all-start.4 = ((bf16[4,320,256]{2,1,0:T(8,128)(2,1)}), bf16[4,320,256]{2,1,0:T(8,128)(2,1)S(1)}, u32[]{:S(2)}, u32[]{:S(2)}) async-start(bf16[4,320,256]{2,1,0:T(8,128)(2,1)} %broadcast_in_dim.10), calls=%async_computation.4 | async-start | bytes 1310720 | tf_op jit(solution)/shard_map/all_to_all | solution.py:325
  117.7 24.5 %collective-permute-start.8 = (bf16[512,256]{1,0:T(8,128)(2,1)}, bf16[512,256]{1,0:T(8,128)(2,1)S(1)}, u32[]{:S(2)}, u32[]{:S(2)}) collective-permute-start(bf16[512,256]{1,0:T(8,128)(2,1)} %get-tuple-element.54), channel_id=1, source_target_pairs={{0,1},{1,2},{2,3},{3,4},{4,5},{5,6},{6,7},{7,0},{8,9},{9,10},{10,1... | collective-permute-start | bytes 786440 | tf_op jit(solution)/shard_map/ppermute | solution.py:312
  119.7 46.4 %collective-permute-start.9 = (bf16[512,256]{1,0:T(8,128)(2,1)}, bf16[512,256]{1,0:T(8,128)(2,1)S(1)}, u32[]{:S(2)}, u32[]{:S(2)}) collective-permute-start(bf16[512,256]{1,0:T(8,128)(2,1)} %get-tuple-element.55), channel_id=1, source_target_pairs={{0,2},{1,3},{2,4},{3,5},{4,6},{5,7},{6,0},{7,1},{8,10},{9,11},{10,... | collective-permute-start | bytes 786440 | tf_op jit(solution)/shard_map/ppermute | solution.py:312
  123.0 47.9 %collective-permute-start.10 = (bf16[512,256]{1,0:T(8,128)(2,1)}, bf16[512,256]{1,0:T(8,128)(2,1)S(1)}, u32[]{:S(2)}, u32[]{:S(2)}) collective-permute-start(bf16[512,256]{1,0:T(8,128)(2,1)} %get-tuple-element.56), channel_id=1, source_target_pairs={{0,3},{1,4},{2,5},{3,6},{4,7},{5,0},{6,1},{7,2},{8,11},{9,12},{10,... | collective-permute-start | bytes 786440 | tf_op jit(solution)/shard_map/ppermute | solution.py:312
  126.1 44.9 %collective-permute-start.11 = (bf16[512,256]{1,0:T(8,128)(2,1)}, bf16[512,256]{1,0:T(8,128)(2,1)S(1)}, u32[]{:S(2)}, u32[]{:S(2)}) collective-permute-start(bf16[512,256]{1,0:T(8,128)(2,1)} %get-tuple-element.57), channel_id=1, source_target_pairs={{0,4},{1,5},{2,6},{3,7},{4,0},{5,1},{6,2},{7,3},{8,12},{9,13},{10,... | collective-permute-start | bytes 786440 | tf_op jit(solution)/shard_map/ppermute | solution.py:312
  130.7 45.7 %collective-permute-start.12 = (bf16[512,256]{1,0:T(8,128)(2,1)}, bf16[512,256]{1,0:T(8,128)(2,1)S(1)}, u32[]{:S(2)}, u32[]{:S(2)}) collective-permute-start(bf16[512,256]{1,0:T(8,128)(2,1)} %get-tuple-element.58), channel_id=1, source_target_pairs={{0,5},{1,6},{2,7},{3,0},{4,1},{5,2},{6,3},{7,4},{8,13},{9,14},{10,... | collective-permute-start | bytes 786440 | tf_op jit(solution)/shard_map/ppermute | solution.py:312
  142.0 1.0 copy-start.20
  142.0 24.1 %copy-start.19 = (bf16[512,256]{1,0:T(8,128)(2,1)S(1)}, bf16[512,256]{1,0:T(8,128)(2,1)}, u32[]{:S(2)}) copy-start(bf16[512,256]{1,0:T(8,128)(2,1)} %get-tuple-element.60) | copy-start | bytes 786436
  142.2 28.7 %copy-start = (bf16[512,256]{1,0:T(8,128)(2,1)}, bf16[512,256]{1,0:T(8,128)(2,1)S(1)}, u32[]{:S(2)}) copy-start(bf16[512,256]{1,0:T(8,128)(2,1)S(1)} %collective-permute-done.8.refs_1_) | copy-start | bytes 786436
  142.9 33.5 %collective-permute-start.13 = (bf16[512,256]{1,0:T(8,128)(2,1)S(1)}, bf16[512,256]{1,0:T(8,128)(2,1)S(1)}, u32[]{:S(2)}, u32[]{:S(2)}) collective-permute-start(bf16[512,256]{1,0:T(8,128)(2,1)S(1)} %copy-done.20), channel_id=1, source_target_pairs={{0,6},{1,7},{2,0},{3,1},{4,2},{5,3},{6,4},{7,5},{8,14},{9,15},{10,... | collective-permute-start | bytes 786440 | tf_op jit(solution)/shard_map/ppermute | solution.py:312
  166.1 4.9 %copy-start.1 = (bf16[512,256]{1,0:T(8,128)(2,1)}, bf16[512,256]{1,0:T(8,128)(2,1)S(1)}, u32[]{:S(2)}) copy-start(bf16[512,256]{1,0:T(8,128)(2,1)S(1)} %collective-permute-done.9.refs_2_) | copy-start | bytes 786436
  166.1 10.3 %collective-permute-start.14 = (bf16[512,256]{1,0:T(8,128)(2,1)S(1)}, bf16[512,256]{1,0:T(8,128)(2,1)S(1)}, u32[]{:S(2)}, u32[]{:S(2)}) collective-permute-start(bf16[512,256]{1,0:T(8,128)(2,1)S(1)} %copy-done.19), channel_id=1, source_target_pairs={{0,7},{1,0},{2,1},{3,2},{4,3},{5,4},{6,5},{7,6},{8,15},{9,8},{10,9... | collective-permute-start | bytes 786440 | tf_op jit(solution)/shard_map/ppermute | solution.py:312
  171.0 5.5 %copy-start.2 = (bf16[512,256]{1,0:T(8,128)(2,1)}, bf16[512,256]{1,0:T(8,128)(2,1)S(1)}, u32[]{:S(2)}) copy-start(bf16[512,256]{1,0:T(8,128)(2,1)S(1)} %collective-permute-done.10.refs_3_) | copy-start | bytes 786436
  171.0 5.4 %copy-start.3 = (bf16[512,256]{1,0:T(8,128)(2,1)}, bf16[512,256]{1,0:T(8,128)(2,1)S(1)}, u32[]{:S(2)}) copy-start(bf16[512,256]{1,0:T(8,128)(2,1)S(1)} %collective-permute-done.11.refs_4_) | copy-start | bytes 786436
  176.4 0.7 copy-start.4
  176.4 0.8 copy-start.5
  176.4 0.9 copy-start.6

commit v4 on v3

--- a/solution.py
+++ b/solution.py
@@ -18,7 +18,6 @@
 FREQ_AXES = ("yh", "x", "z")
 CUT_AXES = ("yl", "core")
 RADIX = 8
-BLOCK_GROUP = 4
 f32 = jnp.float32
 bf16 = jnp.bfloat16
 
@@ -176,16 +175,18 @@
     lax.fori_loop(0, base // 16, aft, 0)
 
 
-def lines_inverse_kernel(me, windows, *refs):
+def lines_inverse_kernel(me, starts, lengths, *refs):
     fields, refs = refs[:RADIX], refs[RADIX:]
     table, turn = refs[:2]
     later, (out, back, turned, final), held, done = refs[2:7], refs[7:11], refs[11:16], refs[16]
-    cos_u, sin_u, pairs, cos_r, sin_r = held
+    cos_u, sin_u, matrices, cos_r, sin_r = held
     copies = fetch(later, held, done)
     rows, base = fields[0].shape[0] // 2, fields[0].shape[1]
-    blocks, reach = pairs.shape[0], pairs.shape[1] // 2
+    cuts, _, share, capacity = matrices.shape[:4]
+    reach = capacity + 16
     tail = pl.ds(RADIX * base, turned.shape[1] - RADIX * base)
     turned[:, tail, :] = jnp.zeros((2, tail.size, rows), bf16)
+    final[:, tail, :] = jnp.zeros((2, tail.size, rows), f32)
     for d, field in enumerate(fields):
         first = lax.dot_general(
             table[:, :base], field[:rows], (((1,), (1,)), ((), ())), preferred_element_type=f32
@@ -220,20 +221,40 @@
 
     lax.fori_loop(0, base // 16, aft, 0)
 
-    def some_blocks(group, carry):
+    spot = lax.broadcasted_iota(jnp.int32, (reach, rows), 0)
+
+    def some_blocks(cut, carry):
         cells, changes = [], []
-        for one in range(BLOCK_GROUP):
-            c = group * BLOCK_GROUP + one
-            cell = pl.ds(pl.multiple_of(windows[c] * 16, 16), reach)
-            both = jnp.concatenate([turned[0, cell, :], turned[1, cell, :]], axis=0)
+        for one in range(share):
+            c = cut * share + one
+            start, length = starts[c], lengths[c]
+            cell = pl.ds(pl.multiple_of(start // 16 * 16, 16), reach)
+            offset = start % 16
+            lift = jnp.where(offset == 0, 0, reach - offset)
+            inside = spot < length
+            parts = []
+            for part in range(2):
+                window = pltpu.roll(turned[part, cell, :].astype(f32), lift, 0)
+                parts.append(jnp.where(inside, window, 0.0)[:capacity].astype(bf16))
+            both = jnp.concatenate([matrices[cut, 0, one], matrices[cut, 1, one]], axis=0)
+            by_re = jnp.dot(both, parts[0], preferred_element_type=f32)
+            by_im = jnp.dot(both, parts[1], preferred_element_type=f32)
+            change = (
+                by_re[:capacity] - by_im[capacity:],
+                by_re[capacity:] + by_im[:capacity],
+            )
+            moved = []
+            for value in change:
+                value = jnp.concatenate([value, jnp.zeros((16, rows), f32)], axis=0)
+                moved.append(pltpu.roll(jnp.where(inside, value, 0.0), offset, 0))
             cells.append(cell)
-            changes.append(jnp.dot(pairs[c], both, preferred_element_type=f32))
+            changes.append(moved)
         for cell, change in zip(cells, changes):
-            final[0, cell, :] += change[:reach]
-            final[1, cell, :] += change[reach:]
-        return carry
-
-    lax.fori_loop(0, blocks // BLOCK_GROUP, some_blocks, 0)
+            final[0, cell, :] += change[0]
+            final[1, cell, :] += change[1]
+        return carry
+
+    lax.fori_loop(0, cuts, some_blocks, 0)
 
     def image(tile, carry):
         cell = pl.ds(pl.multiple_of(tile * 16, 16), 16)
@@ -245,7 +266,7 @@
         ).astype(bf16)
         return carry
 
-    lax.fori_loop(0, RADIX * base // 16, image, 0)
+    lax.fori_loop(0, RADIX * base // 16, image, 0, unroll=4)
 
 
 def call(kernel, out_shape, scratch, *operands, scalars=0, later=0):
@@ -346,23 +367,6 @@
     return jnp.sum(terms.astype(f32), axis=0).astype(kind)
 
 
-def block_windows(matrices, starts, lengths):
-    capacity = matrices.shape[2]
-    reach = capacity + 16
-    windows = starts // 16
-    slots = jnp.arange(capacity, dtype=jnp.int32)
-    spots = jnp.arange(reach, dtype=jnp.int32)
-    place = (spots[None, :, None] == slots[None, None, :] + (starts % 16)[:, None, None]) & (
-        slots[None, None, :] < lengths[:, None, None]
-    )
-    place = place.astype(bf16)
-    moved = jnp.einsum("cia,dcab->dcib", place, matrices, preferred_element_type=f32).astype(bf16)
-    moved = jnp.einsum("dcib,cjb->dcij", moved, place, preferred_element_type=f32).astype(bf16)
-    upper = jnp.concatenate([moved[0], -moved[1]], axis=2)
-    lower = jnp.concatenate([moved[1], moved[0]], axis=2)
-    return windows, jnp.concatenate([upper, lower], axis=1)
-
-
 def step(wavefield, slowness, block_inverse, block_lengths, slab_owner, shot_position):
     counts = tuple(lax.axis_size(name) for name in FREQ_AXES)
     freq_total = math.prod(counts)
@@ -408,10 +412,6 @@
     filled = joined.shape[0]
     joined = jnp.pad(joined, ((0, -filled % pieces), (0, 0)))
     share = join(from_owner(joined, owner_id), "z")
-    columns, prop_re, prop_im, cos_r, sin_r, share = lax.optimization_barrier(
-        (columns, prop_re, prop_im, cos_r, sin_r, share)
-    )
-
     restored = call(
         across_kernel,
         [chunk] * RADIX,
@@ -427,7 +427,8 @@
     )
     row_field = rotate(restored, CUT_AXES)
 
-    joined, _ = lax.optimization_barrier((join(share, "x"), restored[0]))
+    share, _ = lax.optimization_barrier((share, restored[0]))
+    joined = join(share, "x")
     mine = joined[extent_y:filled]
     other = swap(mine, "core", 1)
     first = lax.axis_index("core") == 0
@@ -436,15 +437,13 @@
     )
     operators = join(operators, "yl")
     shape = block_inverse.shape
-    matrices = operators.reshape((cut_count,) + shape[1:]).transpose(1, 0, 2, 3, 4)
-    matrices = matrices.reshape(2, -1, shape[3], shape[4])
+    matrices = operators.reshape((cut_count,) + shape[1:])
     lengths = lax.dynamic_index_in_dim(block_lengths, owner_id, 0, keepdims=False)
     starts = jnp.cumsum(lengths) - lengths
-    windows, pairs = block_windows(matrices, starts, lengths)
     phases = angular * depth_step * (joined[:extent_y].astype(f32) - slow_ref)
     cos_u, sin_u = cos_sin(phases)
 
-    late = (cos_u, sin_u, pairs, cos_r, sin_r)
+    late = (cos_u, sin_u, matrices, cos_r, sin_r)
     part = call(
         lines_inverse_kernel,
         jax.ShapeDtypeStruct(
@@ -457,8 +456,8 @@
             *[pltpu.VMEM(value.shape, value.dtype) for value in late],
             pltpu.SemaphoreType.DMA((len(late),)),
         ],
-        device, windows, *row_field, inverse, turn_cols, *late,
-        scalars=2,
+        device, starts, lengths, *row_field, inverse, turn_cols, *late,
+        scalars=3,
         later=len(late),
     )
     part = sum_over(part, "x", bf16)

time: 239 us -> 262 us (1.096)
  the two profiles are of different devices: /device:TPU:8 before, /device:TPU:16 now
where the time goes in v4:
time: 262 us; the launch traced here: 260 us
  starting transfers between devices  101 us (39%)
  waiting for transfers between devices  49.7 us (19%)
  blocking collectives  38.7 us (15%)
  Pallas kernels  38.1 us (15%)
  other arithmetic  18.8 us (7%)
  local copies, waits for them, and re-layouts  12.6 us (5%)
    ppermute x14, starting transfers between devices, rotate(): lax.ppermute(values[d], axes, [(i, (i + d) % size) for i in range(size)])  63.9 us
    all_to_all x2, blocking collectives, sum_over(): terms = lax.all_to_all(part, axis, 0, 0, tiled=True)  38.7 us
    pallas_call x3, Pallas kernels, call(): pl.pallas_call(kernel, out_shape=out_shape, in_specs=[smem] * scalars + [...  38.1 us
    all_to_all x3, waiting for transfers between devices, join(): copies = lax.all_to_all(copies, axis, 0, 0)  18.3 us
    all_to_all x2, waiting for transfers between devices, split(): shaped = lax.all_to_all(shaped, axis, 0, 0)  17.2 us
    all_to_all x3, starting transfers between devices, join(): copies = lax.all_to_all(copies, axis, 0, 0)  15.7 us
    all_to_all x2, starting transfers between devices, split(): shaped = lax.all_to_all(shaped, axis, 0, 0)  14.6 us
    ppermute x14, waiting for transfers between devices, rotate(): lax.ppermute(values[d], axes, [(i, (i + d) % size) for i in range(size)])  9.37 us
  transfers between devices with their start and end apart: 21, of which 6 were waited for; matrix products, arithmetic and copies ran while one was open for 9% of the time, Pallas kernels for 7%

profile of v4, /device:TPU:16, one launch (start us, length us, event | category | flops | bytes accessed | tf_op | source)
XLA Modules:
  0.0 260.4 jit_solution(15540114451896329667)
XLA Ops:
  0.0 1.1 reshape_squeeze.3
  1.2 1.3 pad_maximum_fusion
  2.5 0.7 copy.17
  3.3 1.2 pad.4.clone
  4.4 4.3 %all-to-all-start = ((bf16[4,640,256]{2,1,0:T(8,128)(2,1)}), bf16[4,640,256]{2,1,0:T(8,128)(2,1)S(1)}, u32[]{:S(2)}, u32[]{:S(2)}) async-start(bf16[4,640,256]{2,1,0:T(8,128)(2,1)} %bitcast.7), calls=%async_computation | async-start | bytes 2621440 | tf_op jit(solution)/shard_map/all_to_all | solution.py:340
  9.4 17.2 %all-to-all-done = bf16[4,640,256]{2,1,0:T(8,128)(2,1)S(1)} async-done(((bf16[4,640,256]{2,1,0:T(8,128)(2,1)}), bf16[4,640,256]{2,1,0:T(8,128)(2,1)S(1)}, u32[]{:S(2)}, u32[]{:S(2)}) %all-to-all-start) | async-done | bytes 1310752 | tf_op jit(solution)/shard_map/all_to_all | solution.py:340
  26.6 0.7 constant_dynamic-slice_fusion
  27.4 10.3 %all-to-all-start.1 = ((bf16[8,80,256]{2,1,0:T(8,128)(2,1)}), bf16[8,80,256]{2,1,0:T(8,128)(2,1)S(1)}, u32[]{:S(2)}, u32[]{:S(2)}) async-start(bf16[8,80,256]{2,1,0:T(8,128)(2,1)} %bitcast.8), calls=%async_computation.1 | async-start | bytes 655360 | tf_op jit(solution)/shard_map/all_to_all | solution.py:340
  37.7 5.3 %shard_map.82 = (bf16[512,256]{1,0:T(8,128)(2,1)}, bf16[512,256]{1,0:T(8,128)(2,1)}, bf16[512,256]{1,0:T(8,128)(2,1)}, bf16[512,256]{1,0:T(8,128)(2,1)}, bf16[51...) custom-call(s32[1]{0:T(128)} %bitcast.me, ...), custom_call_target="tpu_custom_call" | custom-call | tf_op jit(solution)/shard_map/pallas_call | solution.py:276
  43.0 1.9 collective-permute-start
  44.9 3.5 %collective-permute-start.1 = (bf16[512,256]{1,0:T(8,128)(2,1)}, bf16[512,256]{1,0:T(8,128)(2,1)S(1)}, u32[]{:S(2)}, u32[]{:S(2)}) collective-permute-start(bf16[512,256]{1,0:T(8,128)(2,1)} %get-tuple-element.24), channel_id=1, source_target_pairs={{0,2},{1,3},{2,4},{3,5},{4,6},{5,7},{6,0},{7,1},{8,10},{9,11},{10,... | collective-permute-start | bytes 786440 | tf_op jit(solution)/shard_map/ppermute | solution.py:333
  48.4 3.1 %collective-permute-start.2 = (bf16[512,256]{1,0:T(8,128)(2,1)}, bf16[512,256]{1,0:T(8,128)(2,1)S(1)}, u32[]{:S(2)}, u32[]{:S(2)}) collective-permute-start(bf16[512,256]{1,0:T(8,128)(2,1)} %get-tuple-element.25), channel_id=1, source_target_pairs={{0,3},{1,4},{2,5},{3,6},{4,7},{5,0},{6,1},{7,2},{8,11},{9,12},{10,... | collective-permute-start | bytes 786440 | tf_op jit(solution)/shard_map/ppermute | solution.py:333
  51.5 3.6 %collective-permute-start.3 = (bf16[512,256]{1,0:T(8,128)(2,1)}, bf16[512,256]{1,0:T(8,128)(2,1)S(1)}, u32[]{:S(2)}, u32[]{:S(2)}) collective-permute-start(bf16[512,256]{1,0:T(8,128)(2,1)} %get-tuple-element.26), channel_id=1, source_target_pairs={{0,4},{1,5},{2,6},{3,7},{4,0},{5,1},{6,2},{7,3},{8,12},{9,13},{10,... | collective-permute-start | bytes 786440 | tf_op jit(solution)/shard_map/ppermute | solution.py:333
  55.2 5.2 %collective-permute-start.14 = (bf16[80,256]{1,0:T(8,128)(2,1)S(1)}, bf16[80,256]{1,0:T(8,128)(2,1)S(1)}, u32[]{:S(2)}, u32[]{:S(2)}) collective-permute-start(bf16[80,256]{1,0:T(8,128)(2,1)S(1)} %dynamic-slice_bitcast_fusion.1), channel_id=1, source_target_pairs={{0,256},{256,0},{1,257},{257,1},{2,258},{258,2},{3,259},{259,3},{4... | collective-permute-start | bytes 122888 | tf_op jit(solution)/shard_map/ppermute | solution.py:351
  60.4 4.8 %collective-permute-done.14 = bf16[80,256]{1,0:T(8,128)(2,1)S(1)} collective-permute-done((bf16[80,256]{1,0:T(8,128)(2,1)S(1)}, bf16[80,256]{1,0:T(8,128)(2,1)S(1)}, u32[]{:S(2)}, u32[]{:S(2)}) %collective-permute-start.14) | collective-permute-done | bytes 40992 | tf_op jit(solution)/shard_map/ppermute | solution.py:351
  65.2 10.5 %collective-permute-start.4 = (bf16[512,256]{1,0:T(8,128)(2,1)}, bf16[512,256]{1,0:T(8,128)(2,1)S(1)}, u32[]{:S(2)}, u32[]{:S(2)}) collective-permute-start(bf16[512,256]{1,0:T(8,128)(2,1)} %get-tuple-element.27), channel_id=1, source_target_pairs={{0,5},{1,6},{2,7},{3,0},{4,1},{5,2},{6,3},{7,4},{8,13},{9,14},{10,... | collective-permute-start | bytes 786440 | tf_op jit(solution)/shard_map/ppermute | solution.py:333
  75.7 0.8 broadcast_in_dim.8
  76.5 7.2 %all-to-all-start.2 = ((bf16[8,80,256]{2,1,0:T(8,128)(2,1)}), bf16[8,80,256]{2,1,0:T(8,128)(2,1)S(1)}, u32[]{:S(2)}, u32[]{:S(2)}) async-start(bf16[8,80,256]{2,1,0:T(8,128)(2,1)} %broadcast_in_dim.8), calls=%async_computation.2 | async-start | bytes 655360 | tf_op jit(solution)/shard_map/all_to_all | solution.py:346
  83.7 4.2 %collective-permute-start.5 = (bf16[512,256]{1,0:T(8,128)(2,1)}, bf16[512,256]{1,0:T(8,128)(2,1)S(1)}, u32[]{:S(2)}, u32[]{:S(2)}) collective-permute-start(bf16[512,256]{1,0:T(8,128)(2,1)} %get-tuple-element.28), channel_id=1, source_target_pairs={{0,6},{1,7},{2,0},{3,1},{4,2},{5,3},{6,4},{7,5},{8,14},{9,15},{10,... | collective-permute-start | bytes 786440 | tf_op jit(solution)/shard_map/ppermute | solution.py:333
  87.9 2.8 %collective-permute-start.6 = (bf16[512,256]{1,0:T(8,128)(2,1)}, bf16[512,256]{1,0:T(8,128)(2,1)S(1)}, u32[]{:S(2)}, u32[]{:S(2)}) collective-permute-start(bf16[512,256]{1,0:T(8,128)(2,1)} %get-tuple-element.29), channel_id=1, source_target_pairs={{0,7},{1,0},{2,1},{3,2},{4,3},{5,4},{6,5},{7,6},{8,15},{9,8},{10,9... | collective-permute-start | bytes 786440 | tf_op jit(solution)/shard_map/ppermute | solution.py:333
  90.7 5.2 %fusion = (f32[8,256,256]{2,1,0:T(8,128)}, f32[8,256,256]{2,1,0:T(8,128)}) fusion(f32[256]{0:T(256)S(1)} %fusion.34, f32[8,256]{1,0:T(8,128)S(1)} %fusion.31), kind=kLoop, calls=%fused_computation.11 | loop fusion | flops 24641536 | bytes 4203520 | tf_op jit(solution)/shard_map/jit(_where)/select_n | solution.py:325
  96.0 1.6 dynamic-slice_bitcast_fusion.refs_9_
  98.6 13.3 %shard_map.83 = (bf16[512,256]{1,0:T(8,128)(2,1)}, bf16[512,256]{1,0:T(8,128)(2,1)}, bf16[512,256]{1,0:T(8,128)(2,1)}, bf16[512,256]{1,0:T(8,128)(2,1)}, bf16[51...) custom-call(bf16[512,256]{1,0:T(8,128)(2,1)} %get-tuple-element.22.refs_0_, ...), custom_call_target="tpu_custom_call" | custom-call | tf_op jit(solution)/shard_map/pallas_call | solution.py:276
  111.9 1.2 broadcast_in_dim.9
  113.1 3.5 %all-to-all-start.3 = ((bf16[4,640,256]{2,1,0:T(8,128)(2,1)}), bf16[4,640,256]{2,1,0:T(8,128)(2,1)S(1)}, u32[]{:S(2)}, u32[]{:S(2)}) async-start(bf16[4,640,256]{2,1,0:T(8,128)(2,1)} %broadcast_in_dim.9), calls=%async_computation.3 | async-start | bytes 2621440 | tf_op jit(solution)/shard_map/all_to_all | solution.py:346
  117.9 16.6 %all-to-all-done.3 = bf16[4,640,256]{2,1,0:T(8,128)(2,1)S(1)} async-done(((bf16[4,640,256]{2,1,0:T(8,128)(2,1)}), bf16[4,640,256]{2,1,0:T(8,128)(2,1)S(1)}, u32[]{:S(2)}, u32[]{:S(2)}) %all-to-all-start.3) | async-done | bytes 1310752 | tf_op jit(solution)/shard_map/all_to_all | solution.py:346
  134.6 1.9 collective-permute-start.15
  136.5 0.7 multiply_multiply_fusion.4
  137.2 3.5 %collective-permute-start.10 = (bf16[512,256]{1,0:T(8,128)(2,1)S(1)}, bf16[512,256]{1,0:T(8,128)(2,1)S(1)}, u32[]{:S(2)}, u32[]{:S(2)}) collective-permute-start(bf16[512,256]{1,0:T(8,128)(2,1)S(1)} %copy-done.16), channel_id=1, source_target_pairs={{0,4},{1,5},{2,6},{3,7},{4,0},{5,1},{6,2},{7,3},{8,12},{9,13},{10,... | collective-permute-start | bytes 786440 | tf_op jit(solution)/shard_map/ppermute | solution.py:333
  140.7 3.1 %collective-permute-start.11 = (bf16[512,256]{1,0:T(8,128)(2,1)}, bf16[512,256]{1,0:T(8,128)(2,1)S(1)}, u32[]{:S(2)}, u32[]{:S(2)}) collective-permute-start(bf16[512,256]{1,0:T(8,128)(2,1)} %get-tuple-element.35), channel_id=1, source_target_pairs={{0,5},{1,6},{2,7},{3,0},{4,1},{5,2},{6,3},{7,4},{8,13},{9,14},{10,... | collective-permute-start | bytes 786440 | tf_op jit(solution)/shard_map/ppermute | solution.py:333
  143.9 0.9 broadcast_in_dim.10
  144.8 4.9 %all-to-all-start.4 = ((bf16[4,320,256]{2,1,0:T(8,128)(2,1)}), bf16[4,320,256]{2,1,0:T(8,128)(2,1)S(1)}, u32[]{:S(2)}, u32[]{:S(2)}) async-start(bf16[4,320,256]{2,1,0:T(8,128)(2,1)} %broadcast_in_dim.10), calls=%async_computation.4 | async-start | bytes 1310720 | tf_op jit(solution)/shard_map/all_to_all | solution.py:346
  149.7 4.9 %fusion.24 = (f32[2048,256]{1,0:T(8,128)}, f32[2048,256]{1,0:T(8,128)}) fusion(f32[2048]{0:T(1024)S(1)} %multiply_multiply_fusion.3, f32[256]{0:T(256)S(1)} %multiply_multiply_fusion.4, f32[]{:T(128)S(6)} %mul.300), kind=kLoop, calls=%fused_computation.35 | loop fusion | flops 23068672 | bytes 4203524 | tf_op jit(solution)/shard_map/mul | solution.py:408
  155.6 2.5 collective-permute-start.12
  158.1 1.9 collective-permute-start.13
  160.0 2.4 collective-permute-start.7
  162.4 13.9 %collective-permute-start.8 = (bf16[512,256]{1,0:T(8,128)(2,1)}, bf16[512,256]{1,0:T(8,128)(2,1)S(1)}, u32[]{:S(2)}, u32[]{:S(2)}) collective-permute-start(bf16[512,256]{1,0:T(8,128)(2,1)} %get-tuple-element.32), channel_id=1, source_target_pairs={{0,2},{1,3},{2,4},{3,5},{4,6},{5,7},{6,0},{7,1},{8,10},{9,11},{10,... | collective-permute-start | bytes 786440 | tf_op jit(solution)/shard_map/ppermute | solution.py:333
  176.4 7.1 %collective-permute-start.9 = (bf16[512,256]{1,0:T(8,128)(2,1)}, bf16[512,256]{1,0:T(8,128)(2,1)}, u32[]{:S(2)}, u32[]{:S(2)}) collective-permute-start(bf16[512,256]{1,0:T(8,128)(2,1)} %get-tuple-element.33), channel_id=1, source_target_pairs={{0,3},{1,4},{2,5},{3,6},{4,7},{5,0},{6,1},{7,2},{8,11},{9,12},{10,... | collective-permute-start | bytes 786440 | tf_op jit(solution)/shard_map/ppermute | solution.py:333
  183.5 4.3 %negate_select_fusion.2 = (f32[2048,256]{1,0:T(8,128)}, f32[2048,256]{1,0:T(8,128)}) fusion(f32[]{:T(128)S(6)} %mul.283, bf16[2560,256]{1,0:T(8,128)(2,1)S(1)} %bitcast.34), kind=kLoop, calls=%fused_computation.3 | loop fusion | flops 22020096 | bytes 5242884 | tf_op jit(solution)/shard_map/jit(_where)/select_n | solution.py:304
  187.8 1.6 all-to-all-done.4
  189.4 1.6 reshape_reshape.3.refs_12_
  191.0 4.0 %collective-permute-done.12.refs_6_ = bf16[512,256]{1,0:T(8,128)(2,1)S(1)} collective-permute-done((bf16[512,256]{1,0:T(8,128)(2,1)}, bf16[512,256]{1,0:T(8,128)(2,1)S(1)}, u32[]{:S(2)}, u32[]{:S(2)}) %collective-permute-start.12) | collective-permute-done | bytes 262176 | tf_op jit(solution)/shard_map/ppermute | solution.py:333
  195.0 5.3 %collective-permute-done.13.refs_7_ = bf16[512,256]{1,0:T(8,128)(2,1)S(1)} collective-permute-done((bf16[512,256]{1,0:T(8,128)(2,1)}, bf16[512,256]{1,0:T(8,128)(2,1)S(1)}, u32[]{:S(2)}, u32[]{:S(2)}) %collective-permute-start.13) | collective-permute-done | bytes 262176 | tf_op jit(solution)/shard_map/ppermute | solution.py:333
  200.4 0.7 copy-done.3
  201.3 19.5 %shard_map.84 = bf16[4,2,8,32,256]{4,3,2,1,0:T(8,128)(2,1)} custom-call(s32[1]{0:T(128)} %bitcast.me, s32[40]{0:T(128)} %sub.122.starts, s32[40]{0:T(128)} %copy-done.14, bf16[512,256]{1,0:T(8,128)(2,1)} %get-tuple-element.30.refs_0_, bf16[512,256]{1,0:T(8,128)(2,1)} %copy-done.4, bf16[512,256]{1,0:T(8,128)(2,1)} %copy-done.5, ...), custom_call_target="tpu_custom_call" | custom-call | tf_op jit(solution)/shard_map/pallas_call | solution.py:276
  220.8 18.3 %all_to_all.35 = bf16[4,2,8,32,256]{4,3,2,1,0:T(8,128)(2,1)S(1)} all-to-all(bf16[4,2,8,32,256]{4,3,2,1,0:T(8,128)(2,1)} %shard_map.84), channel_id=1, replica_groups=mesh['yh'=2,'x'=4,'z'=8,'yl'=4,'core'=2] {'x'}, dimensions={0} | all-to-all | bytes 2097152 | tf_op jit(solution)/shard_map/all_to_all | solution.py:366
  239.3 20.4 %all_to_all.36 = bf16[16,32,256]{2,1,0:T(8,128)(2,1)S(1)} all-to-all(bf16[16,32,256]{2,1,0:T(8,128)(2,1)S(1)} %bitcast.37), channel_id=1, replica_groups=mesh['yh'=2,'x'=4,'z'=8,'yl'=4,'core'=2] {'yh','z'}, dimensions={0} | all-to-all | bytes 524288 | tf_op jit(solution)/shard_map/all_to_all | solution.py:366
  259.7 0.7 convert_reduce_fusion
  (64 shorter events, 3.9 us)
Async XLA Ops:
  4.4 22.2 %all-to-all-start = ((bf16[4,640,256]{2,1,0:T(8,128)(2,1)}), bf16[4,640,256]{2,1,0:T(8,128)(2,1)S(1)}, u32[]{:S(2)}, u32[]{:S(2)}) async-start(bf16[4,640,256]{2,1,0:T(8,128)(2,1)} %bitcast.7), calls=%async_computation | async-start | bytes 2621440 | tf_op jit(solution)/shard_map/all_to_all | solution.py:340
  27.4 27.8 %all-to-all-start.1 = ((bf16[8,80,256]{2,1,0:T(8,128)(2,1)}), bf16[8,80,256]{2,1,0:T(8,128)(2,1)S(1)}, u32[]{:S(2)}, u32[]{:S(2)}) async-start(bf16[8,80,256]{2,1,0:T(8,128)(2,1)} %bitcast.8), calls=%async_computation.1 | async-start | bytes 655360 | tf_op jit(solution)/shard_map/all_to_all | solution.py:340
  43.0 40.7 %collective-permute-start = (bf16[512,256]{1,0:T(8,128)(2,1)}, bf16[512,256]{1,0:T(8,128)(2,1)S(1)}, u32[]{:S(2)}, u32[]{:S(2)}) collective-permute-start(bf16[512,256]{1,0:T(8,128)(2,1)} %get-tuple-element.23), channel_id=1, source_target_pairs={{0,1},{1,2},{2,3},{3,4},{4,5},{5,6},{6,7},{7,0},{8,9},{9,10},{10,1... | collective-permute-start | bytes 786440 | tf_op jit(solution)/shard_map/ppermute | solution.py:333
  44.9 43.0 %collective-permute-start.1 = (bf16[512,256]{1,0:T(8,128)(2,1)}, bf16[512,256]{1,0:T(8,128)(2,1)S(1)}, u32[]{:S(2)}, u32[]{:S(2)}) collective-permute-start(bf16[512,256]{1,0:T(8,128)(2,1)} %get-tuple-element.24), channel_id=1, source_target_pairs={{0,2},{1,3},{2,4},{3,5},{4,6},{5,7},{6,0},{7,1},{8,10},{9,11},{10,... | collective-permute-start | bytes 786440 | tf_op jit(solution)/shard_map/ppermute | solution.py:333
  48.4 49.1 %collective-permute-start.2 = (bf16[512,256]{1,0:T(8,128)(2,1)}, bf16[512,256]{1,0:T(8,128)(2,1)S(1)}, u32[]{:S(2)}, u32[]{:S(2)}) collective-permute-start(bf16[512,256]{1,0:T(8,128)(2,1)} %get-tuple-element.25), channel_id=1, source_target_pairs={{0,3},{1,4},{2,5},{3,6},{4,7},{5,0},{6,1},{7,2},{8,11},{9,12},{10,... | collective-permute-start | bytes 786440 | tf_op jit(solution)/shard_map/ppermute | solution.py:333
  51.5 46.0 %collective-permute-start.3 = (bf16[512,256]{1,0:T(8,128)(2,1)}, bf16[512,256]{1,0:T(8,128)(2,1)S(1)}, u32[]{:S(2)}, u32[]{:S(2)}) collective-permute-start(bf16[512,256]{1,0:T(8,128)(2,1)} %get-tuple-element.26), channel_id=1, source_target_pairs={{0,4},{1,5},{2,6},{3,7},{4,0},{5,1},{6,2},{7,3},{8,12},{9,13},{10,... | collective-permute-start | bytes 786440 | tf_op jit(solution)/shard_map/ppermute | solution.py:333
  55.2 10.0 %collective-permute-start.14 = (bf16[80,256]{1,0:T(8,128)(2,1)S(1)}, bf16[80,256]{1,0:T(8,128)(2,1)S(1)}, u32[]{:S(2)}, u32[]{:S(2)}) collective-permute-start(bf16[80,256]{1,0:T(8,128)(2,1)S(1)} %dynamic-slice_bitcast_fusion.1), channel_id=1, source_target_pairs={{0,256},{256,0},{1,257},{257,1},{2,258},{258,2},{3,259},{259,3},{4... | collective-permute-start | bytes 122888 | tf_op jit(solution)/shard_map/ppermute | solution.py:351
  65.2 32.3 %collective-permute-start.4 = (bf16[512,256]{1,0:T(8,128)(2,1)}, bf16[512,256]{1,0:T(8,128)(2,1)S(1)}, u32[]{:S(2)}, u32[]{:S(2)}) collective-permute-start(bf16[512,256]{1,0:T(8,128)(2,1)} %get-tuple-element.27), channel_id=1, source_target_pairs={{0,5},{1,6},{2,7},{3,0},{4,1},{5,2},{6,3},{7,4},{8,13},{9,14},{10,... | collective-permute-start | bytes 786440 | tf_op jit(solution)/shard_map/ppermute | solution.py:333
  76.5 35.4 %all-to-all-start.2 = ((bf16[8,80,256]{2,1,0:T(8,128)(2,1)}), bf16[8,80,256]{2,1,0:T(8,128)(2,1)S(1)}, u32[]{:S(2)}, u32[]{:S(2)}) async-start(bf16[8,80,256]{2,1,0:T(8,128)(2,1)} %broadcast_in_dim.8), calls=%async_computation.2 | async-start | bytes 655360 | tf_op jit(solution)/shard_map/all_to_all | solution.py:346
  83.7 12.2 %copy-start.6 = (bf16[512,256]{1,0:T(8,128)(2,1)}, bf16[512,256]{1,0:T(8,128)(2,1)S(1)}, u32[]{:S(2)}) copy-start(bf16[512,256]{1,0:T(8,128)(2,1)S(1)} %collective-permute-done.refs_1_) | copy-start | bytes 786436
  83.7 13.9 %collective-permute-start.5 = (bf16[512,256]{1,0:T(8,128)(2,1)}, bf16[512,256]{1,0:T(8,128)(2,1)S(1)}, u32[]{:S(2)}, u32[]{:S(2)}) collective-permute-start(bf16[512,256]{1,0:T(8,128)(2,1)} %get-tuple-element.28), channel_id=1, source_target_pairs={{0,6},{1,7},{2,0},{3,1},{4,2},{5,3},{6,4},{7,5},{8,14},{9,15},{10,... | collective-permute-start | bytes 786440 | tf_op jit(solution)/shard_map/ppermute | solution.py:333
  87.9 8.1 %copy-start.7 = (bf16[512,256]{1,0:T(8,128)(2,1)}, bf16[512,256]{1,0:T(8,128)(2,1)S(1)}, u32[]{:S(2)}) copy-start(bf16[512,256]{1,0:T(8,128)(2,1)S(1)} %collective-permute-done.1.refs_2_) | copy-start | bytes 786436
  87.9 9.7 %collective-permute-start.6 = (bf16[512,256]{1,0:T(8,128)(2,1)}, bf16[512,256]{1,0:T(8,128)(2,1)S(1)}, u32[]{:S(2)}, u32[]{:S(2)}) collective-permute-start(bf16[512,256]{1,0:T(8,128)(2,1)} %get-tuple-element.29), channel_id=1, source_target_pairs={{0,7},{1,0},{2,1},{3,2},{4,3},{5,4},{6,5},{7,6},{8,15},{9,8},{10,9... | collective-permute-start | bytes 786440 | tf_op jit(solution)/shard_map/ppermute | solution.py:333
  97.5 0.7 copy-start.8
  97.5 0.8 copy-start.9
  97.6 0.9 copy-start.10
  97.6 1.0 copy-start.11
  97.6 1.0 copy-start.12
  111.9 4.7 %copy-start.15 = (s32[2]{0:T(128)S(1)}, s32[2]{0:T(128)}, u32[]{:S(2)}) copy-start(s32[2]{0:T(128)} %param.13) | copy-start | bytes 28
  111.9 25.3 %copy-start.16 = (bf16[512,256]{1,0:T(8,128)(2,1)S(1)}, bf16[512,256]{1,0:T(8,128)(2,1)}, u32[]{:S(2)}) copy-start(bf16[512,256]{1,0:T(8,128)(2,1)} %get-tuple-element.34) | copy-start | bytes 786436
  113.1 21.5 %all-to-all-start.3 = ((bf16[4,640,256]{2,1,0:T(8,128)(2,1)}), bf16[4,640,256]{2,1,0:T(8,128)(2,1)S(1)}, u32[]{:S(2)}, u32[]{:S(2)}) async-start(bf16[4,640,256]{2,1,0:T(8,128)(2,1)} %broadcast_in_dim.9), calls=%async_computation.3 | async-start | bytes 2621440 | tf_op jit(solution)/shard_map/all_to_all | solution.py:346
  134.6 9.2 %collective-permute-start.15 = (bf16[160,256]{1,0:T(8,128)(2,1)S(1)}, bf16[160,256]{1,0:T(8,128)(2,1)S(1)}, u32[]{:S(2)}, u32[]{:S(2)}) collective-permute-start(bf16[160,256]{1,0:T(8,128)(2,1)S(1)} %slice.21), channel_id=1, source_target_pairs={{0,1},{1,0},{2,3},{3,2},{4,5},{5,4},{6,7},{7,6},{8,9},{9,8},{10,11... | collective-permute-start | bytes 245768 | tf_op jit(solution)/shard_map/ppermute | solution.py:351
  137.2 25.2 %collective-permute-start.10 = (bf16[512,256]{1,0:T(8,128)(2,1)S(1)}, bf16[512,256]{1,0:T(8,128)(2,1)S(1)}, u32[]{:S(2)}, u32[]{:S(2)}) collective-permute-start(bf16[512,256]{1,0:T(8,128)(2,1)S(1)} %copy-done.16), channel_id=1, source_target_pairs={{0,4},{1,5},{2,6},{3,7},{4,0},{5,1},{6,2},{7,3},{8,12},{9,13},{10,... | collective-permute-start | bytes 786440 | tf_op jit(solution)/shard_map/ppermute | solution.py:333
  140.7 35.7 %collective-permute-start.11 = (bf16[512,256]{1,0:T(8,128)(2,1)}, bf16[512,256]{1,0:T(8,128)(2,1)S(1)}, u32[]{:S(2)}, u32[]{:S(2)}) collective-permute-start(bf16[512,256]{1,0:T(8,128)(2,1)} %get-tuple-element.35), channel_id=1, source_target_pairs={{0,5},{1,6},{2,7},{3,0},{4,1},{5,2},{6,3},{7,4},{8,13},{9,14},{10,... | collective-permute-start | bytes 786440 | tf_op jit(solution)/shard_map/ppermute | solution.py:333
  144.8 44.6 %all-to-all-start.4 = ((bf16[4,320,256]{2,1,0:T(8,128)(2,1)}), bf16[4,320,256]{2,1,0:T(8,128)(2,1)S(1)}, u32[]{:S(2)}, u32[]{:S(2)}) async-start(bf16[4,320,256]{2,1,0:T(8,128)(2,1)} %broadcast_in_dim.10), calls=%async_computation.4 | async-start | bytes 1310720 | tf_op jit(solution)/shard_map/all_to_all | solution.py:346
  149.7 4.9 %copy-start.13 = (s32[64,40]{0,1:T(8,128)S(1)}, s32[64,40]{0,1:T(8,128)}, u32[]{:S(2)}) copy-start(s32[64,40]{0,1:T(8,128)} %param.11) | copy-start | bytes 30724
  154.8 32.9 %copy-start.14 = (s32[40]{0:T(128)}, s32[40]{0:T(128)S(1)}, u32[]{:S(2)}) copy-start(s32[40]{0:T(128)S(1)} %get-tuple-element.43.lengths) | copy-start | bytes 484
  155.6 39.4 %collective-permute-start.12 = (bf16[512,256]{1,0:T(8,128)(2,1)}, bf16[512,256]{1,0:T(8,128)(2,1)S(1)}, u32[]{:S(2)}, u32[]{:S(2)}) collective-permute-start(bf16[512,256]{1,0:T(8,128)(2,1)} %get-tuple-element.36), channel_id=1, source_target_pairs={{0,6},{1,7},{2,0},{3,1},{4,2},{5,3},{6,4},{7,5},{8,14},{9,15},{10,... | collective-permute-start | bytes 786440 | tf_op jit(solution)/shard_map/ppermute | solution.py:333
  158.1 42.3 %collective-permute-start.13 = (bf16[512,256]{1,0:T(8,128)(2,1)}, bf16[512,256]{1,0:T(8,128)(2,1)S(1)}, u32[]{:S(2)}, u32[]{:S(2)}) collective-permute-start(bf16[512,256]{1,0:T(8,128)(2,1)} %get-tuple-element.37), channel_id=1, source_target_pairs={{0,7},{1,0},{2,1},{3,2},{4,3},{5,4},{6,5},{7,6},{8,15},{9,8},{10,9... | collective-permute-start | bytes 786440 | tf_op jit(solution)/shard_map/ppermute | solution.py:333
  160.0 40.4 %collective-permute-start.7 = (bf16[512,256]{1,0:T(8,128)(2,1)}, bf16[512,256]{1,0:T(8,128)(2,1)S(1)}, u32[]{:S(2)}, u32[]{:S(2)}) collective-permute-start(bf16[512,256]{1,0:T(8,128)(2,1)} %get-tuple-element.31), channel_id=1, source_target_pairs={{0,1},{1,2},{2,3},{3,4},{4,5},{5,6},{6,7},{7,0},{8,9},{9,10},{10,1... | collective-permute-start | bytes 786440 | tf_op jit(solution)/shard_map/ppermute | solution.py:333
  162.4 25.4 %copy-start = (bf16[512,256]{1,0:T(8,128)(2,1)}, bf16[512,256]{1,0:T(8,128)(2,1)S(1)}, u32[]{:S(2)}) copy-start(bf16[512,256]{1,0:T(8,128)(2,1)S(1)} %collective-permute-done.10.refs_4_) | copy-start | bytes 786436
  162.4 37.9 %collective-permute-start.8 = (bf16[512,256]{1,0:T(8,128)(2,1)}, bf16[512,256]{1,0:T(8,128)(2,1)S(1)}, u32[]{:S(2)}, u32[]{:S(2)}) collective-permute-start(bf16[512,256]{1,0:T(8,128)(2,1)} %get-tuple-element.32), channel_id=1, source_target_pairs={{0,2},{1,3},{2,4},{3,5},{4,6},{5,7},{6,0},{7,1},{8,10},{9,11},{10,... | collective-permute-start | bytes 786440 | tf_op jit(solution)/shard_map/ppermute | solution.py:333
  176.4 11.4 %copy-start.1 = (bf16[512,256]{1,0:T(8,128)(2,1)}, bf16[512,256]{1,0:T(8,128)(2,1)S(1)}, u32[]{:S(2)}) copy-start(bf16[512,256]{1,0:T(8,128)(2,1)S(1)} %collective-permute-done.11.refs_5_) | copy-start | bytes 786436
  176.4 24.0 %collective-permute-start.9 = (bf16[512,256]{1,0:T(8,128)(2,1)}, bf16[512,256]{1,0:T(8,128)(2,1)}, u32[]{:S(2)}, u32[]{:S(2)}) collective-permute-start(bf16[512,256]{1,0:T(8,128)(2,1)} %get-tuple-element.33), channel_id=1, source_target_pairs={{0,3},{1,4},{2,5},{3,6},{4,7},{5,0},{6,1},{7,2},{8,11},{9,12},{10,... | collective-permute-start | bytes 786440 | tf_op jit(solution)/shard_map/ppermute | solution.py:333
  195.0 5.4 %copy-start.2 = (bf16[512,256]{1,0:T(8,128)(2,1)}, bf16[512,256]{1,0:T(8,128)(2,1)S(1)}, u32[]{:S(2)}) copy-start(bf16[512,256]{1,0:T(8,128)(2,1)S(1)} %collective-permute-done.12.refs_6_) | copy-start | bytes 786436
  200.4 0.7 copy-start.3
  200.4 0.8 copy-start.4
  200.4 0.9 copy-start.5

commit v5 on v4

--- a/solution.py
+++ b/solution.py
@@ -221,7 +221,9 @@
 
     lax.fori_loop(0, base // 16, aft, 0)
 
-    spot = lax.broadcasted_iota(jnp.int32, (reach, rows), 0)
+    lanes = matrices.shape[4]
+    spot = lax.broadcasted_iota(jnp.int32, (capacity, lanes), 0)
+    mate = lax.broadcasted_iota(jnp.int32, (capacity, lanes), 1)
 
     def some_blocks(cut, carry):
         cells, changes = [], []
@@ -229,26 +231,18 @@
             c = cut * share + one
             start, length = starts[c], lengths[c]
             cell = pl.ds(pl.multiple_of(start // 16 * 16, 16), reach)
-            offset = start % 16
-            lift = jnp.where(offset == 0, 0, reach - offset)
-            inside = spot < length
+            inside = jnp.maximum(spot, mate) < length
             parts = []
             for part in range(2):
-                window = pltpu.roll(turned[part, cell, :].astype(f32), lift, 0)
-                parts.append(jnp.where(inside, window, 0.0)[:capacity].astype(bf16))
-            both = jnp.concatenate([matrices[cut, 0, one], matrices[cut, 1, one]], axis=0)
-            by_re = jnp.dot(both, parts[0], preferred_element_type=f32)
-            by_im = jnp.dot(both, parts[1], preferred_element_type=f32)
-            change = (
-                by_re[:capacity] - by_im[capacity:],
-                by_re[capacity:] + by_im[:capacity],
-            )
-            moved = []
-            for value in change:
-                value = jnp.concatenate([value, jnp.zeros((16, rows), f32)], axis=0)
-                moved.append(pltpu.roll(jnp.where(inside, value, 0.0), offset, 0))
+                value = jnp.where(inside, matrices[cut, part, one].astype(f32), 0.0)
+                value = jnp.concatenate([value, jnp.zeros((reach - capacity, lanes), f32)], axis=0)
+                value = pltpu.roll(pltpu.roll(value, start % 16, 0), start % 16, 1)
+                parts.append(value[:, :reach].astype(bf16))
+            both = jnp.concatenate(parts, axis=0)
+            by_re = jnp.dot(both, turned[0, cell, :], preferred_element_type=f32)
+            by_im = jnp.dot(both, turned[1, cell, :], preferred_element_type=f32)
             cells.append(cell)
-            changes.append(moved)
+            changes.append((by_re[:reach] - by_im[reach:], by_re[reach:] + by_im[:reach]))
         for cell, change in zip(cells, changes):
             final[0, cell, :] += change[0]
             final[1, cell, :] += change[1]
@@ -438,6 +432,7 @@
     operators = join(operators, "yl")
     shape = block_inverse.shape
     matrices = operators.reshape((cut_count,) + shape[1:])
+    matrices = jnp.pad(matrices, ((0, 0),) * 4 + ((0, -shape[4] % 128),))
     lengths = lax.dynamic_index_in_dim(block_lengths, owner_id, 0, keepdims=False)
     starts = jnp.cumsum(lengths) - lengths
     phases = angular * depth_step * (joined[:extent_y].astype(f32) - slow_ref)

time: 262 us -> 259 us (0.989)
  no operation moved by 1% of the time
where the time goes in v5:
time: 259 us; the launch traced here: 258 us
  starting transfers between devices  101 us (39%)
  waiting for transfers between devices  49.2 us (19%)
  blocking collectives  38.7 us (15%)
  Pallas kernels  35.9 us (14%)
  other arithmetic  18.8 us (7%)
  local copies, waits for them, and re-layouts  13 us (5%)
    ppermute x14, starting transfers between devices, rotate(): lax.ppermute(values[d], axes, [(i, (i + d) % size) for i in range(size)])  63.9 us
    all_to_all x2, blocking collectives, sum_over(): terms = lax.all_to_all(part, axis, 0, 0, tiled=True)  38.7 us
    pallas_call x3, Pallas kernels, call(): pl.pallas_call(kernel, out_shape=out_shape, in_specs=[smem] * scalars + [...  35.9 us
    all_to_all x3, waiting for transfers between devices, join(): copies = lax.all_to_all(copies, axis, 0, 0)  18.3 us
    all_to_all x2, waiting for transfers between devices, split(): shaped = lax.all_to_all(shaped, axis, 0, 0)  17.2 us
    all_to_all x3, starting transfers between devices, join(): copies = lax.all_to_all(copies, axis, 0, 0)  15.7 us
    all_to_all x2, starting transfers between devices, split(): shaped = lax.all_to_all(shaped, axis, 0, 0)  14.6 us
    ppermute x14, waiting for transfers between devices, rotate(): lax.ppermute(values[d], axes, [(i, (i + d) % size) for i in range(size)])  8.94 us
  transfers between devices with their start and end apart: 21, of which 6 were waited for; matrix products, arithmetic and copies ran while one was open for 9% of the time, Pallas kernels for 7%

profile of v5, /device:TPU:16, one launch (start us, length us, event | category | flops | bytes accessed | tf_op | source)
XLA Modules:
  0.0 258.2 jit_solution(718003166948504136)
XLA Ops:
  0.0 1.1 reshape_squeeze.3
  1.2 1.3 pad_maximum_fusion
  2.5 0.7 copy.17
  3.3 1.2 pad.8.clone
  4.4 4.3 %all-to-all-start = ((bf16[4,640,256]{2,1,0:T(8,128)(2,1)}), bf16[4,640,256]{2,1,0:T(8,128)(2,1)S(1)}, u32[]{:S(2)}, u32[]{:S(2)}) async-start(bf16[4,640,256]{2,1,0:T(8,128)(2,1)} %bitcast.7), calls=%async_computation | async-start | bytes 2621440 | tf_op jit(solution)/shard_map/all_to_all | solution.py:334
  9.4 17.2 %all-to-all-done = bf16[4,640,256]{2,1,0:T(8,128)(2,1)S(1)} async-done(((bf16[4,640,256]{2,1,0:T(8,128)(2,1)}), bf16[4,640,256]{2,1,0:T(8,128)(2,1)S(1)}, u32[]{:S(2)}, u32[]{:S(2)}) %all-to-all-start) | async-done | bytes 1310752 | tf_op jit(solution)/shard_map/all_to_all | solution.py:334
  26.6 0.7 constant_dynamic-slice_fusion
  27.4 10.3 %all-to-all-start.1 = ((bf16[8,80,256]{2,1,0:T(8,128)(2,1)}), bf16[8,80,256]{2,1,0:T(8,128)(2,1)S(1)}, u32[]{:S(2)}, u32[]{:S(2)}) async-start(bf16[8,80,256]{2,1,0:T(8,128)(2,1)} %bitcast.8), calls=%async_computation.1 | async-start | bytes 655360 | tf_op jit(solution)/shard_map/all_to_all | solution.py:334
  37.7 5.3 %shard_map.82 = (bf16[512,256]{1,0:T(8,128)(2,1)}, bf16[512,256]{1,0:T(8,128)(2,1)}, bf16[512,256]{1,0:T(8,128)(2,1)}, bf16[512,256]{1,0:T(8,128)(2,1)}, bf16[51...) custom-call(s32[1]{0:T(128)} %bitcast.me, ...), custom_call_target="tpu_custom_call" | custom-call | tf_op jit(solution)/shard_map/pallas_call | solution.py:270
  43.0 1.9 collective-permute-start
  44.9 3.5 %collective-permute-start.1 = (bf16[512,256]{1,0:T(8,128)(2,1)}, bf16[512,256]{1,0:T(8,128)(2,1)S(1)}, u32[]{:S(2)}, u32[]{:S(2)}) collective-permute-start(bf16[512,256]{1,0:T(8,128)(2,1)} %get-tuple-element.24), channel_id=1, source_target_pairs={{0,2},{1,3},{2,4},{3,5},{4,6},{5,7},{6,0},{7,1},{8,10},{9,11},{10,... | collective-permute-start | bytes 786440 | tf_op jit(solution)/shard_map/ppermute | solution.py:327
  48.4 3.1 %collective-permute-start.2 = (bf16[512,256]{1,0:T(8,128)(2,1)}, bf16[512,256]{1,0:T(8,128)(2,1)S(1)}, u32[]{:S(2)}, u32[]{:S(2)}) collective-permute-start(bf16[512,256]{1,0:T(8,128)(2,1)} %get-tuple-element.25), channel_id=1, source_target_pairs={{0,3},{1,4},{2,5},{3,6},{4,7},{5,0},{6,1},{7,2},{8,11},{9,12},{10,... | collective-permute-start | bytes 786440 | tf_op jit(solution)/shard_map/ppermute | solution.py:327
  51.5 3.6 %collective-permute-start.3 = (bf16[512,256]{1,0:T(8,128)(2,1)}, bf16[512,256]{1,0:T(8,128)(2,1)S(1)}, u32[]{:S(2)}, u32[]{:S(2)}) collective-permute-start(bf16[512,256]{1,0:T(8,128)(2,1)} %get-tuple-element.26), channel_id=1, source_target_pairs={{0,4},{1,5},{2,6},{3,7},{4,0},{5,1},{6,2},{7,3},{8,12},{9,13},{10,... | collective-permute-start | bytes 786440 | tf_op jit(solution)/shard_map/ppermute | solution.py:327
  55.2 5.2 %collective-permute-start.14 = (bf16[80,256]{1,0:T(8,128)(2,1)S(1)}, bf16[80,256]{1,0:T(8,128)(2,1)S(1)}, u32[]{:S(2)}, u32[]{:S(2)}) collective-permute-start(bf16[80,256]{1,0:T(8,128)(2,1)S(1)} %dynamic-slice_bitcast_fusion.1), channel_id=1, source_target_pairs={{0,256},{256,0},{1,257},{257,1},{2,258},{258,2},{3,259},{259,3},{4... | collective-permute-start | bytes 122888 | tf_op jit(solution)/shard_map/ppermute | solution.py:345
  60.4 4.8 %collective-permute-done.14 = bf16[80,256]{1,0:T(8,128)(2,1)S(1)} collective-permute-done((bf16[80,256]{1,0:T(8,128)(2,1)S(1)}, bf16[80,256]{1,0:T(8,128)(2,1)S(1)}, u32[]{:S(2)}, u32[]{:S(2)}) %collective-permute-start.14) | collective-permute-done | bytes 40992 | tf_op jit(solution)/shard_map/ppermute | solution.py:345
  65.2 10.5 %collective-permute-start.4 = (bf16[512,256]{1,0:T(8,128)(2,1)}, bf16[512,256]{1,0:T(8,128)(2,1)S(1)}, u32[]{:S(2)}, u32[]{:S(2)}) collective-permute-start(bf16[512,256]{1,0:T(8,128)(2,1)} %get-tuple-element.27), channel_id=1, source_target_pairs={{0,5},{1,6},{2,7},{3,0},{4,1},{5,2},{6,3},{7,4},{8,13},{9,14},{10,... | collective-permute-start | bytes 786440 | tf_op jit(solution)/shard_map/ppermute | solution.py:327
  75.7 0.8 broadcast_in_dim.8
  76.5 7.2 %all-to-all-start.2 = ((bf16[8,80,256]{2,1,0:T(8,128)(2,1)}), bf16[8,80,256]{2,1,0:T(8,128)(2,1)S(1)}, u32[]{:S(2)}, u32[]{:S(2)}) async-start(bf16[8,80,256]{2,1,0:T(8,128)(2,1)} %broadcast_in_dim.8), calls=%async_computation.2 | async-start | bytes 655360 | tf_op jit(solution)/shard_map/all_to_all | solution.py:340
  83.7 4.2 %collective-permute-start.5 = (bf16[512,256]{1,0:T(8,128)(2,1)}, bf16[512,256]{1,0:T(8,128)(2,1)S(1)}, u32[]{:S(2)}, u32[]{:S(2)}) collective-permute-start(bf16[512,256]{1,0:T(8,128)(2,1)} %get-tuple-element.28), channel_id=1, source_target_pairs={{0,6},{1,7},{2,0},{3,1},{4,2},{5,3},{6,4},{7,5},{8,14},{9,15},{10,... | collective-permute-start | bytes 786440 | tf_op jit(solution)/shard_map/ppermute | solution.py:327
  87.9 2.8 %collective-permute-start.6 = (bf16[512,256]{1,0:T(8,128)(2,1)}, bf16[512,256]{1,0:T(8,128)(2,1)S(1)}, u32[]{:S(2)}, u32[]{:S(2)}) collective-permute-start(bf16[512,256]{1,0:T(8,128)(2,1)} %get-tuple-element.29), channel_id=1, source_target_pairs={{0,7},{1,0},{2,1},{3,2},{4,3},{5,4},{6,5},{7,6},{8,15},{9,8},{10,9... | collective-permute-start | bytes 786440 | tf_op jit(solution)/shard_map/ppermute | solution.py:327
  90.7 5.2 %fusion = (f32[8,256,256]{2,1,0:T(8,128)}, f32[8,256,256]{2,1,0:T(8,128)}) fusion(f32[256]{0:T(256)S(1)} %fusion.34, f32[8,256]{1,0:T(8,128)S(1)} %fusion.31), kind=kLoop, calls=%fused_computation.11 | loop fusion | flops 24641536 | bytes 4203520 | tf_op jit(solution)/shard_map/jit(_where)/select_n | solution.py:319
  96.0 1.6 dynamic-slice_bitcast_fusion.refs_9_
  98.6 13.3 %shard_map.83 = (bf16[512,256]{1,0:T(8,128)(2,1)}, bf16[512,256]{1,0:T(8,128)(2,1)}, bf16[512,256]{1,0:T(8,128)(2,1)}, bf16[512,256]{1,0:T(8,128)(2,1)}, bf16[51...) custom-call(bf16[512,256]{1,0:T(8,128)(2,1)} %get-tuple-element.22.refs_0_, ...), custom_call_target="tpu_custom_call" | custom-call | tf_op jit(solution)/shard_map/pallas_call | solution.py:270
  111.9 1.2 broadcast_in_dim.9
  113.1 3.5 %all-to-all-start.3 = ((bf16[4,640,256]{2,1,0:T(8,128)(2,1)}), bf16[4,640,256]{2,1,0:T(8,128)(2,1)S(1)}, u32[]{:S(2)}, u32[]{:S(2)}) async-start(bf16[4,640,256]{2,1,0:T(8,128)(2,1)} %broadcast_in_dim.9), calls=%async_computation.3 | async-start | bytes 2621440 | tf_op jit(solution)/shard_map/all_to_all | solution.py:340
  117.9 16.6 %all-to-all-done.3 = bf16[4,640,256]{2,1,0:T(8,128)(2,1)S(1)} async-done(((bf16[4,640,256]{2,1,0:T(8,128)(2,1)}), bf16[4,640,256]{2,1,0:T(8,128)(2,1)S(1)}, u32[]{:S(2)}, u32[]{:S(2)}) %all-to-all-start.3) | async-done | bytes 1310752 | tf_op jit(solution)/shard_map/all_to_all | solution.py:340
  134.6 1.9 collective-permute-start.15
  136.5 0.7 multiply_multiply_fusion.4
  137.2 3.5 %collective-permute-start.10 = (bf16[512,256]{1,0:T(8,128)(2,1)S(1)}, bf16[512,256]{1,0:T(8,128)(2,1)S(1)}, u32[]{:S(2)}, u32[]{:S(2)}) collective-permute-start(bf16[512,256]{1,0:T(8,128)(2,1)S(1)} %copy-done.16), channel_id=1, source_target_pairs={{0,4},{1,5},{2,6},{3,7},{4,0},{5,1},{6,2},{7,3},{8,12},{9,13},{10,... | collective-permute-start | bytes 786440 | tf_op jit(solution)/shard_map/ppermute | solution.py:327
  140.7 3.1 %collective-permute-start.11 = (bf16[512,256]{1,0:T(8,128)(2,1)}, bf16[512,256]{1,0:T(8,128)(2,1)S(1)}, u32[]{:S(2)}, u32[]{:S(2)}) collective-permute-start(bf16[512,256]{1,0:T(8,128)(2,1)} %get-tuple-element.35), channel_id=1, source_target_pairs={{0,5},{1,6},{2,7},{3,0},{4,1},{5,2},{6,3},{7,4},{8,13},{9,14},{10,... | collective-permute-start | bytes 786440 | tf_op jit(solution)/shard_map/ppermute | solution.py:327
  143.9 0.9 broadcast_in_dim.10
  144.8 4.9 %all-to-all-start.4 = ((bf16[4,320,256]{2,1,0:T(8,128)(2,1)}), bf16[4,320,256]{2,1,0:T(8,128)(2,1)S(1)}, u32[]{:S(2)}, u32[]{:S(2)}) async-start(bf16[4,320,256]{2,1,0:T(8,128)(2,1)} %broadcast_in_dim.10), calls=%async_computation.4 | async-start | bytes 1310720 | tf_op jit(solution)/shard_map/all_to_all | solution.py:340
  149.7 4.9 %fusion.24 = (f32[2048,256]{1,0:T(8,128)}, f32[2048,256]{1,0:T(8,128)}) fusion(f32[2048]{0:T(1024)S(1)} %multiply_multiply_fusion.3, f32[256]{0:T(256)S(1)} %multiply_multiply_fusion.4, f32[]{:T(128)S(6)} %mul.300), kind=kLoop, calls=%fused_computation.35 | loop fusion | flops 23068672 | bytes 4203524 | tf_op jit(solution)/shard_map/mul | solution.py:402
  155.6 2.5 collective-permute-start.12
  158.1 1.9 collective-permute-start.13
  160.0 2.4 collective-permute-start.7
  162.4 13.9 %collective-permute-start.8 = (bf16[512,256]{1,0:T(8,128)(2,1)}, bf16[512,256]{1,0:T(8,128)(2,1)S(1)}, u32[]{:S(2)}, u32[]{:S(2)}) collective-permute-start(bf16[512,256]{1,0:T(8,128)(2,1)} %get-tuple-element.32), channel_id=1, source_target_pairs={{0,2},{1,3},{2,4},{3,5},{4,6},{5,7},{6,0},{7,1},{8,10},{9,11},{10,... | collective-permute-start | bytes 786440 | tf_op jit(solution)/shard_map/ppermute | solution.py:327
  176.4 7.1 %collective-permute-start.9 = (bf16[512,256]{1,0:T(8,128)(2,1)}, bf16[512,256]{1,0:T(8,128)(2,1)}, u32[]{:S(2)}, u32[]{:S(2)}) collective-permute-start(bf16[512,256]{1,0:T(8,128)(2,1)} %get-tuple-element.33), channel_id=1, source_target_pairs={{0,3},{1,4},{2,5},{3,6},{4,7},{5,0},{6,1},{7,2},{8,11},{9,12},{10,... | collective-permute-start | bytes 786440 | tf_op jit(solution)/shard_map/ppermute | solution.py:327
  183.5 4.3 %negate_select_fusion.2 = (f32[2048,256]{1,0:T(8,128)}, f32[2048,256]{1,0:T(8,128)}) fusion(f32[]{:T(128)S(6)} %mul.283, bf16[2560,256]{1,0:T(8,128)(2,1)S(1)} %bitcast.34), kind=kLoop, calls=%fused_computation.3 | loop fusion | flops 22020096 | bytes 5242884 | tf_op jit(solution)/shard_map/jit(_where)/select_n | solution.py:298
  187.8 1.6 all-to-all-done.4
  189.9 1.5 pad.9.refs_12_
  191.4 3.6 %collective-permute-done.12.refs_6_ = bf16[512,256]{1,0:T(8,128)(2,1)S(1)} collective-permute-done((bf16[512,256]{1,0:T(8,128)(2,1)}, bf16[512,256]{1,0:T(8,128)(2,1)S(1)}, u32[]{:S(2)}, u32[]{:S(2)}) %collective-permute-start.12) | collective-permute-done | bytes 262176 | tf_op jit(solution)/shard_map/ppermute | solution.py:327
  195.0 5.3 %collective-permute-done.13.refs_7_ = bf16[512,256]{1,0:T(8,128)(2,1)S(1)} collective-permute-done((bf16[512,256]{1,0:T(8,128)(2,1)}, bf16[512,256]{1,0:T(8,128)(2,1)S(1)}, u32[]{:S(2)}, u32[]{:S(2)}) %collective-permute-start.13) | collective-permute-done | bytes 262176 | tf_op jit(solution)/shard_map/ppermute | solution.py:327
  200.4 0.7 copy-done.3
  201.3 17.4 %shard_map.84 = bf16[4,2,8,32,256]{4,3,2,1,0:T(8,128)(2,1)} custom-call(s32[1]{0:T(128)} %bitcast.me, s32[40]{0:T(128)} %sub.122.starts, s32[40]{0:T(128)} %copy-done.14, bf16[512,256]{1,0:T(8,128)(2,1)} %get-tuple-element.30.refs_0_, bf16[512,256]{1,0:T(8,128)(2,1)} %copy-done.4, bf16[512,256]{1,0:T(8,128)(2,1)} %copy-done.5, ...), custom_call_target="tpu_custom_call" | custom-call | tf_op jit(solution)/shard_map/pallas_call | solution.py:270
  218.7 18.3 %all_to_all.35 = bf16[4,2,8,32,256]{4,3,2,1,0:T(8,128)(2,1)S(1)} all-to-all(bf16[4,2,8,32,256]{4,3,2,1,0:T(8,128)(2,1)} %shard_map.84), channel_id=1, replica_groups=mesh['yh'=2,'x'=4,'z'=8,'yl'=4,'core'=2] {'x'}, dimensions={0} | all-to-all | bytes 2097152 | tf_op jit(solution)/shard_map/all_to_all | solution.py:360
  237.2 20.4 %all_to_all.36 = bf16[16,32,256]{2,1,0:T(8,128)(2,1)S(1)} all-to-all(bf16[16,32,256]{2,1,0:T(8,128)(2,1)S(1)} %bitcast.37), channel_id=1, replica_groups=mesh['yh'=2,'x'=4,'z'=8,'yl'=4,'core'=2] {'yh','z'}, dimensions={0} | all-to-all | bytes 524288 | tf_op jit(solution)/shard_map/all_to_all | solution.py:360
  257.6 0.7 convert_reduce_fusion
  (65 shorter events, 4.4 us)
Async XLA Ops:
  4.4 22.2 %all-to-all-start = ((bf16[4,640,256]{2,1,0:T(8,128)(2,1)}), bf16[4,640,256]{2,1,0:T(8,128)(2,1)S(1)}, u32[]{:S(2)}, u32[]{:S(2)}) async-start(bf16[4,640,256]{2,1,0:T(8,128)(2,1)} %bitcast.7), calls=%async_computation | async-start | bytes 2621440 | tf_op jit(solution)/shard_map/all_to_all | solution.py:334
  27.4 27.8 %all-to-all-start.1 = ((bf16[8,80,256]{2,1,0:T(8,128)(2,1)}), bf16[8,80,256]{2,1,0:T(8,128)(2,1)S(1)}, u32[]{:S(2)}, u32[]{:S(2)}) async-start(bf16[8,80,256]{2,1,0:T(8,128)(2,1)} %bitcast.8), calls=%async_computation.1 | async-start | bytes 655360 | tf_op jit(solution)/shard_map/all_to_all | solution.py:334
  43.0 40.7 %collective-permute-start = (bf16[512,256]{1,0:T(8,128)(2,1)}, bf16[512,256]{1,0:T(8,128)(2,1)S(1)}, u32[]{:S(2)}, u32[]{:S(2)}) collective-permute-start(bf16[512,256]{1,0:T(8,128)(2,1)} %get-tuple-element.23), channel_id=1, source_target_pairs={{0,1},{1,2},{2,3},{3,4},{4,5},{5,6},{6,7},{7,0},{8,9},{9,10},{10,1... | collective-permute-start | bytes 786440 | tf_op jit(solution)/shard_map/ppermute | solution.py:327
  44.9 43.0 %collective-permute-start.1 = (bf16[512,256]{1,0:T(8,128)(2,1)}, bf16[512,256]{1,0:T(8,128)(2,1)S(1)}, u32[]{:S(2)}, u32[]{:S(2)}) collective-permute-start(bf16[512,256]{1,0:T(8,128)(2,1)} %get-tuple-element.24), channel_id=1, source_target_pairs={{0,2},{1,3},{2,4},{3,5},{4,6},{5,7},{6,0},{7,1},{8,10},{9,11},{10,... | collective-permute-start | bytes 786440 | tf_op jit(solution)/shard_map/ppermute | solution.py:327
  48.4 49.1 %collective-permute-start.2 = (bf16[512,256]{1,0:T(8,128)(2,1)}, bf16[512,256]{1,0:T(8,128)(2,1)S(1)}, u32[]{:S(2)}, u32[]{:S(2)}) collective-permute-start(bf16[512,256]{1,0:T(8,128)(2,1)} %get-tuple-element.25), channel_id=1, source_target_pairs={{0,3},{1,4},{2,5},{3,6},{4,7},{5,0},{6,1},{7,2},{8,11},{9,12},{10,... | collective-permute-start | bytes 786440 | tf_op jit(solution)/shard_map/ppermute | solution.py:327
  51.5 46.0 %collective-permute-start.3 = (bf16[512,256]{1,0:T(8,128)(2,1)}, bf16[512,256]{1,0:T(8,128)(2,1)S(1)}, u32[]{:S(2)}, u32[]{:S(2)}) collective-permute-start(bf16[512,256]{1,0:T(8,128)(2,1)} %get-tuple-element.26), channel_id=1, source_target_pairs={{0,4},{1,5},{2,6},{3,7},{4,0},{5,1},{6,2},{7,3},{8,12},{9,13},{10,... | collective-permute-start | bytes 786440 | tf_op jit(solution)/shard_map/ppermute | solution.py:327
  55.2 10.0 %collective-permute-start.14 = (bf16[80,256]{1,0:T(8,128)(2,1)S(1)}, bf16[80,256]{1,0:T(8,128)(2,1)S(1)}, u32[]{:S(2)}, u32[]{:S(2)}) collective-permute-start(bf16[80,256]{1,0:T(8,128)(2,1)S(1)} %dynamic-slice_bitcast_fusion.1), channel_id=1, source_target_pairs={{0,256},{256,0},{1,257},{257,1},{2,258},{258,2},{3,259},{259,3},{4... | collective-permute-start | bytes 122888 | tf_op jit(solution)/shard_map/ppermute | solution.py:345
  65.2 32.3 %collective-permute-start.4 = (bf16[512,256]{1,0:T(8,128)(2,1)}, bf16[512,256]{1,0:T(8,128)(2,1)S(1)}, u32[]{:S(2)}, u32[]{:S(2)}) collective-permute-start(bf16[512,256]{1,0:T(8,128)(2,1)} %get-tuple-element.27), channel_id=1, source_target_pairs={{0,5},{1,6},{2,7},{3,0},{4,1},{5,2},{6,3},{7,4},{8,13},{9,14},{10,... | collective-permute-start | bytes 786440 | tf_op jit(solution)/shard_map/ppermute | solution.py:327
  76.5 35.4 %all-to-all-start.2 = ((bf16[8,80,256]{2,1,0:T(8,128)(2,1)}), bf16[8,80,256]{2,1,0:T(8,128)(2,1)S(1)}, u32[]{:S(2)}, u32[]{:S(2)}) async-start(bf16[8,80,256]{2,1,0:T(8,128)(2,1)} %broadcast_in_dim.8), calls=%async_computation.2 | async-start | bytes 655360 | tf_op jit(solution)/shard_map/all_to_all | solution.py:340
  83.7 12.2 %copy-start.6 = (bf16[512,256]{1,0:T(8,128)(2,1)}, bf16[512,256]{1,0:T(8,128)(2,1)S(1)}, u32[]{:S(2)}) copy-start(bf16[512,256]{1,0:T(8,128)(2,1)S(1)} %collective-permute-done.refs_1_) | copy-start | bytes 786436
  83.7 13.9 %collective-permute-start.5 = (bf16[512,256]{1,0:T(8,128)(2,1)}, bf16[512,256]{1,0:T(8,128)(2,1)S(1)}, u32[]{:S(2)}, u32[]{:S(2)}) collective-permute-start(bf16[512,256]{1,0:T(8,128)(2,1)} %get-tuple-element.28), channel_id=1, source_target_pairs={{0,6},{1,7},{2,0},{3,1},{4,2},{5,3},{6,4},{7,5},{8,14},{9,15},{10,... | collective-permute-start | bytes 786440 | tf_op jit(solution)/shard_map/ppermute | solution.py:327
  87.9 8.1 %copy-start.7 = (bf16[512,256]{1,0:T(8,128)(2,1)}, bf16[512,256]{1,0:T(8,128)(2,1)S(1)}, u32[]{:S(2)}) copy-start(bf16[512,256]{1,0:T(8,128)(2,1)S(1)} %collective-permute-done.1.refs_2_) | copy-start | bytes 786436
  87.9 9.7 %collective-permute-start.6 = (bf16[512,256]{1,0:T(8,128)(2,1)}, bf16[512,256]{1,0:T(8,128)(2,1)S(1)}, u32[]{:S(2)}, u32[]{:S(2)}) collective-permute-start(bf16[512,256]{1,0:T(8,128)(2,1)} %get-tuple-element.29), channel_id=1, source_target_pairs={{0,7},{1,0},{2,1},{3,2},{4,3},{5,4},{6,5},{7,6},{8,15},{9,8},{10,9... | collective-permute-start | bytes 786440 | tf_op jit(solution)/shard_map/ppermute | solution.py:327
  97.5 0.7 copy-start.8
  97.5 0.8 copy-start.9
  97.6 0.9 copy-start.10
  97.6 1.0 copy-start.11
  97.6 1.0 copy-start.12
  111.9 4.7 %copy-start.15 = (s32[2]{0:T(128)S(1)}, s32[2]{0:T(128)}, u32[]{:S(2)}) copy-start(s32[2]{0:T(128)} %param.13) | copy-start | bytes 28
  111.9 25.3 %copy-start.16 = (bf16[512,256]{1,0:T(8,128)(2,1)S(1)}, bf16[512,256]{1,0:T(8,128)(2,1)}, u32[]{:S(2)}) copy-start(bf16[512,256]{1,0:T(8,128)(2,1)} %get-tuple-element.34) | copy-start | bytes 786436
  113.1 21.5 %all-to-all-start.3 = ((bf16[4,640,256]{2,1,0:T(8,128)(2,1)}), bf16[4,640,256]{2,1,0:T(8,128)(2,1)S(1)}, u32[]{:S(2)}, u32[]{:S(2)}) async-start(bf16[4,640,256]{2,1,0:T(8,128)(2,1)} %broadcast_in_dim.9), calls=%async_computation.3 | async-start | bytes 2621440 | tf_op jit(solution)/shard_map/all_to_all | solution.py:340
  134.6 9.2 %collective-permute-start.15 = (bf16[160,256]{1,0:T(8,128)(2,1)S(1)}, bf16[160,256]{1,0:T(8,128)(2,1)S(1)}, u32[]{:S(2)}, u32[]{:S(2)}) collective-permute-start(bf16[160,256]{1,0:T(8,128)(2,1)S(1)} %slice.21), channel_id=1, source_target_pairs={{0,1},{1,0},{2,3},{3,2},{4,5},{5,4},{6,7},{7,6},{8,9},{9,8},{10,11... | collective-permute-start | bytes 245768 | tf_op jit(solution)/shard_map/ppermute | solution.py:345
  137.2 25.2 %collective-permute-start.10 = (bf16[512,256]{1,0:T(8,128)(2,1)S(1)}, bf16[512,256]{1,0:T(8,128)(2,1)S(1)}, u32[]{:S(2)}, u32[]{:S(2)}) collective-permute-start(bf16[512,256]{1,0:T(8,128)(2,1)S(1)} %copy-done.16), channel_id=1, source_target_pairs={{0,4},{1,5},{2,6},{3,7},{4,0},{5,1},{6,2},{7,3},{8,12},{9,13},{10,... | collective-permute-start | bytes 786440 | tf_op jit(solution)/shard_map/ppermute | solution.py:327
  140.7 35.7 %collective-permute-start.11 = (bf16[512,256]{1,0:T(8,128)(2,1)}, bf16[512,256]{1,0:T(8,128)(2,1)S(1)}, u32[]{:S(2)}, u32[]{:S(2)}) collective-permute-start(bf16[512,256]{1,0:T(8,128)(2,1)} %get-tuple-element.35), channel_id=1, source_target_pairs={{0,5},{1,6},{2,7},{3,0},{4,1},{5,2},{6,3},{7,4},{8,13},{9,14},{10,... | collective-permute-start | bytes 786440 | tf_op jit(solution)/shard_map/ppermute | solution.py:327
  144.8 44.6 %all-to-all-start.4 = ((bf16[4,320,256]{2,1,0:T(8,128)(2,1)}), bf16[4,320,256]{2,1,0:T(8,128)(2,1)S(1)}, u32[]{:S(2)}, u32[]{:S(2)}) async-start(bf16[4,320,256]{2,1,0:T(8,128)(2,1)} %broadcast_in_dim.10), calls=%async_computation.4 | async-start | bytes 1310720 | tf_op jit(solution)/shard_map/all_to_all | solution.py:340
  149.7 4.9 %copy-start.13 = (s32[64,40]{0,1:T(8,128)S(1)}, s32[64,40]{0,1:T(8,128)}, u32[]{:S(2)}) copy-start(s32[64,40]{0,1:T(8,128)} %param.11) | copy-start | bytes 30724
  154.8 32.9 %copy-start.14 = (s32[40]{0:T(128)}, s32[40]{0:T(128)S(1)}, u32[]{:S(2)}) copy-start(s32[40]{0:T(128)S(1)} %get-tuple-element.43.lengths) | copy-start | bytes 484
  155.6 39.4 %collective-permute-start.12 = (bf16[512,256]{1,0:T(8,128)(2,1)}, bf16[512,256]{1,0:T(8,128)(2,1)S(1)}, u32[]{:S(2)}, u32[]{:S(2)}) collective-permute-start(bf16[512,256]{1,0:T(8,128)(2,1)} %get-tuple-element.36), channel_id=1, source_target_pairs={{0,6},{1,7},{2,0},{3,1},{4,2},{5,3},{6,4},{7,5},{8,14},{9,15},{10,... | collective-permute-start | bytes 786440 | tf_op jit(solution)/shard_map/ppermute | solution.py:327
  158.1 42.3 %collective-permute-start.13 = (bf16[512,256]{1,0:T(8,128)(2,1)}, bf16[512,256]{1,0:T(8,128)(2,1)S(1)}, u32[]{:S(2)}, u32[]{:S(2)}) collective-permute-start(bf16[512,256]{1,0:T(8,128)(2,1)} %get-tuple-element.37), channel_id=1, source_target_pairs={{0,7},{1,0},{2,1},{3,2},{4,3},{5,4},{6,5},{7,6},{8,15},{9,8},{10,9... | collective-permute-start | bytes 786440 | tf_op jit(solution)/shard_map/ppermute | solution.py:327
  160.0 40.4 %collective-permute-start.7 = (bf16[512,256]{1,0:T(8,128)(2,1)}, bf16[512,256]{1,0:T(8,128)(2,1)S(1)}, u32[]{:S(2)}, u32[]{:S(2)}) collective-permute-start(bf16[512,256]{1,0:T(8,128)(2,1)} %get-tuple-element.31), channel_id=1, source_target_pairs={{0,1},{1,2},{2,3},{3,4},{4,5},{5,6},{6,7},{7,0},{8,9},{9,10},{10,1... | collective-permute-start | bytes 786440 | tf_op jit(solution)/shard_map/ppermute | solution.py:327
  162.4 25.4 %copy-start = (bf16[512,256]{1,0:T(8,128)(2,1)}, bf16[512,256]{1,0:T(8,128)(2,1)S(1)}, u32[]{:S(2)}) copy-start(bf16[512,256]{1,0:T(8,128)(2,1)S(1)} %collective-permute-done.10.refs_4_) | copy-start | bytes 786436
  162.4 37.9 %collective-permute-start.8 = (bf16[512,256]{1,0:T(8,128)(2,1)}, bf16[512,256]{1,0:T(8,128)(2,1)S(1)}, u32[]{:S(2)}, u32[]{:S(2)}) collective-permute-start(bf16[512,256]{1,0:T(8,128)(2,1)} %get-tuple-element.32), channel_id=1, source_target_pairs={{0,2},{1,3},{2,4},{3,5},{4,6},{5,7},{6,0},{7,1},{8,10},{9,11},{10,... | collective-permute-start | bytes 786440 | tf_op jit(solution)/shard_map/ppermute | solution.py:327
  176.4 11.4 %copy-start.1 = (bf16[512,256]{1,0:T(8,128)(2,1)}, bf16[512,256]{1,0:T(8,128)(2,1)S(1)}, u32[]{:S(2)}) copy-start(bf16[512,256]{1,0:T(8,128)(2,1)S(1)} %collective-permute-done.11.refs_5_) | copy-start | bytes 786436
  176.4 24.0 %collective-permute-start.9 = (bf16[512,256]{1,0:T(8,128)(2,1)}, bf16[512,256]{1,0:T(8,128)(2,1)}, u32[]{:S(2)}, u32[]{:S(2)}) collective-permute-start(bf16[512,256]{1,0:T(8,128)(2,1)} %get-tuple-element.33), channel_id=1, source_target_pairs={{0,3},{1,4},{2,5},{3,6},{4,7},{5,0},{6,1},{7,2},{8,11},{9,12},{10,... | collective-permute-start | bytes 786440 | tf_op jit(solution)/shard_map/ppermute | solution.py:327
  195.0 5.4 %copy-start.2 = (bf16[512,256]{1,0:T(8,128)(2,1)}, bf16[512,256]{1,0:T(8,128)(2,1)S(1)}, u32[]{:S(2)}) copy-start(bf16[512,256]{1,0:T(8,128)(2,1)S(1)} %collective-permute-done.12.refs_6_) | copy-start | bytes 786436
  200.4 0.7 copy-start.3
  200.4 0.8 copy-start.4
  200.4 0.9 copy-start.5

commit v6 on v5

--- a/solution.py
+++ b/solution.py
@@ -72,6 +72,8 @@
 
 def twist(value, cosine, sine, s):
     real, imag = value
+    if sine is None:
+        return (real * cosine, imag * cosine)
     if s > 0:
         return (real * cosine - imag * sine, imag * cosine + real * sine)
     return (real * cosine + imag * sine, imag * cosine - real * sine)
@@ -99,8 +101,8 @@
                 here = pl.ds(a * base + lane, 128)
                 parts.append((field[0, at, here].astype(f32), field[1, at, here].astype(f32)))
             for k, value in enumerate(fft8(parts, -1)):
-                cosine = turn[2 * k : 2 * k + 1, lane : lane + 128]
-                sine = turn[2 * k + 1 : 2 * k + 2, lane : lane + 128]
+                cosine = turn[2 * k : 2 * k + 1, lane : lane + 128] if k else RADIX**-0.5
+                sine = turn[2 * k + 1 : 2 * k + 2, lane : lane + 128] if k else None
                 real, imag = twist(value, cosine, sine, -1)
                 mid[k, at, pl.ds(lane, 128)] = real.astype(bf16)
                 mid[k, at, pl.ds(base + lane, 128)] = imag.astype(bf16)
@@ -134,8 +136,8 @@
                     )
                 )
             for k, value in enumerate(fft8(parts, 1)):
-                cosine = turn[pl.ds(at, 16), 2 * k : 2 * k + 1]
-                sine = turn[pl.ds(at, 16), 2 * k + 1 : 2 * k + 2]
+                cosine = turn[pl.ds(at, 16), 2 * k : 2 * k + 1] if k else RADIX**-0.5
+                sine = turn[pl.ds(at, 16), 2 * k + 1 : 2 * k + 2] if k else None
                 real, imag = twist(value, cosine, sine, -1)
                 mid[k, pl.ds(at, 16), here] = real.astype(bf16)
                 mid[k, pl.ds(base + at, 16), here] = (-imag).astype(bf16)
@@ -163,8 +165,8 @@
             here = pl.ds(lane, 128)
             parts = []
             for k in range(RADIX):
-                cosine = turn[pl.ds(at, 16), 2 * k : 2 * k + 1]
-                sine = turn[pl.ds(at, 16), 2 * k + 1 : 2 * k + 2]
+                cosine = turn[pl.ds(at, 16), 2 * k : 2 * k + 1] if k else RADIX**-0.5
+                sine = turn[pl.ds(at, 16), 2 * k + 1 : 2 * k + 2] if k else None
                 value = (back[k, pl.ds(at, 16), here], back[k, pl.ds(base + at, 16), here])
                 parts.append(twist(value, cosine, sine, 1))
             for out, (real, imag) in zip(outs, fft8(parts, 1)):
@@ -204,8 +206,8 @@
             here = pl.ds(lane, 128)
             parts = []
             for k in range(RADIX):
-                cosine = turn[pl.ds(at, 16), 2 * k : 2 * k + 1]
-                sine = turn[pl.ds(at, 16), 2 * k + 1 : 2 * k + 2]
+                cosine = turn[pl.ds(at, 16), 2 * k : 2 * k + 1] if k else RADIX**-0.5
+                sine = turn[pl.ds(at, 16), 2 * k + 1 : 2 * k + 2] if k else None
                 value = (back[k, pl.ds(at, 16), here], back[k, pl.ds(base + at, 16), here])
                 parts.append(twist(value, cosine, sine, 1))
             for a, (real, imag) in enumerate(fft8(parts, 1)):
@@ -423,13 +425,16 @@
 
     share, _ = lax.optimization_barrier((share, restored[0]))
     joined = join(share, "x")
-    mine = joined[extent_y:filled]
-    other = swap(mine, "core", 1)
+    operators = join(joined[extent_y:filled], "yl")
+    other = swap(operators, "core", 1)
     first = lax.axis_index("core") == 0
-    operators = jnp.concatenate(
-        [jnp.where(first, mine, other), jnp.where(first, other, mine)], axis=0
-    )
-    operators = join(operators, "yl")
+    operators = jnp.stack(
+        [
+            value.reshape(lax.axis_size("yl"), -1, row_count)
+            for value in (jnp.where(first, operators, other), jnp.where(first, other, operators))
+        ],
+        axis=1,
+    )
     shape = block_inverse.shape
     matrices = operators.reshape((cut_count,) + shape[1:])
     matrices = jnp.pad(matrices, ((0, 0),) * 4 + ((0, -shape[4] % 128),))

time: 259 us -> 254 us (0.981)
  the two profiles are of different devices: /device:TPU:16 before, /device:TPU:8 now
where the time goes in v6:
time: 254 us; the launch traced here: 253 us
  starting transfers between devices  87.8 us (35%)
  waiting for transfers between devices  57.9 us (23%)
  blocking collectives  39.8 us (16%)
  Pallas kernels  35.5 us (14%)
  other arithmetic  18.8 us (7%)
  local copies, waits for them, and re-layouts  11.9 us (5%)
    ppermute x14, starting transfers between devices, rotate(): lax.ppermute(values[d], axes, [(i, (i + d) % size) for i in range(size)])  49.8 us
    all_to_all x2, blocking collectives, sum_over(): terms = lax.all_to_all(part, axis, 0, 0, tiled=True)  39.8 us
    pallas_call x3, Pallas kernels, call(): pl.pallas_call(kernel, out_shape=out_shape, in_specs=[smem] * scalars + [...  35.5 us
    ppermute x14, waiting for transfers between devices, rotate(): lax.ppermute(values[d], axes, [(i, (i + d) % size) for i in range(size)])  20.7 us
    all_to_all x2, waiting for transfers between devices, split(): shaped = lax.all_to_all(shaped, axis, 0, 0)  17.2 us
    all_to_all x3, waiting for transfers between devices, join(): copies = lax.all_to_all(copies, axis, 0, 0)  15.7 us
    all_to_all x3, starting transfers between devices, join(): copies = lax.all_to_all(copies, axis, 0, 0)  15.4 us
    all_to_all x2, starting transfers between devices, split(): shaped = lax.all_to_all(shaped, axis, 0, 0)  14.6 us
  transfers between devices with their start and end apart: 21, of which 7 were waited for; matrix products, arithmetic and copies ran while one was open for 9% of the time, Pallas kernels for 7%

profile of v6, /device:TPU:8, one launch (start us, length us, event | category | flops | bytes accessed | tf_op | source)
XLA Modules:
  0.0 252.9 jit_solution(8330035871095514029)
XLA Ops:
  0.0 1.1 reshape_squeeze.3
  1.2 1.3 pad_maximum_fusion
  2.5 0.7 copy.17
  3.3 1.2 pad.8.clone
  4.4 4.3 %all-to-all-start = ((bf16[4,640,256]{2,1,0:T(8,128)(2,1)}), bf16[4,640,256]{2,1,0:T(8,128)(2,1)S(1)}, u32[]{:S(2)}, u32[]{:S(2)}) async-start(bf16[4,640,256]{2,1,0:T(8,128)(2,1)} %bitcast.7), calls=%async_computation | async-start | bytes 2621440 | tf_op jit(solution)/shard_map/all_to_all | solution.py:336
  9.4 17.2 %all-to-all-done = bf16[4,640,256]{2,1,0:T(8,128)(2,1)S(1)} async-done(((bf16[4,640,256]{2,1,0:T(8,128)(2,1)}), bf16[4,640,256]{2,1,0:T(8,128)(2,1)S(1)}, u32[]{:S(2)}, u32[]{:S(2)}) %all-to-all-start) | async-done | bytes 1310752 | tf_op jit(solution)/shard_map/all_to_all | solution.py:336
  26.6 0.7 constant_dynamic-slice_fusion
  27.4 10.3 %all-to-all-start.1 = ((bf16[8,80,256]{2,1,0:T(8,128)(2,1)}), bf16[8,80,256]{2,1,0:T(8,128)(2,1)S(1)}, u32[]{:S(2)}, u32[]{:S(2)}) async-start(bf16[8,80,256]{2,1,0:T(8,128)(2,1)} %bitcast.8), calls=%async_computation.1 | async-start | bytes 655360 | tf_op jit(solution)/shard_map/all_to_all | solution.py:336
  37.7 5.2 %shard_map.82 = (bf16[512,256]{1,0:T(8,128)(2,1)}, bf16[512,256]{1,0:T(8,128)(2,1)}, bf16[512,256]{1,0:T(8,128)(2,1)}, bf16[512,256]{1,0:T(8,128)(2,1)}, bf16[51...) custom-call(s32[1]{0:T(128)} %bitcast.me, ...), custom_call_target="tpu_custom_call" | custom-call | tf_op jit(solution)/shard_map/pallas_call | solution.py:272
  42.9 1.9 collective-permute-start
  44.8 3.5 %collective-permute-start.1 = (bf16[512,256]{1,0:T(8,128)(2,1)}, bf16[512,256]{1,0:T(8,128)(2,1)S(1)}, u32[]{:S(2)}, u32[]{:S(2)}) collective-permute-start(bf16[512,256]{1,0:T(8,128)(2,1)} %get-tuple-element.24), channel_id=1, source_target_pairs={{0,2},{1,3},{2,4},{3,5},{4,6},{5,7},{6,0},{7,1},{8,10},{9,11},{10,... | collective-permute-start | bytes 786440 | tf_op jit(solution)/shard_map/ppermute | solution.py:329
  48.3 3.2 %collective-permute-start.2 = (bf16[512,256]{1,0:T(8,128)(2,1)}, bf16[512,256]{1,0:T(8,128)(2,1)S(1)}, u32[]{:S(2)}, u32[]{:S(2)}) collective-permute-start(bf16[512,256]{1,0:T(8,128)(2,1)} %get-tuple-element.25), channel_id=1, source_target_pairs={{0,3},{1,4},{2,5},{3,6},{4,7},{5,0},{6,1},{7,2},{8,11},{9,12},{10,... | collective-permute-start | bytes 786440 | tf_op jit(solution)/shard_map/ppermute | solution.py:329
  51.5 4.4 %collective-permute-start.3 = (bf16[512,256]{1,0:T(8,128)(2,1)}, bf16[512,256]{1,0:T(8,128)(2,1)S(1)}, u32[]{:S(2)}, u32[]{:S(2)}) collective-permute-start(bf16[512,256]{1,0:T(8,128)(2,1)} %get-tuple-element.26), channel_id=1, source_target_pairs={{0,4},{1,5},{2,6},{3,7},{4,0},{5,1},{6,2},{7,3},{8,12},{9,13},{10,... | collective-permute-start | bytes 786440 | tf_op jit(solution)/shard_map/ppermute | solution.py:329
  56.0 5.9 %collective-permute-start.14 = (bf16[80,256]{1,0:T(8,128)(2,1)S(1)}, bf16[80,256]{1,0:T(8,128)(2,1)S(1)}, u32[]{:S(2)}, u32[]{:S(2)}) collective-permute-start(bf16[80,256]{1,0:T(8,128)(2,1)S(1)} %dynamic-slice_bitcast_fusion.1), channel_id=1, source_target_pairs={{0,256},{256,0},{1,257},{257,1},{2,258},{258,2},{3,259},{259,3},{4... | collective-permute-start | bytes 122888 | tf_op jit(solution)/shard_map/ppermute | solution.py:347
  62.0 4.3 %collective-permute-done.14 = bf16[80,256]{1,0:T(8,128)(2,1)S(1)} collective-permute-done((bf16[80,256]{1,0:T(8,128)(2,1)S(1)}, bf16[80,256]{1,0:T(8,128)(2,1)S(1)}, u32[]{:S(2)}, u32[]{:S(2)}) %collective-permute-start.14) | collective-permute-done | bytes 40992 | tf_op jit(solution)/shard_map/ppermute | solution.py:347
  66.3 11.1 %collective-permute-start.4 = (bf16[512,256]{1,0:T(8,128)(2,1)}, bf16[512,256]{1,0:T(8,128)(2,1)S(1)}, u32[]{:S(2)}, u32[]{:S(2)}) collective-permute-start(bf16[512,256]{1,0:T(8,128)(2,1)} %get-tuple-element.27), channel_id=1, source_target_pairs={{0,5},{1,6},{2,7},{3,0},{4,1},{5,2},{6,3},{7,4},{8,13},{9,14},{10,... | collective-permute-start | bytes 786440 | tf_op jit(solution)/shard_map/ppermute | solution.py:329
  77.4 0.8 broadcast_in_dim.8
  78.2 7.2 %all-to-all-start.2 = ((bf16[8,80,256]{2,1,0:T(8,128)(2,1)}), bf16[8,80,256]{2,1,0:T(8,128)(2,1)S(1)}, u32[]{:S(2)}, u32[]{:S(2)}) async-start(bf16[8,80,256]{2,1,0:T(8,128)(2,1)} %broadcast_in_dim.8), calls=%async_computation.2 | async-start | bytes 655360 | tf_op jit(solution)/shard_map/all_to_all | solution.py:342
  85.4 1.9 collective-permute-start.5
  87.3 3.1 %collective-permute-start.6 = (bf16[512,256]{1,0:T(8,128)(2,1)}, bf16[512,256]{1,0:T(8,128)(2,1)S(1)}, u32[]{:S(2)}, u32[]{:S(2)}) collective-permute-start(bf16[512,256]{1,0:T(8,128)(2,1)} %get-tuple-element.29), channel_id=1, source_target_pairs={{0,7},{1,0},{2,1},{3,2},{4,3},{5,4},{6,5},{7,6},{8,15},{9,8},{10,9... | collective-permute-start | bytes 786440 | tf_op jit(solution)/shard_map/ppermute | solution.py:329
  90.4 5.2 %fusion = (f32[8,256,256]{2,1,0:T(8,128)}, f32[8,256,256]{2,1,0:T(8,128)}) fusion(f32[256]{0:T(256)S(1)} %fusion.34, f32[8,256]{1,0:T(8,128)S(1)} %fusion.31), kind=kLoop, calls=%fused_computation.11 | loop fusion | flops 24641536 | bytes 4203520 | tf_op jit(solution)/shard_map/jit(_where)/select_n | solution.py:321
  95.7 1.6 dynamic-slice_bitcast_fusion.refs_9_
  98.3 13.1 %shard_map.83 = (bf16[512,256]{1,0:T(8,128)(2,1)}, bf16[512,256]{1,0:T(8,128)(2,1)}, bf16[512,256]{1,0:T(8,128)(2,1)}, bf16[512,256]{1,0:T(8,128)(2,1)}, bf16[51...) custom-call(bf16[512,256]{1,0:T(8,128)(2,1)} %get-tuple-element.22.refs_0_, ...), custom_call_target="tpu_custom_call" | custom-call | tf_op jit(solution)/shard_map/pallas_call | solution.py:272
  111.4 1.2 broadcast_in_dim.9
  112.6 3.5 %all-to-all-start.3 = ((bf16[4,640,256]{2,1,0:T(8,128)(2,1)}), bf16[4,640,256]{2,1,0:T(8,128)(2,1)S(1)}, u32[]{:S(2)}, u32[]{:S(2)}) async-start(bf16[4,640,256]{2,1,0:T(8,128)(2,1)} %broadcast_in_dim.9), calls=%async_computation.3 | async-start | bytes 2621440 | tf_op jit(solution)/shard_map/all_to_all | solution.py:342
  117.6 0.6 multiply_multiply_fusion.4
  118.9 15.7 %all-to-all-done.3 = bf16[4,640,256]{2,1,0:T(8,128)(2,1)S(1)} async-done(((bf16[4,640,256]{2,1,0:T(8,128)(2,1)}), bf16[4,640,256]{2,1,0:T(8,128)(2,1)S(1)}, u32[]{:S(2)}, u32[]{:S(2)}) %all-to-all-start.3) | async-done | bytes 1310752 | tf_op jit(solution)/shard_map/all_to_all | solution.py:342
  134.6 0.8 broadcast_in_dim.10
  135.3 4.7 %all-to-all-start.4 = ((bf16[4,160,256]{2,1,0:T(8,128)(2,1)}), bf16[4,160,256]{2,1,0:T(8,128)(2,1)S(1)}, u32[]{:S(2)}, u32[]{:S(2)}) async-start(bf16[4,160,256]{2,1,0:T(8,128)(2,1)} %broadcast_in_dim.10), calls=%async_computation.4 | async-start | bytes 655360 | tf_op jit(solution)/shard_map/all_to_all | solution.py:342
  140.0 5.0 %fusion.24 = (f32[2048,256]{1,0:T(8,128)}, f32[2048,256]{1,0:T(8,128)}) fusion(f32[2048]{0:T(1024)S(1)} %multiply_multiply_fusion.3, f32[256]{0:T(256)S(1)} %multiply_multiply_fusion.4, f32[]{:T(128)S(6)} %mul.300), kind=kLoop, calls=%fused_computation.35 | loop fusion | flops 23068672 | bytes 4203524 | tf_op jit(solution)/shard_map/mul | solution.py:404
  144.9 4.3 %collective-permute-start.10 = (bf16[512,256]{1,0:T(8,128)(2,1)S(1)}, bf16[512,256]{1,0:T(8,128)(2,1)S(1)}, u32[]{:S(2)}, u32[]{:S(2)}) collective-permute-start(bf16[512,256]{1,0:T(8,128)(2,1)S(1)} %copy-done.17), channel_id=1, source_target_pairs={{0,4},{1,5},{2,6},{3,7},{4,0},{5,1},{6,2},{7,3},{8,12},{9,13},{10,... | collective-permute-start | bytes 786440 | tf_op jit(solution)/shard_map/ppermute | solution.py:329
  149.2 1.9 collective-permute-start.11
  151.1 2.5 collective-permute-start.12
  153.6 3.1 %collective-permute-start.13 = (bf16[512,256]{1,0:T(8,128)(2,1)}, bf16[512,256]{1,0:T(8,128)(2,1)S(1)}, u32[]{:S(2)}, u32[]{:S(2)}) collective-permute-start(bf16[512,256]{1,0:T(8,128)(2,1)} %get-tuple-element.37), channel_id=1, source_target_pairs={{0,7},{1,0},{2,1},{3,2},{4,3},{5,4},{6,5},{7,6},{8,15},{9,8},{10,9... | collective-permute-start | bytes 786440 | tf_op jit(solution)/shard_map/ppermute | solution.py:329
  156.7 2.0 collective-permute-start.15
  158.8 4.3 %negate_select_fusion.2 = (f32[2048,256]{1,0:T(8,128)}, f32[2048,256]{1,0:T(8,128)}) fusion(f32[]{:T(128)S(6)} %mul.283, bf16[2560,256]{1,0:T(8,128)(2,1)S(1)} %bitcast.40), kind=kLoop, calls=%fused_computation.3 | loop fusion | flops 22020096 | bytes 5242884 | tf_op jit(solution)/shard_map/jit(_where)/select_n | solution.py:300
  163.1 11.3 %collective-permute-done.10.refs_4_ = bf16[512,256]{1,0:T(8,128)(2,1)S(1)} collective-permute-done((bf16[512,256]{1,0:T(8,128)(2,1)S(1)}, bf16[512,256]{1,0:T(8,128)(2,1)S(1)}, u32[]{:S(2)}, u32[]{:S(2)}) %collective-permute-start.10) | collective-permute-done | bytes 262176 | tf_op jit(solution)/shard_map/ppermute | solution.py:329
  174.4 1.9 collective-permute-start.7
  176.3 1.2 collective-permute-done.11.refs_5_
  177.5 1.9 collective-permute-start.8
  179.4 5.2 %collective-permute-start.9 = (bf16[512,256]{1,0:T(8,128)(2,1)}, bf16[512,256]{1,0:T(8,128)(2,1)}, u32[]{:S(2)}, u32[]{:S(2)}) collective-permute-start(bf16[512,256]{1,0:T(8,128)(2,1)} %get-tuple-element.33), channel_id=1, source_target_pairs={{0,3},{1,4},{2,5},{3,6},{4,7},{5,0},{6,1},{7,2},{8,11},{9,12},{10,... | collective-permute-start | bytes 786440 | tf_op jit(solution)/shard_map/ppermute | solution.py:329
  185.3 1.5 pad.9.refs_12_
  186.9 1.9 collective-permute-done.8.refs_2_
  188.8 6.2 %collective-permute-done.9.refs_3_ = bf16[512,256]{1,0:T(8,128)(2,1)} collective-permute-done((bf16[512,256]{1,0:T(8,128)(2,1)}, bf16[512,256]{1,0:T(8,128)(2,1)}, u32[]{:S(2)}, u32[]{:S(2)}) %collective-permute-start.9) | collective-permute-done | bytes 262176 | tf_op jit(solution)/shard_map/ppermute | solution.py:329
  195.0 17.2 %shard_map.84 = bf16[4,2,8,32,256]{4,3,2,1,0:T(8,128)(2,1)} custom-call(s32[1]{0:T(128)} %bitcast.me, s32[40]{0:T(128)} %sub.122.starts, s32[40]{0:T(128)} %copy-done.14, bf16[512,256]{1,0:T(8,128)(2,1)} %get-tuple-element.30.refs_0_, bf16[512,256]{1,0:T(8,128)(2,1)} %copy-done.4, bf16[512,256]{1,0:T(8,128)(2,1)} %copy-done.5, ...), custom_call_target="tpu_custom_call" | custom-call | tf_op jit(solution)/shard_map/pallas_call | solution.py:272
  212.3 19.0 %all_to_all.35 = bf16[4,2,8,32,256]{4,3,2,1,0:T(8,128)(2,1)S(1)} all-to-all(bf16[4,2,8,32,256]{4,3,2,1,0:T(8,128)(2,1)} %shard_map.84), channel_id=1, replica_groups=mesh['yh'=2,'x'=4,'z'=8,'yl'=4,'core'=2] {'x'}, dimensions={0} | all-to-all | bytes 2097152 | tf_op jit(solution)/shard_map/all_to_all | solution.py:362
  231.4 20.8 %all_to_all.36 = bf16[16,32,256]{2,1,0:T(8,128)(2,1)S(1)} all-to-all(bf16[16,32,256]{2,1,0:T(8,128)(2,1)S(1)} %bitcast.46), channel_id=1, replica_groups=mesh['yh'=2,'x'=4,'z'=8,'yl'=4,'core'=2] {'yh','z'}, dimensions={0} | all-to-all | bytes 524288 | tf_op jit(solution)/shard_map/all_to_all | solution.py:362
  252.3 0.7 convert_reduce_fusion
  (67 shorter events, 4.1 us)
Async XLA Ops:
  4.4 22.2 %all-to-all-start = ((bf16[4,640,256]{2,1,0:T(8,128)(2,1)}), bf16[4,640,256]{2,1,0:T(8,128)(2,1)S(1)}, u32[]{:S(2)}, u32[]{:S(2)}) async-start(bf16[4,640,256]{2,1,0:T(8,128)(2,1)} %bitcast.7), calls=%async_computation | async-start | bytes 2621440 | tf_op jit(solution)/shard_map/all_to_all | solution.py:336
  27.4 28.6 %all-to-all-start.1 = ((bf16[8,80,256]{2,1,0:T(8,128)(2,1)}), bf16[8,80,256]{2,1,0:T(8,128)(2,1)S(1)}, u32[]{:S(2)}, u32[]{:S(2)}) async-start(bf16[8,80,256]{2,1,0:T(8,128)(2,1)} %bitcast.8), calls=%async_computation.1 | async-start | bytes 655360 | tf_op jit(solution)/shard_map/all_to_all | solution.py:336
  42.9 42.5 %collective-permute-start = (bf16[512,256]{1,0:T(8,128)(2,1)}, bf16[512,256]{1,0:T(8,128)(2,1)S(1)}, u32[]{:S(2)}, u32[]{:S(2)}) collective-permute-start(bf16[512,256]{1,0:T(8,128)(2,1)} %get-tuple-element.23), channel_id=1, source_target_pairs={{0,1},{1,2},{2,3},{3,4},{4,5},{5,6},{6,7},{7,0},{8,9},{9,10},{10,1... | collective-permute-start | bytes 786440 | tf_op jit(solution)/shard_map/ppermute | solution.py:329
  44.8 42.6 %collective-permute-start.1 = (bf16[512,256]{1,0:T(8,128)(2,1)}, bf16[512,256]{1,0:T(8,128)(2,1)S(1)}, u32[]{:S(2)}, u32[]{:S(2)}) collective-permute-start(bf16[512,256]{1,0:T(8,128)(2,1)} %get-tuple-element.24), channel_id=1, source_target_pairs={{0,2},{1,3},{2,4},{3,5},{4,6},{5,7},{6,0},{7,1},{8,10},{9,11},{10,... | collective-permute-start | bytes 786440 | tf_op jit(solution)/shard_map/ppermute | solution.py:329
  48.3 49.0 %collective-permute-start.2 = (bf16[512,256]{1,0:T(8,128)(2,1)}, bf16[512,256]{1,0:T(8,128)(2,1)S(1)}, u32[]{:S(2)}, u32[]{:S(2)}) collective-permute-start(bf16[512,256]{1,0:T(8,128)(2,1)} %get-tuple-element.25), channel_id=1, source_target_pairs={{0,3},{1,4},{2,5},{3,6},{4,7},{5,0},{6,1},{7,2},{8,11},{9,12},{10,... | collective-permute-start | bytes 786440 | tf_op jit(solution)/shard_map/ppermute | solution.py:329
  51.5 45.7 %collective-permute-start.3 = (bf16[512,256]{1,0:T(8,128)(2,1)}, bf16[512,256]{1,0:T(8,128)(2,1)S(1)}, u32[]{:S(2)}, u32[]{:S(2)}) collective-permute-start(bf16[512,256]{1,0:T(8,128)(2,1)} %get-tuple-element.26), channel_id=1, source_target_pairs={{0,4},{1,5},{2,6},{3,7},{4,0},{5,1},{6,2},{7,3},{8,12},{9,13},{10,... | collective-permute-start | bytes 786440 | tf_op jit(solution)/shard_map/ppermute | solution.py:329
  56.0 10.3 %collective-permute-start.14 = (bf16[80,256]{1,0:T(8,128)(2,1)S(1)}, bf16[80,256]{1,0:T(8,128)(2,1)S(1)}, u32[]{:S(2)}, u32[]{:S(2)}) collective-permute-start(bf16[80,256]{1,0:T(8,128)(2,1)S(1)} %dynamic-slice_bitcast_fusion.1), channel_id=1, source_target_pairs={{0,256},{256,0},{1,257},{257,1},{2,258},{258,2},{3,259},{259,3},{4... | collective-permute-start | bytes 122888 | tf_op jit(solution)/shard_map/ppermute | solution.py:347
  66.3 30.9 %collective-permute-start.4 = (bf16[512,256]{1,0:T(8,128)(2,1)}, bf16[512,256]{1,0:T(8,128)(2,1)S(1)}, u32[]{:S(2)}, u32[]{:S(2)}) collective-permute-start(bf16[512,256]{1,0:T(8,128)(2,1)} %get-tuple-element.27), channel_id=1, source_target_pairs={{0,5},{1,6},{2,7},{3,0},{4,1},{5,2},{6,3},{7,4},{8,13},{9,14},{10,... | collective-permute-start | bytes 786440 | tf_op jit(solution)/shard_map/ppermute | solution.py:329
  78.2 33.2 %all-to-all-start.2 = ((bf16[8,80,256]{2,1,0:T(8,128)(2,1)}), bf16[8,80,256]{2,1,0:T(8,128)(2,1)S(1)}, u32[]{:S(2)}, u32[]{:S(2)}) async-start(bf16[8,80,256]{2,1,0:T(8,128)(2,1)} %broadcast_in_dim.8), calls=%async_computation.2 | async-start | bytes 655360 | tf_op jit(solution)/shard_map/all_to_all | solution.py:342
  85.4 10.3 %copy-start.6 = (bf16[512,256]{1,0:T(8,128)(2,1)}, bf16[512,256]{1,0:T(8,128)(2,1)S(1)}, u32[]{:S(2)}) copy-start(bf16[512,256]{1,0:T(8,128)(2,1)S(1)} %collective-permute-done.refs_1_) | copy-start | bytes 786436
  85.4 11.9 %collective-permute-start.5 = (bf16[512,256]{1,0:T(8,128)(2,1)}, bf16[512,256]{1,0:T(8,128)(2,1)S(1)}, u32[]{:S(2)}, u32[]{:S(2)}) collective-permute-start(bf16[512,256]{1,0:T(8,128)(2,1)} %get-tuple-element.28), channel_id=1, source_target_pairs={{0,6},{1,7},{2,0},{3,1},{4,2},{5,3},{6,4},{7,5},{8,14},{9,15},{10,... | collective-permute-start | bytes 786440 | tf_op jit(solution)/shard_map/ppermute | solution.py:329
  87.3 8.3 %copy-start.7 = (bf16[512,256]{1,0:T(8,128)(2,1)}, bf16[512,256]{1,0:T(8,128)(2,1)S(1)}, u32[]{:S(2)}) copy-start(bf16[512,256]{1,0:T(8,128)(2,1)S(1)} %collective-permute-done.1.refs_2_) | copy-start | bytes 786436
  87.3 9.9 %collective-permute-start.6 = (bf16[512,256]{1,0:T(8,128)(2,1)}, bf16[512,256]{1,0:T(8,128)(2,1)S(1)}, u32[]{:S(2)}, u32[]{:S(2)}) collective-permute-start(bf16[512,256]{1,0:T(8,128)(2,1)} %get-tuple-element.29), channel_id=1, source_target_pairs={{0,7},{1,0},{2,1},{3,2},{4,3},{5,4},{6,5},{7,6},{8,15},{9,8},{10,9... | collective-permute-start | bytes 786440 | tf_op jit(solution)/shard_map/ppermute | solution.py:329
  97.2 0.7 copy-start.8
  97.2 0.8 copy-start.9
  97.2 0.9 copy-start.10
  97.3 0.9 copy-start.11
  97.3 1.0 copy-start.12
  111.4 4.7 %copy-start.13 = (s32[64,40]{0,1:T(8,128)S(1)}, s32[64,40]{0,1:T(8,128)}, u32[]{:S(2)}) copy-start(s32[64,40]{0,1:T(8,128)} %param.11) | copy-start | bytes 30724
  111.4 5.7 %copy-start.15 = (s32[2]{0:T(128)S(1)}, s32[2]{0:T(128)}, u32[]{:S(2)}) copy-start(s32[2]{0:T(128)} %param.13) | copy-start | bytes 28
  112.6 22.0 %all-to-all-start.3 = ((bf16[4,640,256]{2,1,0:T(8,128)(2,1)}), bf16[4,640,256]{2,1,0:T(8,128)(2,1)S(1)}, u32[]{:S(2)}, u32[]{:S(2)}) async-start(bf16[4,640,256]{2,1,0:T(8,128)(2,1)} %broadcast_in_dim.9), calls=%async_computation.3 | async-start | bytes 2621440 | tf_op jit(solution)/shard_map/all_to_all | solution.py:342
  116.3 28.6 %copy-start.14 = (s32[40]{0:T(128)}, s32[40]{0:T(128)S(1)}, u32[]{:S(2)}) copy-start(s32[40]{0:T(128)S(1)} %get-tuple-element.43.lengths) | copy-start | bytes 484
  135.3 21.4 %all-to-all-start.4 = ((bf16[4,160,256]{2,1,0:T(8,128)(2,1)}), bf16[4,160,256]{2,1,0:T(8,128)(2,1)S(1)}, u32[]{:S(2)}, u32[]{:S(2)}) async-start(bf16[4,160,256]{2,1,0:T(8,128)(2,1)} %broadcast_in_dim.10), calls=%async_computation.4 | async-start | bytes 655360 | tf_op jit(solution)/shard_map/all_to_all | solution.py:342
  140.0 5.0 %copy-start.17 = (bf16[512,256]{1,0:T(8,128)(2,1)S(1)}, bf16[512,256]{1,0:T(8,128)(2,1)}, u32[]{:S(2)}) copy-start(bf16[512,256]{1,0:T(8,128)(2,1)} %get-tuple-element.34) | copy-start | bytes 786436
  140.0 9.2 %copy-start.16 = (bf16[512,256]{1,0:T(8,128)(2,1)S(1)}, bf16[512,256]{1,0:T(8,128)(2,1)}, u32[]{:S(2)}) copy-start(bf16[512,256]{1,0:T(8,128)(2,1)} %get-tuple-element.35) | copy-start | bytes 786436
  144.9 29.5 %collective-permute-start.10 = (bf16[512,256]{1,0:T(8,128)(2,1)S(1)}, bf16[512,256]{1,0:T(8,128)(2,1)S(1)}, u32[]{:S(2)}, u32[]{:S(2)}) collective-permute-start(bf16[512,256]{1,0:T(8,128)(2,1)S(1)} %copy-done.17), channel_id=1, source_target_pairs={{0,4},{1,5},{2,6},{3,7},{4,0},{5,1},{6,2},{7,3},{8,12},{9,13},{10,... | collective-permute-start | bytes 786440 | tf_op jit(solution)/shard_map/ppermute | solution.py:329
  149.2 28.3 %collective-permute-start.11 = (bf16[512,256]{1,0:T(8,128)(2,1)S(1)}, bf16[512,256]{1,0:T(8,128)(2,1)S(1)}, u32[]{:S(2)}, u32[]{:S(2)}) collective-permute-start(bf16[512,256]{1,0:T(8,128)(2,1)S(1)} %copy-done.16), channel_id=1, source_target_pairs={{0,5},{1,6},{2,7},{3,0},{4,1},{5,2},{6,3},{7,4},{8,13},{9,14},{10,... | collective-permute-start | bytes 786440 | tf_op jit(solution)/shard_map/ppermute | solution.py:329
  151.1 35.7 %collective-permute-start.12 = (bf16[512,256]{1,0:T(8,128)(2,1)}, bf16[512,256]{1,0:T(8,128)(2,1)S(1)}, u32[]{:S(2)}, u32[]{:S(2)}) collective-permute-start(bf16[512,256]{1,0:T(8,128)(2,1)} %get-tuple-element.36), channel_id=1, source_target_pairs={{0,6},{1,7},{2,0},{3,1},{4,2},{5,3},{6,4},{7,5},{8,14},{9,15},{10,... | collective-permute-start | bytes 786440 | tf_op jit(solution)/shard_map/ppermute | solution.py:329
  153.6 33.2 %collective-permute-start.13 = (bf16[512,256]{1,0:T(8,128)(2,1)}, bf16[512,256]{1,0:T(8,128)(2,1)S(1)}, u32[]{:S(2)}, u32[]{:S(2)}) collective-permute-start(bf16[512,256]{1,0:T(8,128)(2,1)} %get-tuple-element.37), channel_id=1, source_target_pairs={{0,7},{1,0},{2,1},{3,2},{4,3},{5,4},{6,5},{7,6},{8,15},{9,8},{10,9... | collective-permute-start | bytes 786440 | tf_op jit(solution)/shard_map/ppermute | solution.py:329
  156.7 22.7 %collective-permute-start.15 = (bf16[640,256]{1,0:T(8,128)(2,1)S(1)}, bf16[640,256]{1,0:T(8,128)(2,1)S(1)}, u32[]{:S(2)}, u32[]{:S(2)}) collective-permute-start(bf16[640,256]{1,0:T(8,128)(2,1)S(1)} %bitcast.45), channel_id=1, source_target_pairs={{0,1},{1,0},{2,3},{3,2},{4,5},{5,4},{6,7},{7,6},{8,9},{9,8},{10,11... | collective-permute-start | bytes 983048 | tf_op jit(solution)/shard_map/ppermute | solution.py:347
  174.4 10.9 %copy-start = (bf16[512,256]{1,0:T(8,128)(2,1)}, bf16[512,256]{1,0:T(8,128)(2,1)S(1)}, u32[]{:S(2)}) copy-start(bf16[512,256]{1,0:T(8,128)(2,1)S(1)} %collective-permute-done.10.refs_4_) | copy-start | bytes 786436
  174.4 12.4 %collective-permute-start.7 = (bf16[512,256]{1,0:T(8,128)(2,1)}, bf16[512,256]{1,0:T(8,128)(2,1)S(1)}, u32[]{:S(2)}, u32[]{:S(2)}) collective-permute-start(bf16[512,256]{1,0:T(8,128)(2,1)} %get-tuple-element.31), channel_id=1, source_target_pairs={{0,1},{1,2},{2,3},{3,4},{4,5},{5,6},{6,7},{7,0},{8,9},{9,10},{10,1... | collective-permute-start | bytes 786440 | tf_op jit(solution)/shard_map/ppermute | solution.py:329
  177.5 7.8 %copy-start.1 = (bf16[512,256]{1,0:T(8,128)(2,1)}, bf16[512,256]{1,0:T(8,128)(2,1)S(1)}, u32[]{:S(2)}) copy-start(bf16[512,256]{1,0:T(8,128)(2,1)S(1)} %collective-permute-done.11.refs_5_) | copy-start | bytes 786436
  177.5 11.3 %collective-permute-start.8 = (bf16[512,256]{1,0:T(8,128)(2,1)}, bf16[512,256]{1,0:T(8,128)(2,1)S(1)}, u32[]{:S(2)}, u32[]{:S(2)}) collective-permute-start(bf16[512,256]{1,0:T(8,128)(2,1)} %get-tuple-element.32), channel_id=1, source_target_pairs={{0,2},{1,3},{2,4},{3,5},{4,6},{5,7},{6,0},{7,1},{8,10},{9,11},{10,... | collective-permute-start | bytes 786440 | tf_op jit(solution)/shard_map/ppermute | solution.py:329
  179.4 15.6 %collective-permute-start.9 = (bf16[512,256]{1,0:T(8,128)(2,1)}, bf16[512,256]{1,0:T(8,128)(2,1)}, u32[]{:S(2)}, u32[]{:S(2)}) collective-permute-start(bf16[512,256]{1,0:T(8,128)(2,1)} %get-tuple-element.33), channel_id=1, source_target_pairs={{0,3},{1,4},{2,5},{3,6},{4,7},{5,0},{6,1},{7,2},{8,11},{9,12},{10,... | collective-permute-start | bytes 786440 | tf_op jit(solution)/shard_map/ppermute | solution.py:329
  186.8 8.2 %copy-start.2 = (bf16[512,256]{1,0:T(8,128)(2,1)}, bf16[512,256]{1,0:T(8,128)(2,1)S(1)}, u32[]{:S(2)}) copy-start(bf16[512,256]{1,0:T(8,128)(2,1)S(1)} %collective-permute-done.12.refs_6_) | copy-start | bytes 786436
  186.8 8.2 %copy-start.3 = (bf16[512,256]{1,0:T(8,128)(2,1)}, bf16[512,256]{1,0:T(8,128)(2,1)S(1)}, u32[]{:S(2)}) copy-start(bf16[512,256]{1,0:T(8,128)(2,1)S(1)} %collective-permute-done.13.refs_7_) | copy-start | bytes 786436
  186.8 8.2 %copy-start.4 = (bf16[512,256]{1,0:T(8,128)(2,1)}, bf16[512,256]{1,0:T(8,128)(2,1)S(1)}, u32[]{:S(2)}) copy-start(bf16[512,256]{1,0:T(8,128)(2,1)S(1)} %collective-permute-done.7.refs_1_) | copy-start | bytes 786436
  188.8 6.2 %copy-start.5 = (bf16[512,256]{1,0:T(8,128)(2,1)}, bf16[512,256]{1,0:T(8,128)(2,1)S(1)}, u32[]{:S(2)}) copy-start(bf16[512,256]{1,0:T(8,128)(2,1)S(1)} %collective-permute-done.8.refs_2_) | copy-start | bytes 786436

commit v7 on v6

--- a/solution.py
+++ b/solution.py
@@ -250,7 +250,7 @@
             final[1, cell, :] += change[1]
         return carry
 
-    lax.fori_loop(0, cuts, some_blocks, 0)
+    lax.fori_loop(0, cuts, some_blocks, 0, unroll=2)
 
     def image(tile, carry):
         cell = pl.ds(pl.multiple_of(tile * 16, 16), 16)
@@ -262,7 +262,7 @@
         ).astype(bf16)
         return carry
 
-    lax.fori_loop(0, RADIX * base // 16, image, 0, unroll=4)
+    lax.fori_loop(0, RADIX * base // 16, image, 0, unroll=8)
 
 
 def call(kernel, out_shape, scratch, *operands, scalars=0, later=0):
@@ -393,14 +393,12 @@
 
     prop_re, prop_im = propagator(angular, cut_index, extent_x, extent_y)
     rows_x = cut_index * row_count + jnp.arange(row_count, dtype=jnp.int32)
+    cols_y = jnp.arange(extent_y, dtype=jnp.int32)
     offset_x = (rows_x - shot_position[0]).astype(f32) * grid_step
-    offset_y = (jnp.arange(extent_y, dtype=jnp.int32) - shot_position[1]).astype(f32) * grid_step
-    distance = jnp.sqrt(
-        offset_x[None, :] ** 2 + offset_y[:, None] ** 2 + depth_step * depth_step
-    )
-    ray = angular * slow_ref * distance
+    offset_y = (cols_y - shot_position[1]).astype(f32) * grid_step
+    distance = jnp.sqrt(offset_x[None, :] ** 2 + offset_y[:, None] ** 2 + depth_step * depth_step)
     level = 1.0 / math.sqrt(freq_total)
-    cos_r, sin_r = cos_sin(ray)
+    cos_r, sin_r = cos_sin(angular * slow_ref * distance)
     cos_r, sin_r = cos_r * level, sin_r * level
     owner_id = slab_owner[0]
     pieces = counts[1] * counts[2] * 16
@@ -425,6 +423,7 @@
 
     share, _ = lax.optimization_barrier((share, restored[0]))
     joined = join(share, "x")
+    joined, block_lengths = lax.optimization_barrier((joined, block_lengths))
     operators = join(joined[extent_y:filled], "yl")
     other = swap(operators, "core", 1)
     first = lax.axis_index("core") == 0

time: 254 us -> 255 us (level)
  the two profiles are of different devices: /device:TPU:8 before, /device:TPU:2 now
where the time goes in v7:
time: 255 us; the launch traced here: 254 us
  starting transfers between devices  99.7 us (39%)
  waiting for transfers between devices  49 us (19%)
  blocking collectives  38.9 us (15%)
  Pallas kernels  34.5 us (14%)
  other arithmetic  18.8 us (7%)
  local copies, waits for them, and re-layouts  11.8 us (5%)
    ppermute x14, starting transfers between devices, rotate(): lax.ppermute(values[d], axes, [(i, (i + d) % size) for i in range(size)])  55.6 us
    all_to_all x2, blocking collectives, sum_over(): terms = lax.all_to_all(part, axis, 0, 0, tiled=True)  38.9 us
    pallas_call x3, Pallas kernels, call(): pl.pallas_call(kernel, out_shape=out_shape, in_specs=[smem] * scalars + [...  34.5 us
    all_to_all x2, starting transfers between devices, split(): shaped = lax.all_to_all(shaped, axis, 0, 0)  19.7 us
    all_to_all x3, waiting for transfers between devices, join(): copies = lax.all_to_all(copies, axis, 0, 0)  15.8 us
    all_to_all x3, starting transfers between devices, join(): copies = lax.all_to_all(copies, axis, 0, 0)  15.6 us
    ppermute x14, waiting for transfers between devices, rotate(): lax.ppermute(values[d], axes, [(i, (i + d) % size) for i in range(size)])  11.3 us
    all_to_all x2, waiting for transfers between devices, split(): shaped = lax.all_to_all(shaped, axis, 0, 0)  11.2 us
  transfers between devices with their start and end apart: 21, of which 8 were waited for; matrix products, arithmetic and copies ran while one was open for 9% of the time, Pallas kernels for 7%

profile of v7, /device:TPU:2, one launch (start us, length us, event | category | flops | bytes accessed | tf_op | source)
XLA Modules:
  0.0 254.0 jit_solution(7715153627379127427)
XLA Ops:
  0.0 1.1 reshape_squeeze.3
  1.2 1.3 pad_maximum_fusion
  2.5 0.7 copy.17
  3.3 1.2 pad.8.clone
  4.4 9.4 %all-to-all-start = ((bf16[4,640,256]{2,1,0:T(8,128)(2,1)}), bf16[4,640,256]{2,1,0:T(8,128)(2,1)S(1)}, u32[]{:S(2)}, u32[]{:S(2)}) async-start(bf16[4,640,256]{2,1,0:T(8,128)(2,1)} %bitcast.4), calls=%async_computation | async-start | bytes 2621440 | tf_op jit(solution)/shard_map/all_to_all | solution.py:336
  14.5 11.2 %all-to-all-done = bf16[4,640,256]{2,1,0:T(8,128)(2,1)S(1)} async-done(((bf16[4,640,256]{2,1,0:T(8,128)(2,1)}), bf16[4,640,256]{2,1,0:T(8,128)(2,1)S(1)}, u32[]{:S(2)}, u32[]{:S(2)}) %all-to-all-start) | async-done | bytes 1310752 | tf_op jit(solution)/shard_map/all_to_all | solution.py:336
  25.7 0.7 constant_dynamic-slice_fusion
  26.4 10.3 %all-to-all-start.1 = ((bf16[8,80,256]{2,1,0:T(8,128)(2,1)}), bf16[8,80,256]{2,1,0:T(8,128)(2,1)S(1)}, u32[]{:S(2)}, u32[]{:S(2)}) async-start(bf16[8,80,256]{2,1,0:T(8,128)(2,1)} %bitcast.5), calls=%async_computation.1 | async-start | bytes 655360 | tf_op jit(solution)/shard_map/all_to_all | solution.py:336
  36.8 5.2 %shard_map.82 = (bf16[512,256]{1,0:T(8,128)(2,1)}, bf16[512,256]{1,0:T(8,128)(2,1)}, bf16[512,256]{1,0:T(8,128)(2,1)}, bf16[512,256]{1,0:T(8,128)(2,1)}, bf16[51...) custom-call(s32[1]{0:T(128)} %bitcast.me, ...), custom_call_target="tpu_custom_call" | custom-call | tf_op jit(solution)/shard_map/pallas_call | solution.py:272
  41.9 1.9 collective-permute-start.1
  43.8 3.5 %collective-permute-start.2 = (bf16[512,256]{1,0:T(8,128)(2,1)}, bf16[512,256]{1,0:T(8,128)(2,1)S(1)}, u32[]{:S(2)}, u32[]{:S(2)}) collective-permute-start(bf16[512,256]{1,0:T(8,128)(2,1)} %get-tuple-element.26), channel_id=1, source_target_pairs={{0,2},{1,3},{2,4},{3,5},{4,6},{5,7},{6,0},{7,1},{8,10},{9,11},{10,... | collective-permute-start | bytes 786440 | tf_op jit(solution)/shard_map/ppermute | solution.py:329
  47.3 4.5 %collective-permute-start.3 = (bf16[512,256]{1,0:T(8,128)(2,1)}, bf16[512,256]{1,0:T(8,128)(2,1)S(1)}, u32[]{:S(2)}, u32[]{:S(2)}) collective-permute-start(bf16[512,256]{1,0:T(8,128)(2,1)} %get-tuple-element.27), channel_id=1, source_target_pairs={{0,3},{1,4},{2,5},{3,6},{4,7},{5,0},{6,1},{7,2},{8,11},{9,12},{10,... | collective-permute-start | bytes 786440 | tf_op jit(solution)/shard_map/ppermute | solution.py:329
  51.8 3.1 %collective-permute-start.4 = (bf16[512,256]{1,0:T(8,128)(2,1)}, bf16[512,256]{1,0:T(8,128)(2,1)S(1)}, u32[]{:S(2)}, u32[]{:S(2)}) collective-permute-start(bf16[512,256]{1,0:T(8,128)(2,1)} %get-tuple-element.28), channel_id=1, source_target_pairs={{0,4},{1,5},{2,6},{3,7},{4,0},{5,1},{6,2},{7,3},{8,12},{9,13},{10,... | collective-permute-start | bytes 786440 | tf_op jit(solution)/shard_map/ppermute | solution.py:329
  55.1 6.8 %collective-permute-start = (bf16[80,256]{1,0:T(8,128)(2,1)S(1)}, bf16[80,256]{1,0:T(8,128)(2,1)S(1)}, u32[]{:S(2)}, u32[]{:S(2)}) collective-permute-start(bf16[80,256]{1,0:T(8,128)(2,1)S(1)} %dynamic-slice_bitcast_fusion.1), channel_id=1, source_target_pairs={{0,256},{256,0},{1,257},{257,1},{2,258},{258,2},{3,259},{259,3},{4... | collective-permute-start | bytes 122888 | tf_op jit(solution)/shard_map/ppermute | solution.py:347
  62.0 10.7 %collective-permute-done = bf16[80,256]{1,0:T(8,128)(2,1)S(1)} collective-permute-done((bf16[80,256]{1,0:T(8,128)(2,1)S(1)}, bf16[80,256]{1,0:T(8,128)(2,1)S(1)}, u32[]{:S(2)}, u32[]{:S(2)}) %collective-permute-start) | collective-permute-done | bytes 40992 | tf_op jit(solution)/shard_map/ppermute | solution.py:347
  72.7 1.9 collective-permute-start.5
  74.6 0.8 broadcast_in_dim.8
  75.4 7.2 %all-to-all-start.2 = ((bf16[8,80,256]{2,1,0:T(8,128)(2,1)}), bf16[8,80,256]{2,1,0:T(8,128)(2,1)S(1)}, u32[]{:S(2)}, u32[]{:S(2)}) async-start(bf16[8,80,256]{2,1,0:T(8,128)(2,1)} %broadcast_in_dim.8), calls=%async_computation.2 | async-start | bytes 655360 | tf_op jit(solution)/shard_map/all_to_all | solution.py:342
  82.6 5.1 %collective-permute-start.6 = (bf16[512,256]{1,0:T(8,128)(2,1)}, bf16[512,256]{1,0:T(8,128)(2,1)S(1)}, u32[]{:S(2)}, u32[]{:S(2)}) collective-permute-start(bf16[512,256]{1,0:T(8,128)(2,1)} %get-tuple-element.30), channel_id=1, source_target_pairs={{0,6},{1,7},{2,0},{3,1},{4,2},{5,3},{6,4},{7,5},{8,14},{9,15},{10,... | collective-permute-start | bytes 786440 | tf_op jit(solution)/shard_map/ppermute | solution.py:329
  87.7 1.9 collective-permute-start.7
  89.6 5.2 %fusion = (f32[8,256,256]{2,1,0:T(8,128)}, f32[8,256,256]{2,1,0:T(8,128)}) fusion(f32[256]{0:T(256)S(1)} %fusion.34, f32[8,256]{1,0:T(8,128)S(1)} %fusion.31), kind=kLoop, calls=%fused_computation.11 | loop fusion | flops 24641536 | bytes 4203520 | tf_op jit(solution)/shard_map/jit(_where)/select_n | solution.py:321
  94.9 1.6 dynamic-slice_bitcast_fusion.refs_9_
  97.5 13.1 %shard_map.83 = (bf16[512,256]{1,0:T(8,128)(2,1)}, bf16[512,256]{1,0:T(8,128)(2,1)}, bf16[512,256]{1,0:T(8,128)(2,1)}, bf16[512,256]{1,0:T(8,128)(2,1)}, bf16[51...) custom-call(bf16[512,256]{1,0:T(8,128)(2,1)} %get-tuple-element.24.refs_0_, ...), custom_call_target="tpu_custom_call" | custom-call | tf_op jit(solution)/shard_map/pallas_call | solution.py:272
  110.6 1.2 broadcast_in_dim.9
  111.8 5.0 %all-to-all-start.3 = ((bf16[4,640,256]{2,1,0:T(8,128)(2,1)}), bf16[4,640,256]{2,1,0:T(8,128)(2,1)S(1)}, u32[]{:S(2)}, u32[]{:S(2)}) async-start(bf16[4,640,256]{2,1,0:T(8,128)(2,1)} %broadcast_in_dim.9), calls=%async_computation.3 | async-start | bytes 2621440 | tf_op jit(solution)/shard_map/all_to_all | solution.py:342
  116.7 0.7 fusion.35
  118.6 15.7 %all-to-all-done.3 = bf16[4,640,256]{2,1,0:T(8,128)(2,1)S(1)} async-done(((bf16[4,640,256]{2,1,0:T(8,128)(2,1)}), bf16[4,640,256]{2,1,0:T(8,128)(2,1)S(1)}, u32[]{:S(2)}, u32[]{:S(2)}) %all-to-all-start.3) | async-done | bytes 1310752 | tf_op jit(solution)/shard_map/all_to_all | solution.py:342
  134.4 0.8 broadcast_in_dim.10
  135.2 3.5 %all-to-all-start.4 = ((bf16[4,160,256]{2,1,0:T(8,128)(2,1)}), bf16[4,160,256]{2,1,0:T(8,128)(2,1)S(1)}, u32[]{:S(2)}, u32[]{:S(2)}) async-start(bf16[4,160,256]{2,1,0:T(8,128)(2,1)} %broadcast_in_dim.10), calls=%async_computation.4 | async-start | bytes 655360 | tf_op jit(solution)/shard_map/all_to_all | solution.py:342
  138.6 5.0 %fusion.24 = (f32[2048,256]{1,0:T(8,128)}, f32[2048,256]{1,0:T(8,128)}) fusion(f32[2048]{0:T(1024)S(1)} %multiply_multiply_fusion.3, f32[256]{0:T(256)S(1)} %multiply_multiply_fusion.4, f32[]{:T(128)S(6)} %mul.300), kind=kLoop, calls=%fused_computation.35 | loop fusion | flops 23068672 | bytes 4203524 | tf_op jit(solution)/shard_map/mul | solution.py:402
  143.6 3.3 %collective-permute-start.10 = (bf16[512,256]{1,0:T(8,128)(2,1)S(1)}, bf16[512,256]{1,0:T(8,128)(2,1)S(1)}, u32[]{:S(2)}, u32[]{:S(2)}) collective-permute-start(bf16[512,256]{1,0:T(8,128)(2,1)S(1)} %copy-done.17), channel_id=1, source_target_pairs={{0,3},{1,4},{2,5},{3,6},{4,7},{5,0},{6,1},{7,2},{8,11},{9,12},{10,... | collective-permute-start | bytes 786440 | tf_op jit(solution)/shard_map/ppermute | solution.py:329
  146.9 4.3 %collective-permute-start.11 = (bf16[512,256]{1,0:T(8,128)(2,1)S(1)}, bf16[512,256]{1,0:T(8,128)(2,1)S(1)}, u32[]{:S(2)}, u32[]{:S(2)}) collective-permute-start(bf16[512,256]{1,0:T(8,128)(2,1)S(1)} %copy-done.16), channel_id=1, source_target_pairs={{0,4},{1,5},{2,6},{3,7},{4,0},{5,1},{6,2},{7,3},{8,12},{9,13},{10,... | collective-permute-start | bytes 786440 | tf_op jit(solution)/shard_map/ppermute | solution.py:329
  151.2 3.4 %collective-permute-start.12 = (bf16[512,256]{1,0:T(8,128)(2,1)}, bf16[512,256]{1,0:T(8,128)(2,1)S(1)}, u32[]{:S(2)}, u32[]{:S(2)}) collective-permute-start(bf16[512,256]{1,0:T(8,128)(2,1)} %get-tuple-element.39), channel_id=1, source_target_pairs={{0,5},{1,6},{2,7},{3,0},{4,1},{5,2},{6,3},{7,4},{8,13},{9,14},{10,... | collective-permute-start | bytes 786440 | tf_op jit(solution)/shard_map/ppermute | solution.py:329
  154.6 3.4 %collective-permute-start.13 = (bf16[512,256]{1,0:T(8,128)(2,1)}, bf16[512,256]{1,0:T(8,128)(2,1)S(1)}, u32[]{:S(2)}, u32[]{:S(2)}) collective-permute-start(bf16[512,256]{1,0:T(8,128)(2,1)} %get-tuple-element.40), channel_id=1, source_target_pairs={{0,6},{1,7},{2,0},{3,1},{4,2},{5,3},{6,4},{7,5},{8,14},{9,15},{10,... | collective-permute-start | bytes 786440 | tf_op jit(solution)/shard_map/ppermute | solution.py:329
  158.0 1.9 collective-permute-start.15
  159.9 4.3 %negate_select_fusion.2 = (f32[2048,256]{1,0:T(8,128)}, f32[2048,256]{1,0:T(8,128)}) fusion(f32[]{:T(128)S(6)} %mul.283, bf16[2560,256]{1,0:T(8,128)(2,1)S(1)} %bitcast.40), kind=kLoop, calls=%fused_computation.3 | loop fusion | flops 22020096 | bytes 5242884 | tf_op jit(solution)/shard_map/jit(_where)/select_n | solution.py:300
  165.1 2.5 collective-permute-done.10.refs_3_
  167.6 1.9 collective-permute-start.14
  169.5 1.1 collective-permute-done.11.refs_4_
  170.6 4.4 %collective-permute-start.8 = (bf16[512,256]{1,0:T(8,128)(2,1)}, bf16[512,256]{1,0:T(8,128)(2,1)S(1)}, u32[]{:S(2)}, u32[]{:S(2)}) collective-permute-start(bf16[512,256]{1,0:T(8,128)(2,1)} %get-tuple-element.35), channel_id=1, source_target_pairs={{0,1},{1,2},{2,3},{3,4},{4,5},{5,6},{6,7},{7,0},{8,9},{9,10},{10,1... | collective-permute-start | bytes 786440 | tf_op jit(solution)/shard_map/ppermute | solution.py:329
  175.1 13.1 %collective-permute-start.9 = (bf16[512,256]{1,0:T(8,128)(2,1)}, bf16[512,256]{1,0:T(8,128)(2,1)}, u32[]{:S(2)}, u32[]{:S(2)}) collective-permute-start(bf16[512,256]{1,0:T(8,128)(2,1)} %get-tuple-element.36), channel_id=1, source_target_pairs={{0,2},{1,3},{2,4},{3,5},{4,6},{5,7},{6,0},{7,1},{8,10},{9,11},{10,... | collective-permute-start | bytes 786440 | tf_op jit(solution)/shard_map/ppermute | solution.py:329
  188.8 1.5 pad.9.refs_12_
  190.4 2.2 collective-permute-done.8.refs_1_
  192.6 5.3 %collective-permute-done.9.refs_2_ = bf16[512,256]{1,0:T(8,128)(2,1)} collective-permute-done((bf16[512,256]{1,0:T(8,128)(2,1)}, bf16[512,256]{1,0:T(8,128)(2,1)}, u32[]{:S(2)}, u32[]{:S(2)}) %collective-permute-start.9) | collective-permute-done | bytes 262176 | tf_op jit(solution)/shard_map/ppermute | solution.py:329
  198.0 16.2 %shard_map.84 = bf16[4,2,8,32,256]{4,3,2,1,0:T(8,128)(2,1)} custom-call(s32[1]{0:T(128)} %bitcast.me, s32[40]{0:T(128)} %sub.137.starts, s32[40]{0:T(128)} %copy-done.14, bf16[512,256]{1,0:T(8,128)(2,1)} %get-tuple-element.32.refs_0_, bf16[512,256]{1,0:T(8,128)(2,1)} %copy-done.5, bf16[512,256]{1,0:T(8,128)(2,1)} %collective-permute-done.9.refs_2_, ...), custom_call_target="tpu_custom_call" | custom-call | tf_op jit(solution)/shard_map/pallas_call | solution.py:272
  214.2 19.1 %all_to_all.35 = bf16[4,2,8,32,256]{4,3,2,1,0:T(8,128)(2,1)S(1)} all-to-all(bf16[4,2,8,32,256]{4,3,2,1,0:T(8,128)(2,1)} %shard_map.84), channel_id=1, replica_groups=mesh['yh'=2,'x'=4,'z'=8,'yl'=4,'core'=2] {'x'}, dimensions={0} | all-to-all | bytes 2097152 | tf_op jit(solution)/shard_map/all_to_all | solution.py:362
  233.5 19.8 %all_to_all.36 = bf16[16,32,256]{2,1,0:T(8,128)(2,1)S(1)} all-to-all(bf16[16,32,256]{2,1,0:T(8,128)(2,1)S(1)} %bitcast.46), channel_id=1, replica_groups=mesh['yh'=2,'x'=4,'z'=8,'yl'=4,'core'=2] {'yh','z'}, dimensions={0} | all-to-all | bytes 524288 | tf_op jit(solution)/shard_map/all_to_all | solution.py:362
  253.3 0.7 convert_reduce_fusion
  (67 shorter events, 4.2 us)
Async XLA Ops:
  4.4 21.3 %all-to-all-start = ((bf16[4,640,256]{2,1,0:T(8,128)(2,1)}), bf16[4,640,256]{2,1,0:T(8,128)(2,1)S(1)}, u32[]{:S(2)}, u32[]{:S(2)}) async-start(bf16[4,640,256]{2,1,0:T(8,128)(2,1)} %bitcast.4), calls=%async_computation | async-start | bytes 2621440 | tf_op jit(solution)/shard_map/all_to_all | solution.py:336
  26.4 28.6 %all-to-all-start.1 = ((bf16[8,80,256]{2,1,0:T(8,128)(2,1)}), bf16[8,80,256]{2,1,0:T(8,128)(2,1)S(1)}, u32[]{:S(2)}, u32[]{:S(2)}) async-start(bf16[8,80,256]{2,1,0:T(8,128)(2,1)} %bitcast.5), calls=%async_computation.1 | async-start | bytes 655360 | tf_op jit(solution)/shard_map/all_to_all | solution.py:336
  41.9 40.7 %collective-permute-start.1 = (bf16[512,256]{1,0:T(8,128)(2,1)}, bf16[512,256]{1,0:T(8,128)(2,1)S(1)}, u32[]{:S(2)}, u32[]{:S(2)}) collective-permute-start(bf16[512,256]{1,0:T(8,128)(2,1)} %get-tuple-element.25), channel_id=1, source_target_pairs={{0,1},{1,2},{2,3},{3,4},{4,5},{5,6},{6,7},{7,0},{8,9},{9,10},{10,1... | collective-permute-start | bytes 786440 | tf_op jit(solution)/shard_map/ppermute | solution.py:329
  43.8 43.8 %collective-permute-start.2 = (bf16[512,256]{1,0:T(8,128)(2,1)}, bf16[512,256]{1,0:T(8,128)(2,1)S(1)}, u32[]{:S(2)}, u32[]{:S(2)}) collective-permute-start(bf16[512,256]{1,0:T(8,128)(2,1)} %get-tuple-element.26), channel_id=1, source_target_pairs={{0,2},{1,3},{2,4},{3,5},{4,6},{5,7},{6,0},{7,1},{8,10},{9,11},{10,... | collective-permute-start | bytes 786440 | tf_op jit(solution)/shard_map/ppermute | solution.py:329
  47.3 49.1 %collective-permute-start.3 = (bf16[512,256]{1,0:T(8,128)(2,1)}, bf16[512,256]{1,0:T(8,128)(2,1)S(1)}, u32[]{:S(2)}, u32[]{:S(2)}) collective-permute-start(bf16[512,256]{1,0:T(8,128)(2,1)} %get-tuple-element.27), channel_id=1, source_target_pairs={{0,3},{1,4},{2,5},{3,6},{4,7},{5,0},{6,1},{7,2},{8,11},{9,12},{10,... | collective-permute-start | bytes 786440 | tf_op jit(solution)/shard_map/ppermute | solution.py:329
  51.8 44.6 %collective-permute-start.4 = (bf16[512,256]{1,0:T(8,128)(2,1)}, bf16[512,256]{1,0:T(8,128)(2,1)S(1)}, u32[]{:S(2)}, u32[]{:S(2)}) collective-permute-start(bf16[512,256]{1,0:T(8,128)(2,1)} %get-tuple-element.28), channel_id=1, source_target_pairs={{0,4},{1,5},{2,6},{3,7},{4,0},{5,1},{6,2},{7,3},{8,12},{9,13},{10,... | collective-permute-start | bytes 786440 | tf_op jit(solution)/shard_map/ppermute | solution.py:329
  55.1 17.6 %collective-permute-start = (bf16[80,256]{1,0:T(8,128)(2,1)S(1)}, bf16[80,256]{1,0:T(8,128)(2,1)S(1)}, u32[]{:S(2)}, u32[]{:S(2)}) collective-permute-start(bf16[80,256]{1,0:T(8,128)(2,1)S(1)} %dynamic-slice_bitcast_fusion.1), channel_id=1, source_target_pairs={{0,256},{256,0},{1,257},{257,1},{2,258},{258,2},{3,259},{259,3},{4... | collective-permute-start | bytes 122888 | tf_op jit(solution)/shard_map/ppermute | solution.py:347
  72.7 23.7 %collective-permute-start.5 = (bf16[512,256]{1,0:T(8,128)(2,1)}, bf16[512,256]{1,0:T(8,128)(2,1)S(1)}, u32[]{:S(2)}, u32[]{:S(2)}) collective-permute-start(bf16[512,256]{1,0:T(8,128)(2,1)} %get-tuple-element.29), channel_id=1, source_target_pairs={{0,5},{1,6},{2,7},{3,0},{4,1},{5,2},{6,3},{7,4},{8,13},{9,14},{10,... | collective-permute-start | bytes 786440 | tf_op jit(solution)/shard_map/ppermute | solution.py:329
  75.4 35.2 %all-to-all-start.2 = ((bf16[8,80,256]{2,1,0:T(8,128)(2,1)}), bf16[8,80,256]{2,1,0:T(8,128)(2,1)S(1)}, u32[]{:S(2)}, u32[]{:S(2)}) async-start(bf16[8,80,256]{2,1,0:T(8,128)(2,1)} %broadcast_in_dim.8), calls=%async_computation.2 | async-start | bytes 655360 | tf_op jit(solution)/shard_map/all_to_all | solution.py:342
  82.6 12.3 %copy-start.6 = (bf16[512,256]{1,0:T(8,128)(2,1)}, bf16[512,256]{1,0:T(8,128)(2,1)S(1)}, u32[]{:S(2)}) copy-start(bf16[512,256]{1,0:T(8,128)(2,1)S(1)} %collective-permute-done.1.refs_1_) | copy-start | bytes 786436
  82.6 13.8 %collective-permute-start.6 = (bf16[512,256]{1,0:T(8,128)(2,1)}, bf16[512,256]{1,0:T(8,128)(2,1)S(1)}, u32[]{:S(2)}, u32[]{:S(2)}) collective-permute-start(bf16[512,256]{1,0:T(8,128)(2,1)} %get-tuple-element.30), channel_id=1, source_target_pairs={{0,6},{1,7},{2,0},{3,1},{4,2},{5,3},{6,4},{7,5},{8,14},{9,15},{10,... | collective-permute-start | bytes 786440 | tf_op jit(solution)/shard_map/ppermute | solution.py:329
  87.7 7.2 %copy-start.7 = (bf16[512,256]{1,0:T(8,128)(2,1)}, bf16[512,256]{1,0:T(8,128)(2,1)S(1)}, u32[]{:S(2)}) copy-start(bf16[512,256]{1,0:T(8,128)(2,1)S(1)} %collective-permute-done.2.refs_2_) | copy-start | bytes 786436
  87.7 8.9 %collective-permute-start.7 = (bf16[512,256]{1,0:T(8,128)(2,1)}, bf16[512,256]{1,0:T(8,128)(2,1)S(1)}, u32[]{:S(2)}, u32[]{:S(2)}) collective-permute-start(bf16[512,256]{1,0:T(8,128)(2,1)} %get-tuple-element.31), channel_id=1, source_target_pairs={{0,7},{1,0},{2,1},{3,2},{4,3},{5,4},{6,5},{7,6},{8,15},{9,8},{10,9... | collective-permute-start | bytes 786440 | tf_op jit(solution)/shard_map/ppermute | solution.py:329
  96.4 0.7 copy-start.8
  96.4 0.8 copy-start.9
  96.4 0.9 copy-start.10
  96.5 0.9 copy-start.11
  96.6 0.9 copy-start.12
  110.6 6.1 %copy-start.15 = (s32[2]{0:T(128)S(1)}, s32[2]{0:T(128)}, u32[]{:S(2)}) copy-start(s32[2]{0:T(128)} %param.13) | copy-start | bytes 28
  111.8 22.6 %all-to-all-start.3 = ((bf16[4,640,256]{2,1,0:T(8,128)(2,1)}), bf16[4,640,256]{2,1,0:T(8,128)(2,1)S(1)}, u32[]{:S(2)}, u32[]{:S(2)}) async-start(bf16[4,640,256]{2,1,0:T(8,128)(2,1)} %broadcast_in_dim.9), calls=%async_computation.3 | async-start | bytes 2621440 | tf_op jit(solution)/shard_map/all_to_all | solution.py:342
  135.2 22.8 %all-to-all-start.4 = ((bf16[4,160,256]{2,1,0:T(8,128)(2,1)}), bf16[4,160,256]{2,1,0:T(8,128)(2,1)S(1)}, u32[]{:S(2)}, u32[]{:S(2)}) async-start(bf16[4,160,256]{2,1,0:T(8,128)(2,1)} %broadcast_in_dim.10), calls=%async_computation.4 | async-start | bytes 655360 | tf_op jit(solution)/shard_map/all_to_all | solution.py:342
  138.6 5.0 %copy-start.17 = (bf16[512,256]{1,0:T(8,128)(2,1)S(1)}, bf16[512,256]{1,0:T(8,128)(2,1)}, u32[]{:S(2)}) copy-start(bf16[512,256]{1,0:T(8,128)(2,1)} %get-tuple-element.37) | copy-start | bytes 786436
  138.6 8.3 %copy-start.16 = (bf16[512,256]{1,0:T(8,128)(2,1)S(1)}, bf16[512,256]{1,0:T(8,128)(2,1)}, u32[]{:S(2)}) copy-start(bf16[512,256]{1,0:T(8,128)(2,1)} %get-tuple-element.38) | copy-start | bytes 786436
  143.6 24.0 %collective-permute-start.10 = (bf16[512,256]{1,0:T(8,128)(2,1)S(1)}, bf16[512,256]{1,0:T(8,128)(2,1)S(1)}, u32[]{:S(2)}, u32[]{:S(2)}) collective-permute-start(bf16[512,256]{1,0:T(8,128)(2,1)S(1)} %copy-done.17), channel_id=1, source_target_pairs={{0,3},{1,4},{2,5},{3,6},{4,7},{5,0},{6,1},{7,2},{8,11},{9,12},{10,... | collective-permute-start | bytes 786440 | tf_op jit(solution)/shard_map/ppermute | solution.py:329
  146.9 23.7 %collective-permute-start.11 = (bf16[512,256]{1,0:T(8,128)(2,1)S(1)}, bf16[512,256]{1,0:T(8,128)(2,1)S(1)}, u32[]{:S(2)}, u32[]{:S(2)}) collective-permute-start(bf16[512,256]{1,0:T(8,128)(2,1)S(1)} %copy-done.16), channel_id=1, source_target_pairs={{0,4},{1,5},{2,6},{3,7},{4,0},{5,1},{6,2},{7,3},{8,12},{9,13},{10,... | collective-permute-start | bytes 786440 | tf_op jit(solution)/shard_map/ppermute | solution.py:329
  151.2 39.2 %collective-permute-start.12 = (bf16[512,256]{1,0:T(8,128)(2,1)}, bf16[512,256]{1,0:T(8,128)(2,1)S(1)}, u32[]{:S(2)}, u32[]{:S(2)}) collective-permute-start(bf16[512,256]{1,0:T(8,128)(2,1)} %get-tuple-element.39), channel_id=1, source_target_pairs={{0,5},{1,6},{2,7},{3,0},{4,1},{5,2},{6,3},{7,4},{8,13},{9,14},{10,... | collective-permute-start | bytes 786440 | tf_op jit(solution)/shard_map/ppermute | solution.py:329
  154.6 35.8 %collective-permute-start.13 = (bf16[512,256]{1,0:T(8,128)(2,1)}, bf16[512,256]{1,0:T(8,128)(2,1)S(1)}, u32[]{:S(2)}, u32[]{:S(2)}) collective-permute-start(bf16[512,256]{1,0:T(8,128)(2,1)} %get-tuple-element.40), channel_id=1, source_target_pairs={{0,6},{1,7},{2,0},{3,1},{4,2},{5,3},{6,4},{7,5},{8,14},{9,15},{10,... | collective-permute-start | bytes 786440 | tf_op jit(solution)/shard_map/ppermute | solution.py:329
  158.0 6.3 %copy-start.13 = (s32[64,40]{0,1:T(8,128)S(1)}, s32[64,40]{0,1:T(8,128)}, u32[]{:S(2)}) copy-start(s32[64,40]{0,1:T(8,128)} %param.11) | copy-start | bytes 30724
  158.0 17.1 %collective-permute-start.15 = (bf16[640,256]{1,0:T(8,128)(2,1)S(1)}, bf16[640,256]{1,0:T(8,128)(2,1)S(1)}, u32[]{:S(2)}, u32[]{:S(2)}) collective-permute-start(bf16[640,256]{1,0:T(8,128)(2,1)S(1)} %bitcast.45), channel_id=1, source_target_pairs={{0,1},{1,0},{2,3},{3,2},{4,5},{5,4},{6,7},{7,6},{8,9},{9,8},{10,11... | collective-permute-start | bytes 983048 | tf_op jit(solution)/shard_map/ppermute | solution.py:347
  164.4 24.4 %copy-start.14 = (s32[40]{0:T(128)}, s32[40]{0:T(128)S(1)}, u32[]{:S(2)}) copy-start(s32[40]{0:T(128)S(1)} %get-tuple-element.47.lengths) | copy-start | bytes 484
  167.6 21.3 %copy-start = (bf16[512,256]{1,0:T(8,128)(2,1)}, bf16[512,256]{1,0:T(8,128)(2,1)S(1)}, u32[]{:S(2)}) copy-start(bf16[512,256]{1,0:T(8,128)(2,1)S(1)} %collective-permute-done.10.refs_3_) | copy-start | bytes 786436
  167.6 22.8 %collective-permute-start.14 = (bf16[512,256]{1,0:T(8,128)(2,1)}, bf16[512,256]{1,0:T(8,128)(2,1)S(1)}, u32[]{:S(2)}, u32[]{:S(2)}) collective-permute-start(bf16[512,256]{1,0:T(8,128)(2,1)} %get-tuple-element.41), channel_id=1, source_target_pairs={{0,7},{1,0},{2,1},{3,2},{4,3},{5,4},{6,5},{7,6},{8,15},{9,8},{10,9... | collective-permute-start | bytes 786440 | tf_op jit(solution)/shard_map/ppermute | solution.py:329
  170.6 18.2 %copy-start.1 = (bf16[512,256]{1,0:T(8,128)(2,1)}, bf16[512,256]{1,0:T(8,128)(2,1)S(1)}, u32[]{:S(2)}) copy-start(bf16[512,256]{1,0:T(8,128)(2,1)S(1)} %collective-permute-done.11.refs_4_) | copy-start | bytes 786436
  170.6 22.0 %collective-permute-start.8 = (bf16[512,256]{1,0:T(8,128)(2,1)}, bf16[512,256]{1,0:T(8,128)(2,1)S(1)}, u32[]{:S(2)}, u32[]{:S(2)}) collective-permute-start(bf16[512,256]{1,0:T(8,128)(2,1)} %get-tuple-element.35), channel_id=1, source_target_pairs={{0,1},{1,2},{2,3},{3,4},{4,5},{5,6},{6,7},{7,0},{8,9},{9,10},{10,1... | collective-permute-start | bytes 786440 | tf_op jit(solution)/shard_map/ppermute | solution.py:329
  175.1 22.9 %collective-permute-start.9 = (bf16[512,256]{1,0:T(8,128)(2,1)}, bf16[512,256]{1,0:T(8,128)(2,1)}, u32[]{:S(2)}, u32[]{:S(2)}) collective-permute-start(bf16[512,256]{1,0:T(8,128)(2,1)} %get-tuple-element.36), channel_id=1, source_target_pairs={{0,2},{1,3},{2,4},{3,5},{4,6},{5,7},{6,0},{7,1},{8,10},{9,11},{10,... | collective-permute-start | bytes 786440 | tf_op jit(solution)/shard_map/ppermute | solution.py:329
  190.4 7.6 %copy-start.2 = (bf16[512,256]{1,0:T(8,128)(2,1)}, bf16[512,256]{1,0:T(8,128)(2,1)S(1)}, u32[]{:S(2)}) copy-start(bf16[512,256]{1,0:T(8,128)(2,1)S(1)} %collective-permute-done.12.refs_5_) | copy-start | bytes 786436
  190.4 7.6 %copy-start.3 = (bf16[512,256]{1,0:T(8,128)(2,1)}, bf16[512,256]{1,0:T(8,128)(2,1)S(1)}, u32[]{:S(2)}) copy-start(bf16[512,256]{1,0:T(8,128)(2,1)S(1)} %collective-permute-done.13.refs_6_) | copy-start | bytes 786436
  190.4 7.6 %copy-start.4 = (bf16[512,256]{1,0:T(8,128)(2,1)}, bf16[512,256]{1,0:T(8,128)(2,1)S(1)}, u32[]{:S(2)}) copy-start(bf16[512,256]{1,0:T(8,128)(2,1)S(1)} %collective-permute-done.14.refs_7_) | copy-start | bytes 786436
  192.6 5.4 %copy-start.5 = (bf16[512,256]{1,0:T(8,128)(2,1)}, bf16[512,256]{1,0:T(8,128)(2,1)S(1)}, u32[]{:S(2)}) copy-start(bf16[512,256]{1,0:T(8,128)(2,1)S(1)} %collective-permute-done.8.refs_1_) | copy-start | bytes 786436
